TPU v7x, 32 devices: a whole 2x2x4 slice. The times are simulated.
32 devices in a mesh: section: 2 (over core), dp: 4 (over y, x), tensor: 4 (over z).
Axes of the slice: x: 2, y: 2, z: 4, core: 2. Of those that a mesh axis runs over, the one named last changes fastest.
Arguments:
- inputs: bfloat16 [4, 4, 1024, 1024], P('dp', None, 'tensor'), may hold values from -6 to 6
- segments: int32 [4, 4, 1024], P('dp'), may hold values from 0 to 3, never falling along the last dimension, each value on 1 to 512 neighbouring positions
- projection_in: bfloat16 [2, 1024, 3, 1024], P('section', None, None, 'tensor'), may hold values from -0.1875 to 0.1875
- projection_out: bfloat16 [2, 1024, 1024], P('section', 'tensor'), may hold values from -0.1875 to 0.1875
- up_weight: bfloat16 [2, 1024, 4096], P('section', None, 'tensor'), may hold values from -0.1875 to 0.1875
- down_weight: bfloat16 [2, 4096, 1024], P('section', 'tensor'), may hold values from -0.09375 to 0.09375
- norm_gains: float32 [2, 4, 1024], P('section'), may hold values from 0.25 to 1.75
- cotangent: bfloat16 [4, 4, 1024, 1024], P('dp', None, 'tensor'), may hold values from -6 to 6
Outputs:
- layer_outputs: bfloat16 [2, 4, 4, 1024, 1024], P('section', 'dp', None, 'tensor')
- input_grads: bfloat16 [2, 4, 4, 1024, 1024], P('section', 'dp', None, 'tensor')
- projection_in_grad: float32 [2, 1024, 3, 1024], P('section', None, None, 'tensor')
- projection_out_grad: float32 [2, 1024, 1024], P('section', 'tensor')
- up_grad: float32 [2, 1024, 4096], P('section', None, 'tensor')
- down_grad: float32 [2, 4096, 1024], P('section', 'tensor')
- gains_grad: float32 [2, 4, 1024], P('section')
Inputs may be any that keep to these rules, and one draw needn't show every extreme that they name: `segments`: in each pack of 1024 positions the segment numbers never fall; a number covers one document of at most 512 positions, and one document has exactly that many.
All inputs are finite; a program needn't handle non-finite values.
Results may differ from a plain program's by a relative error of at most 0.025.
Values may be sent and summed in bfloat16 or wider, within the bound.
No kernel may reach another device: no remote copies, remote signals or barrier semaphores. Data moves between devices by JAX's collectives and lax.ppermute only.
A program may use at most 320 MiB of HBM per device.

v0:
```python
from functools import partial
import math

import jax
import jax.numpy as jnp
from jax import lax
from jax.sharding import PartitionSpec as P

HEAD_DIM = 64
QBLOCK = 512


EPSILON = 1e-05
ROTARY_BASE = 10000.0
NEGATIVE = -1e30


def from_behind(shard, axis, by):
    length = lax.axis_size(axis)
    pairs = [(i, i + by) for i in range(length) if 0 <= i + by < length]
    return lax.ppermute(shard, axis, pairs)


def rms_parts(values, gain):
    inverse = lax.rsqrt(jnp.mean(values * values, axis=-1, keepdims=True) + EPSILON)
    return (values * inverse * gain, inverse)


def rms_back(values, inverse, gain, upstream):
    normed = values * inverse
    scaled = upstream * gain
    back = inverse * (scaled - normed * jnp.mean(scaled * normed, axis=-1, keepdims=True))
    return (back, jnp.sum(upstream * normed, axis=0))


def rotary_tables(length):
    half = HEAD_DIM // 2
    freqs = ROTARY_BASE ** (-2.0 * jnp.arange(half, dtype=jnp.float32) / HEAD_DIM)
    angles = jnp.arange(length, dtype=jnp.float32)[:, None] * freqs[None, :]
    return (jnp.cos(angles)[:, None, :], jnp.sin(angles)[:, None, :])


def rotate(values, cosine, sine):
    half = values.shape[-1] // 2
    first = values[..., :half]
    second = values[..., half:]
    return jnp.concatenate(
        [first * cosine - second * sine, second * cosine + first * sine], axis=-1
    )


def unrotate(upstream, cosine, sine):
    half = upstream.shape[-1] // 2
    first = upstream[..., :half]
    second = upstream[..., half:]
    return jnp.concatenate(
        [first * cosine + second * sine, second * cosine - first * sine], axis=-1
    )


def times_transposed(left, right):
    return lax.dot_general(
        left, right, (((1,), (1,)), ((), ())), preferred_element_type=jnp.float32
    )


def transposed_times(left, right):
    return lax.dot_general(
        left, right, (((0,), (0,)), ((), ())), preferred_element_type=jnp.float32
    )


def split_heads(projected, inner, cosine, sine):
    length = projected.shape[0]
    heads = inner // HEAD_DIM
    queries = rotate(projected[:, :inner].reshape(length, heads, HEAD_DIM), cosine, sine).astype(
        jnp.bfloat16
    )
    keys = rotate(
        projected[:, inner : 2 * inner].reshape(length, heads, HEAD_DIM), cosine, sine
    ).astype(jnp.bfloat16)
    values = projected[:, 2 * inner :].reshape(length, heads, HEAD_DIM).astype(jnp.bfloat16)
    return (queries, keys, values)


def block_scores(query_block, keys, segment_block, position_block, segment, position):
    scale = 1.0 / math.sqrt(HEAD_DIM)
    scores = (
        jnp.einsum("qhd,khd->hqk", query_block, keys, preferred_element_type=jnp.float32) * scale
    )
    allowed = (segment_block[:, None] == segment[None, :]) & (
        position_block[:, None] >= position[None, :]
    )
    return jnp.where(allowed[None], scores, NEGATIVE)


def attend(queries, keys, values, segment):
    length, heads, width = queries.shape
    blocks = length // QBLOCK
    position = jnp.arange(length, dtype=jnp.int32)

    def one_block(pieces):
        query_block, segment_block, position_block = pieces
        scores = block_scores(query_block, keys, segment_block, position_block, segment, position)
        largest = jnp.max(scores, axis=-1, keepdims=True)
        exponent = jnp.exp(scores - largest)
        totals = jnp.sum(exponent, axis=-1, keepdims=True)
        probs = (exponent / totals).astype(jnp.bfloat16)
        mixed = jnp.einsum("hqk,khd->qhd", probs, values, preferred_element_type=jnp.float32)
        return (
            mixed.reshape(QBLOCK, heads * width).astype(jnp.bfloat16),
            (largest + jnp.log(totals))[..., 0],
        )

    attended, logsum = lax.map(
        one_block,
        (
            queries.reshape(blocks, QBLOCK, heads, width),
            segment.reshape(blocks, QBLOCK),
            position.reshape(blocks, QBLOCK),
        ),
    )
    return (attended.reshape(length, heads * width), logsum)


def attend_back(queries, keys, values, segment, logsum, upstream):
    length, heads, width = queries.shape
    blocks = length // QBLOCK
    scale = 1.0 / math.sqrt(width)
    position = jnp.arange(length, dtype=jnp.int32)

    def one_block(carry, pieces):
        key_grad, value_grad = carry
        query_block, segment_block, position_block, logsum_block, upstream_block = pieces
        scores = block_scores(query_block, keys, segment_block, position_block, segment, position)
        probs = jnp.exp(scores - logsum_block[:, :, None])
        upstream_heads = upstream_block.reshape(QBLOCK, heads, width)
        prob_grad = jnp.einsum(
            "qhd,khd->hqk", upstream_heads, values, preferred_element_type=jnp.float32
        )
        score_grad = (
            probs * (prob_grad - jnp.sum(probs * prob_grad, axis=-1, keepdims=True))
        ).astype(jnp.bfloat16)
        query_grad = (
            jnp.einsum("hqk,khd->qhd", score_grad, keys, preferred_element_type=jnp.float32) * scale
        )
        key_grad = (
            key_grad
            + jnp.einsum(
                "hqk,qhd->khd", score_grad, query_block, preferred_element_type=jnp.float32
            )
            * scale
        )
        value_grad = value_grad + jnp.einsum(
            "hqk,qhd->khd",
            probs.astype(jnp.bfloat16),
            upstream_heads,
            preferred_element_type=jnp.float32,
        )
        return ((key_grad, value_grad), query_grad)

    zeros = jnp.zeros((length, heads, width), jnp.float32)
    carried, query_grad = lax.scan(
        one_block,
        (zeros, zeros),
        (
            queries.reshape(blocks, QBLOCK, heads, width),
            segment.reshape(blocks, QBLOCK),
            position.reshape(blocks, QBLOCK),
            logsum,
            upstream.reshape(blocks, QBLOCK, heads * width),
        ),
    )
    return (query_grad.reshape(length, heads, width), carried[0], carried[1])


def layer_forward(layer_in, segment, params):
    weight_in, weight_out, weight_up, weight_down, gain_table = params
    inner = weight_out.shape[0]
    inputs_float = layer_in.astype(jnp.float32)
    normed, _ = rms_parts(inputs_float, gain_table[0])
    normed_full = lax.all_gather(normed.astype(jnp.bfloat16), "tensor", axis=0, tiled=True)
    cosine, sine = rotary_tables(normed_full.shape[0])
    projected = jnp.dot(normed_full, weight_in, preferred_element_type=jnp.float32)
    queries, keys, values = split_heads(projected, inner, cosine, sine)
    attended, logsum = attend(queries, keys, values, segment)
    branch = lax.psum_scatter(
        jnp.dot(attended, weight_out, preferred_element_type=jnp.float32).astype(jnp.bfloat16),
        "tensor",
        scatter_dimension=0,
        tiled=True,
    ).astype(jnp.float32)
    branch_normed, _ = rms_parts(branch, gain_table[1])
    middle = inputs_float + branch_normed
    normed_mid, _ = rms_parts(middle, gain_table[2])
    mid_rows = lax.all_gather(normed_mid.astype(jnp.bfloat16), "tensor", axis=0, tiled=True)
    hidden = jax.nn.gelu(
        jnp.dot(mid_rows, weight_up, preferred_element_type=jnp.float32), approximate=False
    ).astype(jnp.bfloat16)
    mixed = lax.psum_scatter(
        jnp.dot(hidden, weight_down, preferred_element_type=jnp.float32).astype(jnp.bfloat16),
        "tensor",
        scatter_dimension=0,
        tiled=True,
    ).astype(jnp.float32)
    mixed_normed, _ = rms_parts(mixed, gain_table[3])
    return (middle + mixed_normed, (branch, mixed, attended, logsum, normed_full, mid_rows))


def layer_backward(layer_in, segment, params, kept, upstream):
    weight_in, weight_out, weight_up, weight_down, gain_table = params
    inner = weight_out.shape[0]
    branch, mixed, attended, logsum, normed_full, mid_rows = kept
    inputs_float = layer_in.astype(jnp.float32)
    _, in_inverse = rms_parts(inputs_float, gain_table[0])
    branch_normed, branch_inverse = rms_parts(branch, gain_table[1])
    middle = inputs_float + branch_normed
    _, mid_inverse = rms_parts(middle, gain_table[2])
    _, mixed_inverse = rms_parts(mixed, gain_table[3])
    mixed_grad, gain_three = rms_back(mixed, mixed_inverse, gain_table[3], upstream)
    mixed_rows = lax.all_gather(mixed_grad.astype(jnp.bfloat16), "tensor", axis=0, tiled=True)
    preact = jnp.dot(mid_rows, weight_up, preferred_element_type=jnp.float32)
    hidden, gelu_back = jax.vjp(partial(jax.nn.gelu, approximate=False), preact)
    hidden = hidden.astype(jnp.bfloat16)
    down_part = transposed_times(hidden, mixed_rows)
    preact_grad = gelu_back(times_transposed(mixed_rows, weight_down))[0].astype(jnp.bfloat16)
    up_part = transposed_times(mid_rows, preact_grad)
    mid_grad = lax.psum_scatter(
        times_transposed(preact_grad, weight_up).astype(jnp.bfloat16),
        "tensor",
        scatter_dimension=0,
        tiled=True,
    ).astype(jnp.float32)
    middle_back, gain_two = rms_back(middle, mid_inverse, gain_table[2], mid_grad)
    middle_grad = upstream + middle_back
    branch_grad, gain_one = rms_back(branch, branch_inverse, gain_table[1], middle_grad)
    branch_full = lax.all_gather(branch_grad.astype(jnp.bfloat16), "tensor", axis=0, tiled=True)
    out_part = transposed_times(attended, branch_full)
    attended_grad = times_transposed(branch_full, weight_out).astype(jnp.bfloat16)
    length = normed_full.shape[0]
    cosine, sine = rotary_tables(length)
    projected = jnp.dot(normed_full, weight_in, preferred_element_type=jnp.float32)
    queries, keys, values = split_heads(projected, inner, cosine, sine)
    query_grad, key_grad, value_grad = attend_back(
        queries, keys, values, segment, logsum, attended_grad
    )
    projected_grad = jnp.concatenate(
        [
            unrotate(query_grad, cosine, sine).reshape(length, inner),
            unrotate(key_grad, cosine, sine).reshape(length, inner),
            value_grad.reshape(length, inner),
        ],
        axis=1,
    ).astype(jnp.bfloat16)
    in_part = transposed_times(normed_full, projected_grad)
    normed_grad = lax.psum_scatter(
        times_transposed(projected_grad, weight_in).astype(jnp.bfloat16),
        "tensor",
        scatter_dimension=0,
        tiled=True,
    ).astype(jnp.float32)
    input_back, gain_zero = rms_back(inputs_float, in_inverse, gain_table[0], normed_grad)
    gain_parts = jnp.stack([gain_zero, gain_one, gain_two, gain_three])
    return (middle_grad + input_back, (in_part, out_part, up_part, down_part), gain_parts)


def take_slot(buffer, slot):
    return lax.dynamic_index_in_dim(buffer, slot, 0, keepdims=False)


def put_slot(buffer, slot, value, valid):
    merged = jnp.where(valid, value, take_slot(buffer, slot))
    return lax.dynamic_update_index_in_dim(buffer, merged, slot, 0)


def per_device(
    inputs, segments, projection_in, projection_out, up_weight, down_weight, norm_gains, cotangent
):
    section = lax.axis_index("section")
    micro = inputs.shape[1]
    rows = inputs.shape[2]
    width = inputs.shape[3]
    inner = projection_out.shape[1]
    up_use, down_use = (up_weight[0], down_weight[0])
    params = (
        projection_in[0].reshape(width, 3 * inner),
        projection_out[0],
        up_use,
        down_use,
        norm_gains[0],
    )
    received = jnp.zeros((rows, width), jnp.bfloat16)
    stored_inputs = jnp.zeros((micro, rows, width), jnp.bfloat16)
    layer_store = jnp.zeros((micro, rows, width), jnp.bfloat16)
    saved = None
    for period in range(micro + 1):
        index = period - section
        valid = (index >= 0) & (index < micro)
        slot = jnp.clip(index, 0, micro - 1)
        own_rows = take_slot(inputs[0], slot)
        layer_in = jnp.where(section == 0, own_rows, received)
        segment = take_slot(segments[0], slot)
        result, kept = layer_forward(layer_in, segment, params)
        result_low = result.astype(jnp.bfloat16)
        if saved is None:
            saved = jax.tree.map(lambda item: jnp.zeros((micro,) + item.shape, item.dtype), kept)
        saved = jax.tree.map(lambda buffer, item: put_slot(buffer, slot, item, valid), saved, kept)
        stored_inputs = put_slot(stored_inputs, slot, layer_in, valid)
        layer_store = put_slot(layer_store, slot, result_low, valid)
        if period < micro:
            received = from_behind(result_low, "section", 1)
    grad_back = jnp.zeros((rows, width), jnp.bfloat16)
    grad_store = jnp.zeros((micro, rows, width), jnp.bfloat16)
    total_in = jnp.zeros((width, 3 * inner), jnp.float32)
    total_out = jnp.zeros((inner, width), jnp.float32)
    total_up = jnp.zeros(up_use.shape, jnp.float32)
    total_down = jnp.zeros(down_use.shape, jnp.float32)
    total_gain = jnp.zeros((4, width), jnp.float32)
    for period in range(micro + 1):
        index = period - (1 - section)
        valid = (index >= 0) & (index < micro)
        slot = jnp.clip(index, 0, micro - 1)
        own_grad = take_slot(cotangent[0], slot)
        upstream = jnp.where(section == 1, own_grad, grad_back).astype(jnp.float32)
        kept = jax.tree.map(lambda buffer: take_slot(buffer, slot), saved)
        layer_in = take_slot(stored_inputs, slot)
        segment = take_slot(segments[0], slot)
        input_grad, weight_parts, gain_parts = layer_backward(
            layer_in, segment, params, kept, upstream
        )
        total_in = total_in + jnp.where(valid, weight_parts[0], 0.0)
        total_out = total_out + jnp.where(valid, weight_parts[1], 0.0)
        total_up = total_up + jnp.where(valid, weight_parts[2], 0.0)
        total_down = total_down + jnp.where(valid, weight_parts[3], 0.0)
        total_gain = total_gain + jnp.where(valid, gain_parts, 0.0)
        grad_low = input_grad.astype(jnp.bfloat16)
        grad_store = put_slot(grad_store, slot, grad_low, valid)
        if period < micro:
            grad_back = from_behind(grad_low, "section", -1)
    total_in, total_out, total_up, total_down = (
        lax.psum(total_in.astype(jnp.bfloat16), "dp").astype(jnp.float32),
        lax.psum(total_out.astype(jnp.bfloat16), "dp").astype(jnp.float32),
        lax.psum(total_up.astype(jnp.bfloat16), "dp").astype(jnp.float32),
        lax.psum(total_down.astype(jnp.bfloat16), "dp").astype(jnp.float32),
    )
    total_gain = lax.psum(total_gain, ("dp", "tensor"))
    return (
        layer_store[None, None],
        grad_store[None, None],
        total_in.reshape(1, width, 3, inner),
        total_out[None],
        total_up[None],
        total_down[None],
        total_gain[None],
    )


def solution(mesh):
    placed = (
        P("dp", None, "tensor", None),
        P("dp", None, None),
        P("section", None, None, "tensor"),
        P("section", "tensor", None),
        P("section", None, "tensor"),
        P("section", "tensor", None),
        P("section", None, None),
        P("dp", None, "tensor", None),
    )
    return jax.shard_map(
        per_device,
        mesh=mesh,
        in_specs=placed,
        out_specs=(
            P("section", "dp", None, "tensor", None),
            P("section", "dp", None, "tensor", None),
            P("section", None, None, "tensor"),
            P("section", "tensor", None),
            P("section", None, "tensor"),
            P("section", "tensor", None),
            P("section", None, None),
        ),
        check_vma=False,
    )
```

profile of v0, /device:TPU:0, one launch (start us, length us, event | category | flops | bytes accessed | tf_op | source)
XLA Modules:
  0.0 2846.8 jit_solution(16435209325790439689)
XLA Ops:
  97.8 42.6 %reduce-scatter.21.cloned.1.call-done = bf16[256,1024]{1,0:T(8,128)(2,1)} async-done(((bf16[1024,1024]{1,0:T(8,128)(2,1)}), bf16[256,1024]{1,0:T(8,128)(2,1)}) %reduce-scatter.21.cloned.1.call-update) | async-done | bytes 524304 | tf_op jit(solution)/shard_map/reduce_scatter | solution.py:187
  145.8 45.2 %all-gather.23.cloned.1.call-done = bf16[1024,1024]{1,0:T(8,128)(2,1)} async-done(((bf16[256,1024]{1,0:T(8,128)(2,1)}), bf16[1024,1024]{1,0:T(8,128)(2,1)}) %all-gather.23.cloned.1.call-update) | async-done | bytes 2097168 | tf_op jit(solution)/shard_map/all_gather | solution.py:196
  206.5 42.7 %reduce-scatter.23.cloned.1.call-done = bf16[256,1024]{1,0:T(8,128)(2,1)} async-done(((bf16[1024,1024]{1,0:T(8,128)(2,1)}), bf16[256,1024]{1,0:T(8,128)(2,1)}) %reduce-scatter.23.cloned.1.call-update) | async-done | bytes 524304 | tf_op jit(solution)/shard_map/reduce_scatter | solution.py:200
  265.7 44.0 %all-gather.25.cloned.1.call-done = bf16[1024,1024]{1,0:T(8,128)(2,1)} async-done(((bf16[256,1024]{1,0:T(8,128)(2,1)}), bf16[1024,1024]{1,0:T(8,128)(2,1)}) %all-gather.25.cloned.1.call-update) | async-done | bytes 2097168 | tf_op jit(solution)/shard_map/all_gather | solution.py:182
  346.6 42.7 %reduce-scatter.25.cloned.1.call-done = bf16[256,1024]{1,0:T(8,128)(2,1)} async-done(((bf16[1024,1024]{1,0:T(8,128)(2,1)}), bf16[256,1024]{1,0:T(8,128)(2,1)}) %reduce-scatter.25.cloned.1.call-update) | async-done | bytes 524304 | tf_op jit(solution)/shard_map/reduce_scatter | solution.py:187
  394.7 44.9 %all-gather.27.cloned.1.call-done = bf16[1024,1024]{1,0:T(8,128)(2,1)} async-done(((bf16[256,1024]{1,0:T(8,128)(2,1)}), bf16[1024,1024]{1,0:T(8,128)(2,1)}) %all-gather.27.cloned.1.call-update) | async-done | bytes 2097168 | tf_op jit(solution)/shard_map/all_gather | solution.py:196
  509.2 44.8 %all-gather.29.cloned.1.call-done = bf16[1024,1024]{1,0:T(8,128)(2,1)} async-done(((bf16[256,1024]{1,0:T(8,128)(2,1)}), bf16[1024,1024]{1,0:T(8,128)(2,1)}) %all-gather.29.cloned.1.call-update) | async-done | bytes 2097168 | tf_op jit(solution)/shard_map/all_gather | solution.py:182
  590.9 42.7 %reduce-scatter.29.cloned.1.call-done = bf16[256,1024]{1,0:T(8,128)(2,1)} async-done(((bf16[1024,1024]{1,0:T(8,128)(2,1)}), bf16[256,1024]{1,0:T(8,128)(2,1)}) %reduce-scatter.29.cloned.1.call-update) | async-done | bytes 524304 | tf_op jit(solution)/shard_map/reduce_scatter | solution.py:187
  638.8 45.1 %all-gather.31.cloned.1.call-done = bf16[1024,1024]{1,0:T(8,128)(2,1)} async-done(((bf16[256,1024]{1,0:T(8,128)(2,1)}), bf16[1024,1024]{1,0:T(8,128)(2,1)}) %all-gather.31.cloned.1.call-update) | async-done | bytes 2097168 | tf_op jit(solution)/shard_map/all_gather | solution.py:196
  753.6 44.8 %all-gather.33.cloned.1.call-done = bf16[1024,1024]{1,0:T(8,128)(2,1)} async-done(((bf16[256,1024]{1,0:T(8,128)(2,1)}), bf16[1024,1024]{1,0:T(8,128)(2,1)}) %all-gather.33.cloned.1.call-update) | async-done | bytes 2097168 | tf_op jit(solution)/shard_map/all_gather | solution.py:182
  833.4 42.7 %reduce-scatter.33.cloned.1.call-done = bf16[256,1024]{1,0:T(8,128)(2,1)} async-done(((bf16[1024,1024]{1,0:T(8,128)(2,1)}), bf16[256,1024]{1,0:T(8,128)(2,1)}) %reduce-scatter.33.cloned.1.call-update) | async-done | bytes 524304 | tf_op jit(solution)/shard_map/reduce_scatter | solution.py:187
  881.6 44.9 %all-gather.35.cloned.1.call-done = bf16[1024,1024]{1,0:T(8,128)(2,1)} async-done(((bf16[256,1024]{1,0:T(8,128)(2,1)}), bf16[1024,1024]{1,0:T(8,128)(2,1)}) %all-gather.35.cloned.1.call-update) | async-done | bytes 2097168 | tf_op jit(solution)/shard_map/all_gather | solution.py:196
  1137.9 45.1 %all-gather.39.cloned.1.call-done = bf16[1024,1024]{1,0:T(8,128)(2,1)} async-done(((bf16[256,1024]{1,0:T(8,128)(2,1)}), bf16[1024,1024]{1,0:T(8,128)(2,1)}) %all-gather.39.cloned.1.call-update) | async-done | bytes 2097168 | tf_op jit(solution)/shard_map/all_gather | solution.py:196
  1411.8 59.7 %while.145 = (s32[]{:T(128)}, f32[1024,4,64]{0,2,1:T(8,128)S(1)}, f32[1024,4,64]{0,2,1:T(8,128)}, f32[2,512,4,64]{1,0,3,2:T(2,128)}, bf16[2,512,4,64]{1,3,2,0:T(...) while((s32[]{:T(128)}, f32[1024,4,64]{0,2,1:T(8,128)S(1)}, ...), condition=%wide.region_60.61_spmd.clone, body=%wide.region_58.60_spmd.clone.sunk | while | flops 1376647168 | bytes 90415552 | solution.py:163
  1483.9 42.7 %reduce-scatter.43.cloned.1.call-done = bf16[256,1024]{1,0:T(8,128)(2,1)} async-done(((bf16[1024,1024]{1,0:T(8,128)(2,1)}), bf16[256,1024]{1,0:T(8,128)(2,1)}) %reduce-scatter.43.cloned.1.call-update) | async-done | bytes 524304 | tf_op jit(solution)/shard_map/reduce_scatter | solution.py:256
  1598.8 42.6 %reduce-scatter.45.cloned.1.call-done = bf16[256,1024]{1,0:T(8,128)(2,1)} async-done(((bf16[1024,1024]{1,0:T(8,128)(2,1)}), bf16[256,1024]{1,0:T(8,128)(2,1)}) %reduce-scatter.45.cloned.1.call-update) | async-done | bytes 524304 | tf_op jit(solution)/shard_map/reduce_scatter | solution.py:228
  1701.4 60.9 %while.146 = (s32[]{:T(128)}, f32[1024,4,64]{0,2,1:T(8,128)S(1)}, f32[1024,4,64]{0,2,1:T(8,128)}, f32[2,512,4,64]{1,0,3,2:T(2,128)}, bf16[2,512,4,64]{1,3,2,0:T(...) while((s32[]{:T(128)}, f32[1024,4,64]{0,2,1:T(8,128)S(1)}, ...), condition=%wide.region_73.74_spmd.clone, body=%wide.region_71.73_spmd.clone.sunk | while | flops 1376647168 | bytes 90284416 | solution.py:163
  1888.2 42.6 %reduce-scatter.49.cloned.1.call-done = bf16[256,1024]{1,0:T(8,128)(2,1)} async-done(((bf16[1024,1024]{1,0:T(8,128)(2,1)}), bf16[256,1024]{1,0:T(8,128)(2,1)}) %reduce-scatter.49.cloned.1.call-update) | async-done | bytes 524304 | tf_op jit(solution)/shard_map/reduce_scatter | solution.py:228
  1990.8 60.9 %while.147 = (s32[]{:T(128)}, f32[1024,4,64]{0,2,1:T(8,128)S(1)}, f32[1024,4,64]{0,2,1:T(8,128)}, f32[2,512,4,64]{1,0,3,2:T(2,128)}, bf16[2,512,4,64]{1,3,2,0:T(...) while((s32[]{:T(128)}, f32[1024,4,64]{0,2,1:T(8,128)S(1)}, ...), condition=%wide.region_86.87_spmd.clone, body=%wide.region_84.86_spmd.clone.sunk | while | flops 1376647168 | bytes 90284416 | solution.py:163
  2175.7 42.6 %reduce-scatter.53.cloned.1.call-done = bf16[256,1024]{1,0:T(8,128)(2,1)} async-done(((bf16[1024,1024]{1,0:T(8,128)(2,1)}), bf16[256,1024]{1,0:T(8,128)(2,1)}) %reduce-scatter.53.cloned.1.call-update) | async-done | bytes 524304 | tf_op jit(solution)/shard_map/reduce_scatter | solution.py:228
  2277.8 61.0 %while.148 = (s32[]{:T(128)}, f32[1024,4,64]{0,2,1:T(8,128)S(1)}, f32[1024,4,64]{0,2,1:T(8,128)}, f32[2,512,4,64]{1,0,3,2:T(2,128)}, bf16[2,512,4,64]{1,3,2,0:T(...) while((s32[]{:T(128)}, f32[1024,4,64]{0,2,1:T(8,128)S(1)}, ...), condition=%wide.region_99.100_spmd.clone, body=%wide.region_97.99_spmd.clone.sunk | while | flops 1376647168 | bytes 90284416 | solution.py:163
  2571.2 60.8 %while.149 = (s32[]{:T(128)}, f32[1024,4,64]{0,2,1:T(8,128)S(1)}, f32[1024,4,64]{0,2,1:T(8,128)}, f32[2,512,4,64]{1,0,3,2:T(2,128)}, bf16[2,512,4,64]{1,3,2,0:T(...) while((s32[]{:T(128)}, f32[1024,4,64]{0,2,1:T(8,128)S(1)}, ...), condition=%wide.region_112.113_spmd.clone, body=%wide.region_110.112_spmd.clone.sunk | while | flops 1376647168 | bytes 90284416 | solution.py:163
  2687.0 76.5 %psum.39 = f32[1,4,1024]{2,1,0:T(4,128)} all-reduce(f32[1,4,1024]{2,1,0:T(4,128)S(1)} %fusion.875), channel_id=1, replica_groups=mesh['section'=2,'dp'=4,'tensor'=4] {'dp','tensor'}, use_global_device_ids=true, to_apply=%region_139.140 | all-reduce | flops 4096 | bytes 32768 | tf_op jit(solution)/shard_map/psum | solution.py:346
  2766.6 62.6 %all-reduce.3.cloned.1.call-done = (bf16[1,1024,3,256]{3,1,2,0:T(8,128)(2,1)}, bf16[1,256,1024]{2,1,0:T(8,128)(2,1)}, bf16[1,1024,1024]{2,1,0:T(8,128)(2,1)}, bf16[1,1024,1024]{2,1,0:T(8,128)(2,1)}) async-done(((bf16[1,1024,3,256]{3,1,2,0:T(8,128)(2,1)}, bf16[1,256,1024]{2,1,0:T(8,128)(2,1)}, bf16[1,1024,1024]{2,1,0:T(8,128)(2,1)}, bf16[1,1024,1024]{2,1,0:T(8,128)(2,1)}), ...) | async-done | bytes 6291472 | tf_op jit(solution)/shard_map/psum | solution.py:341
  (1394 shorter events, 2067.1 us)
Async XLA Ops:
  12.2 128.2 %reduce-scatter.21.cloned.1.call-start = ((), (), s32[]{:S(2)}) async-start(), calls=%async_computation.21 | async-start | bytes 2621440 | tf_op jit(solution)/shard_map/reduce_scatter | solution.py:187
  145.6 103.6 %reduce-scatter.23.cloned.1.call-start = ((), (), s32[]{:S(2)}) async-start(), calls=%async_computation.23 | async-start | bytes 2621440 | tf_op jit(solution)/shard_map/reduce_scatter | solution.py:200
  206.4 103.3 %all-gather.25.cloned.1.call-start = ((), (), s32[]{:S(2)}) async-start(), calls=%async_computation.24 | async-start | bytes 2621440 | tf_op jit(solution)/shard_map/all_gather | solution.py:182
  264.1 125.2 %reduce-scatter.25.cloned.1.call-start = ((), (), s32[]{:S(2)}) async-start(), calls=%async_computation.25 | async-start | bytes 2621440 | tf_op jit(solution)/shard_map/reduce_scatter | solution.py:187
  394.2 103.6 %reduce-scatter.27.cloned.1.call-start = ((), (), s32[]{:S(2)}) async-start(), calls=%async_computation.27 | async-start | bytes 2621440 | tf_op jit(solution)/shard_map/reduce_scatter | solution.py:200
  508.4 125.2 %reduce-scatter.29.cloned.1.call-start = ((), (), s32[]{:S(2)}) async-start(), calls=%async_computation.29 | async-start | bytes 2621440 | tf_op jit(solution)/shard_map/reduce_scatter | solution.py:187
  638.5 103.6 %reduce-scatter.31.cloned.1.call-start = ((), (), s32[]{:S(2)}) async-start(), calls=%async_computation.31 | async-start | bytes 2621440 | tf_op jit(solution)/shard_map/reduce_scatter | solution.py:200
  752.7 123.5 %reduce-scatter.33.cloned.1.call-start = ((), (), s32[]{:S(2)}) async-start(), calls=%async_computation.33 | async-start | bytes 2621440 | tf_op jit(solution)/shard_map/reduce_scatter | solution.py:187
  881.1 103.6 %reduce-scatter.35.cloned.1.call-start = ((), (), s32[]{:S(2)}) async-start(), calls=%async_computation.35 | async-start | bytes 2621440 | tf_op jit(solution)/shard_map/reduce_scatter | solution.py:200
  995.2 131.9 %reduce-scatter.37.cloned.1.call-start = ((), (), s32[]{:S(2)}) async-start(), calls=%async_computation.37 | async-start | bytes 2621440 | tf_op jit(solution)/shard_map/reduce_scatter | solution.py:187
  1137.6 103.6 %reduce-scatter.39.cloned.1.call-start = ((), (), s32[]{:S(2)}) async-start(), calls=%async_computation.39 | async-start | bytes 2621440 | tf_op jit(solution)/shard_map/reduce_scatter | solution.py:200
  1250.1 101.6 %reduce-scatter.41.cloned.1.call-start = ((), (), s32[]{:S(2)}) async-start(), calls=%async_computation.41 | async-start | bytes 2621440 | tf_op jit(solution)/shard_map/reduce_scatter | solution.py:228
  1361.9 164.7 %reduce-scatter.43.cloned.1.call-start = ((), (), s32[]{:S(2)}) async-start(), calls=%async_computation.43 | async-start | bytes 2621440 | tf_op jit(solution)/shard_map/reduce_scatter | solution.py:256
  1483.8 101.7 %all-gather.45.cloned.1.call-start = ((), (), s32[]{:S(2)}) async-start(), calls=%async_computation.44 | async-start | bytes 2621440 | tf_op jit(solution)/shard_map/all_gather | solution.py:221
  1540.1 101.3 %reduce-scatter.45.cloned.1.call-start = ((), (), s32[]{:S(2)}) async-start(), calls=%async_computation.45 | async-start | bytes 2621440 | tf_op jit(solution)/shard_map/reduce_scatter | solution.py:228
  1651.5 166.0 %reduce-scatter.47.cloned.1.call-start = ((), (), s32[]{:S(2)}) async-start(), calls=%async_computation.47 | async-start | bytes 2621440 | tf_op jit(solution)/shard_map/reduce_scatter | solution.py:256
  1829.5 101.3 %reduce-scatter.49.cloned.1.call-start = ((), (), s32[]{:S(2)}) async-start(), calls=%async_computation.49 | async-start | bytes 2621440 | tf_op jit(solution)/shard_map/reduce_scatter | solution.py:228
  1940.9 164.1 %reduce-scatter.51.cloned.1.call-start = ((), (), s32[]{:S(2)}) async-start(), calls=%async_computation.51 | async-start | bytes 2621440 | tf_op jit(solution)/shard_map/reduce_scatter | solution.py:256
  2117.0 101.3 %reduce-scatter.53.cloned.1.call-start = ((), (), s32[]{:S(2)}) async-start(), calls=%async_computation.53 | async-start | bytes 2621440 | tf_op jit(solution)/shard_map/reduce_scatter | solution.py:228
  2228.0 164.2 %reduce-scatter.55.cloned.1.call-start = ((), (), s32[]{:S(2)}) async-start(), calls=%async_computation.55 | async-start | bytes 2621440 | tf_op jit(solution)/shard_map/reduce_scatter | solution.py:256
  2349.4 101.0 %all-gather.57.cloned.1.call-start = ((), (), s32[]{:S(2)}) async-start(), calls=%async_computation.56 | async-start | bytes 2621440 | tf_op jit(solution)/shard_map/all_gather | solution.py:221
  2405.0 107.3 %reduce-scatter.57.cloned.1.call-start = ((), (), s32[]{:S(2)}) async-start(), calls=%async_computation.57 | async-start | bytes 2621440 | tf_op jit(solution)/shard_map/reduce_scatter | solution.py:228
  2521.3 163.8 %reduce-scatter.59.cloned.1.call-start = ((), (), s32[]{:S(2)}) async-start(), calls=%async_computation.59 | async-start | bytes 2621440 | tf_op jit(solution)/shard_map/reduce_scatter | solution.py:256
  2642.3 186.8 %all-reduce.3.cloned.1.call-start = ((), (), s32[]{:S(2)}) async-start(), calls=%async_computation.60 | async-start | bytes 12582912 | tf_op jit(solution)/shard_map/psum | solution.py:341
  (348 other events, 9725.6 us)
Sparse Core Ops, SparseCore 0:
  12.3 48.6 all-gather.20
  145.7 45.2 all-gather.22
  264.2 45.4 all-gather.24
  394.3 45.2 all-gather.26
  508.5 45.5 all-gather.28
  591.0 42.5 reduce-scatter.28
  638.6 45.2 all-gather.30
  752.8 45.5 all-gather.32
  881.2 45.2 all-gather.34
  995.4 45.4 all-gather.36
  1137.7 45.2 all-gather.38
  1250.2 45.2 all-gather.40
  1308.8 42.8 reduce-scatter.40
  1362.0 45.2 all-gather.42
  1540.2 45.2 all-gather.44
  1598.8 42.5 reduce-scatter.44
  1651.6 45.2 all-gather.46
  1829.7 45.2 all-gather.48
  1941.0 45.2 all-gather.50
  2117.1 45.2 all-gather.52
  2228.1 45.2 all-gather.54
  2405.1 45.2 all-gather.56
  2521.4 45.2 all-gather.58
  2689.4 139.7 all-reduce.2
  (17 shorter events, 722.7 us)
where the time goes:
time: 2870 us; the launch traced here: 2850 us
  waiting for transfers between devices  1540 us (54%)
  matrix products  551 us (19%)
  local copies, waits for them, and re-layouts  329 us (11%)
  other arithmetic  309 us (11%)
  blocking collectives  76.5 us (3%)
    all_gather x5, waiting for transfers between devices, layer_forward(): lax.all_gather(normed_mid.astype(jnp.bfloat16), 'tensor', axis=0, tiled=T...  225 us
    all_gather x5, waiting for transfers between devices, layer_forward(): lax.all_gather(normed.astype(jnp.bfloat16), 'tensor', axis=0, tiled=True)  208 us
    reduce_scatter x5, waiting for transfers between devices, layer_forward(): lax.psum_scatter(jnp.dot(attended, weight_out, preferred_element_type=jnp...  208 us
    reduce_scatter x5, waiting for transfers between devices, layer_forward(): lax.psum_scatter(jnp.dot(hidden, weight_down, preferred_element_type=jnp....  191 us
    reduce_scatter x5, waiting for transfers between devices, layer_backward(): lax.psum_scatter(times_transposed(preact_grad, weight_up).astype(jnp.bflo...  174 us
    reduce_scatter x5, waiting for transfers between devices, layer_backward(): lax.psum_scatter(times_transposed(projected_grad, weight_in).astype(jnp.b...  166 us
    all_gather x5, waiting for transfers between devices, layer_backward(): lax.all_gather(branch_grad.astype(jnp.bfloat16), 'tensor', axis=0, tiled=...  160 us
    all_gather x5, waiting for transfers between devices, layer_backward(): lax.all_gather(mixed_grad.astype(jnp.bfloat16), 'tensor', axis=0, tiled=T...  137 us
  transfers between devices with their start and end apart: 49, of which 48 were waited for; matrix products, arithmetic and copies ran while one was open for 10% of the time, Pallas kernels for 0%

commit v1 on v0

--- a/solution.py
+++ b/solution.py
@@ -4,6 +4,8 @@
 import jax
 import jax.numpy as jnp
 from jax import lax
+from jax.experimental import pallas as pl
+from jax.experimental.pallas import tpu as pltpu
 from jax.sharding import PartitionSpec as P
 
 HEAD_DIM = 64
@@ -355,6 +357,514 @@
     )
 
 
+BF16 = jnp.bfloat16
+F32 = jnp.float32
+QROWS = 256
+WINDOW = 512
+
+
+def rope_lanes(length, lanes):
+    half = HEAD_DIM // 2
+    lane = jnp.arange(lanes, dtype=jnp.int32)
+    freqs = ROTARY_BASE ** (-2.0 * jnp.arange(half, dtype=F32) / HEAD_DIM)
+    angles = jnp.arange(length, dtype=F32)[:, None] * freqs[None, :]
+    repeat = lanes // half
+    cosine = jnp.tile(jnp.cos(angles), (1, repeat))
+    sine = jnp.tile(jnp.sin(angles), (1, repeat))
+    first = (lane % HEAD_DIM) < half
+    return (cosine, jnp.where(first[None, :], -sine, sine))
+
+
+def partner(values):
+    lanes = values.shape[-1]
+    half = HEAD_DIM // 2
+    lane = lax.broadcasted_iota(jnp.int32, values.shape, 1)
+    return jnp.where(
+        (lane % HEAD_DIM) < half,
+        pltpu.roll(values, lanes - half, 1),
+        pltpu.roll(values, half, 1),
+    )
+
+
+def head_lanes(shape, head):
+    lane = lax.broadcasted_iota(jnp.int32, shape, 1)
+    return (lane // HEAD_DIM) == head
+
+
+def nt(left, right):
+    return lax.dot_general(left, right, (((1,), (1,)), ((), ())), preferred_element_type=F32)
+
+
+def nn(left, right):
+    return lax.dot_general(left, right, (((1,), (0,)), ((), ())), preferred_element_type=F32)
+
+
+def allowed_keys(row0, rows, key0, keys, seg_col, seg_row):
+    query_at = row0 + lax.broadcasted_iota(jnp.int32, (rows, keys), 0)
+    key_at = key0 + lax.broadcasted_iota(jnp.int32, (rows, keys), 1)
+    same = seg_col[row0 : row0 + rows, :] == seg_row[:, key0 : key0 + keys]
+    return same & (query_at >= key_at)
+
+
+def windows(length):
+    rows = min(QROWS, length)
+    for row0 in range(0, length, rows):
+        key0 = max(0, row0 - WINDOW)
+        yield row0, rows, key0, row0 + rows - key0
+
+
+def attend_kernel(normed, weight, cosine, sine, seg_col, seg_row, qkv, mixed):
+    length = normed.shape[0]
+    lanes = mixed.shape[1]
+    projected = nn(normed[...], weight[...])
+    for part in range(2):
+        raw = projected[:, part * lanes : (part + 1) * lanes]
+        turned = raw * cosine[...] + partner(raw) * sine[...]
+        qkv[:, part * lanes : (part + 1) * lanes] = turned.astype(BF16)
+    qkv[:, 2 * lanes :] = projected[:, 2 * lanes :].astype(BF16)
+    scale = 1.0 / math.sqrt(HEAD_DIM)
+    for row0, rows, key0, keys in windows(length):
+        keep = allowed_keys(row0, rows, key0, keys, seg_col, seg_row)
+        query = qkv[row0 : row0 + rows, :lanes].astype(F32) * scale
+        key = qkv[key0 : key0 + keys, lanes : 2 * lanes]
+        value = qkv[key0 : key0 + keys, 2 * lanes :]
+        total = jnp.zeros((rows, lanes), F32)
+        for head in range(lanes // HEAD_DIM):
+            mine = head_lanes((rows, lanes), head)
+            scores = nt(jnp.where(mine, query, 0.0).astype(BF16), key)
+            scores = jnp.where(keep, scores, NEGATIVE)
+            largest = jnp.max(scores, axis=-1, keepdims=True)
+            exponent = jnp.exp(scores - largest)
+            inverse = 1.0 / jnp.sum(exponent, axis=-1, keepdims=True)
+            probs = (exponent * inverse).astype(BF16)
+            total = jnp.where(mine, nn(probs, value), total)
+        mixed[row0 : row0 + rows, :] = total.astype(BF16)
+
+
+def attend_forward(normed, weight, cosine, sine, seg_col, seg_row, lanes):
+    length, width = normed.shape
+    pieces = weight.shape[1] // (3 * lanes)
+    whole = lambda shape: pl.BlockSpec(shape, lambda j: (0, 0))
+    return pl.pallas_call(
+        attend_kernel,
+        grid=(pieces,),
+        in_specs=[
+            whole((length, width)),
+            pl.BlockSpec((width, 3 * lanes), lambda j: (0, j)),
+            whole((length, lanes)),
+            whole((length, lanes)),
+            whole((length, 1)),
+            whole((1, length)),
+        ],
+        out_specs=[
+            pl.BlockSpec((length, 3 * lanes), lambda j: (0, j)),
+            pl.BlockSpec((length, lanes), lambda j: (0, j)),
+        ],
+        out_shape=[
+            jax.ShapeDtypeStruct((length, pieces * 3 * lanes), BF16),
+            jax.ShapeDtypeStruct((length, pieces * lanes), BF16),
+        ],
+        compiler_params=pltpu.CompilerParams(vmem_limit_bytes=48 * 1024 * 1024),
+        cost_estimate=pl.CostEstimate(
+            flops=pieces * length * 12 * lanes * width,
+            bytes_accessed=2 * length * (width + pieces * 7 * lanes),
+            transcendentals=pieces * 2 * length * length // 2,
+        ),
+    )(normed, weight, cosine, sine, seg_col, seg_row)
+
+
+def attend_back_kernel(qkv, upstream, cosine, sine, seg_col, seg_row, grads, key_acc, value_acc):
+    length = qkv.shape[0]
+    lanes = upstream.shape[1]
+    scale = 1.0 / math.sqrt(HEAD_DIM)
+    key_acc[...] = jnp.zeros_like(key_acc)
+    value_acc[...] = jnp.zeros_like(value_acc)
+    for row0, rows, key0, keys in windows(length):
+        keep = allowed_keys(row0, rows, key0, keys, seg_col, seg_row)
+        query = qkv[row0 : row0 + rows, :lanes].astype(F32) * scale
+        above = upstream[row0 : row0 + rows, :].astype(F32)
+        key = qkv[key0 : key0 + keys, lanes : 2 * lanes]
+        value = qkv[key0 : key0 + keys, 2 * lanes :]
+        query_grad = jnp.zeros((rows, lanes), F32)
+        key_sum = jnp.zeros((lanes, keys), F32)
+        value_sum = jnp.zeros((lanes, keys), F32)
+        for head in range(lanes // HEAD_DIM):
+            mine = head_lanes((rows, lanes), head)
+            query_low = jnp.where(mine, query, 0.0).astype(BF16)
+            above_low = jnp.where(mine, above, 0.0).astype(BF16)
+            scores = jnp.where(keep, nt(query_low, key), NEGATIVE)
+            largest = jnp.max(scores, axis=-1, keepdims=True)
+            exponent = jnp.exp(scores - largest)
+            probs = exponent * (1.0 / jnp.sum(exponent, axis=-1, keepdims=True))
+            prob_grad = nt(above_low, value)
+            centre = jnp.sum(probs * prob_grad, axis=-1, keepdims=True)
+            score_grad = (probs * (prob_grad - centre)).astype(BF16)
+            query_grad = jnp.where(mine, nn(score_grad, key), query_grad)
+            key_sum = key_sum + nn(jnp.where(mine, query, 0.0).T.astype(BF16), score_grad)
+            value_sum = value_sum + nn(
+                jnp.where(mine, above, 0.0).T.astype(BF16), probs.astype(BF16)
+            )
+        key_acc[:, key0 : key0 + keys] += key_sum
+        value_acc[:, key0 : key0 + keys] += value_sum
+        query_grad = query_grad * scale
+        near, far = (cosine[row0 : row0 + rows, :], sine[row0 : row0 + rows, :])
+        grads[row0 : row0 + rows, :lanes] = (query_grad * near - partner(query_grad) * far).astype(
+            BF16
+        )
+    key_grad = key_acc[...].T
+    grads[:, lanes : 2 * lanes] = (key_grad * cosine[...] - partner(key_grad) * sine[...]).astype(
+        BF16
+    )
+    grads[:, 2 * lanes :] = value_acc[...].T.astype(BF16)
+
+
+def attend_backward(qkv, upstream, cosine, sine, seg_col, seg_row, lanes):
+    length = qkv.shape[0]
+    pieces = upstream.shape[1] // lanes
+    whole = lambda shape: pl.BlockSpec(shape, lambda j: (0, 0))
+    return pl.pallas_call(
+        attend_back_kernel,
+        grid=(pieces,),
+        in_specs=[
+            pl.BlockSpec((length, 3 * lanes), lambda j: (0, j)),
+            pl.BlockSpec((length, lanes), lambda j: (0, j)),
+            whole((length, lanes)),
+            whole((length, lanes)),
+            whole((length, 1)),
+            whole((1, length)),
+        ],
+        out_specs=pl.BlockSpec((length, 3 * lanes), lambda j: (0, j)),
+        out_shape=jax.ShapeDtypeStruct((length, pieces * 3 * lanes), BF16),
+        scratch_shapes=[pltpu.VMEM((lanes, length), F32), pltpu.VMEM((lanes, length), F32)],
+        compiler_params=pltpu.CompilerParams(vmem_limit_bytes=48 * 1024 * 1024),
+        cost_estimate=pl.CostEstimate(
+            flops=pieces * 10 * length * length * lanes,
+            bytes_accessed=2 * length * pieces * 7 * lanes,
+            transcendentals=pieces * 2 * length * length // 2,
+        ),
+    )(qkv, upstream, cosine, sine, seg_col, seg_row)
+
+
+def gelu_kernel(rows_ref, weight, hidden, slope):
+    length = rows_ref.shape[0]
+    step = min(QROWS, length)
+    for row0 in range(0, length, step):
+        preact = nn(rows_ref[row0 : row0 + step, :], weight[...])
+        cumulative = 0.5 + 0.5 * lax.erf(preact * (1.0 / math.sqrt(2.0)))
+        density = jnp.exp(preact * preact * -0.5) * (1.0 / math.sqrt(2.0 * math.pi))
+        hidden[row0 : row0 + step, :] = (preact * cumulative).astype(BF16)
+        slope[row0 : row0 + step, :] = (cumulative + preact * density).astype(BF16)
+
+
+def gelu_forward(rows, weight, first, count, block):
+    length, width = rows.shape
+    return pl.pallas_call(
+        gelu_kernel,
+        grid=(count,),
+        in_specs=[
+            pl.BlockSpec((length, width), lambda j: (0, 0)),
+            pl.BlockSpec((width, block), lambda j: (0, first + j)),
+        ],
+        out_specs=[pl.BlockSpec((length, block), lambda j: (0, j))] * 2,
+        out_shape=[jax.ShapeDtypeStruct((length, count * block), BF16)] * 2,
+        compiler_params=pltpu.CompilerParams(vmem_limit_bytes=48 * 1024 * 1024),
+        cost_estimate=pl.CostEstimate(
+            flops=2 * length * width * count * block,
+            bytes_accessed=2 * (length * width + width * count * block + 2 * length * count * block),
+            transcendentals=2 * length * count * block,
+        ),
+    )(rows, weight)
+
+
+def ring(length, by):
+    return [(i, (i + by) % length) for i in range(length)]
+
+
+def other_core(values):
+    return lax.ppermute(values, "section", [(0, 1), (1, 0)])
+
+
+def both_cores(partial_sum):
+    low = partial_sum.astype(BF16)
+    return low.astype(F32) + other_core(low).astype(F32)
+
+
+def pack_rows(blocks, section, tensor, count):
+    _, rows, width = blocks.shape
+    half = rows // 2
+    mine = lambda pack: lax.dynamic_slice(blocks, (pack, section * half, 0), (1, half, width))[0]
+    got = [(tensor, mine(tensor))]
+    for by in range(1, count):
+        sent = mine((tensor + by) % count)
+        got.append(((tensor + count - by) % count, lax.ppermute(sent, "tensor", ring(count, by))))
+    out = jnp.zeros((count, 2, half, width), blocks.dtype)
+    for source, block in got:
+        out = lax.dynamic_update_slice(out, block[None, None], (source, section, 0, 0))
+    owned = jnp.concatenate([block[None] for _, block in got])
+    theirs = other_core(owned)
+    for step in range(count):
+        source = (tensor + count - step) % count
+        out = lax.dynamic_update_slice(
+            out, theirs[step][None, None], (source, 1 - section, 0, 0)
+        )
+    return out.reshape(count * rows, width)
+
+
+def unpack_rows(values, tensor, count):
+    length, width = values.shape
+    rows = length // count
+    out = jnp.zeros((count, rows, width), values.dtype)
+    for by in range(count):
+        target = (tensor + by) % count
+        block = lax.dynamic_slice(values, (target * rows, 0), (rows, width))
+        if by:
+            block = lax.ppermute(block, "tensor", ring(count, by))
+        source = (tensor + count - by) % count
+        out = lax.dynamic_update_slice(out, block[None], (source, 0, 0))
+    return out
+
+
+def gather_weights(own, column, group, count, dp):
+    rows = own.shape[0] // dp
+    piece = lax.dynamic_slice(own, (column * rows, 0), (rows, own.shape[1]))
+    pieces = []
+    for _ in range(count - 1):
+        piece = lax.ppermute(piece, "tensor", ring(count, 1))
+        pieces.append(piece)
+    ordered = []
+    start = 0
+    for size in group:
+        ordered += [item[:, start : start + size] for item in pieces]
+        start += size
+    rest = lax.all_gather(jnp.concatenate(ordered, axis=1), "dp", axis=0, tiled=True)
+    return rest
+
+
+def split_group(own, rest, group, count):
+    out = []
+    start = 0
+    for size in group:
+        out.append(
+            (
+                own[:, start : start + size],
+                rest[:, start * (count - 1) : (start + size) * (count - 1)],
+            )
+        )
+        start += size
+    return out
+
+
+def reduce_weights(parts, group, count):
+    own = jnp.concatenate([part[0] for part in parts], axis=1)
+    rest = jnp.concatenate([part[1] for part in parts], axis=1)
+    whole = jnp.concatenate([own, rest], axis=1)
+    summed = lax.psum_scatter(whole, "dp", scatter_dimension=0, tiled=True)
+    total_size = sum(group)
+
+    def slot(index):
+        if index == 0:
+            return summed[:, :total_size]
+        pieces = []
+        start = 0
+        for size in group:
+            at = total_size + start * (count - 1) + (index - 1) * size
+            pieces.append(summed[:, at : at + size])
+            start += size
+        return jnp.concatenate(pieces, axis=1)
+
+    running = slot(1)
+    for index in range(2, count + 1):
+        arrived = lax.ppermute(running, "tensor", ring(count, 1))
+        running = (arrived.astype(F32) + slot(index % count).astype(F32)).astype(BF16)
+    return lax.all_gather(running, "dp", axis=0, tiled=True)
+
+
+def packed_forward(layer_in, weights, gain_table, tables, lanes, hidden_block):
+    attn, mlp = weights
+    (in_own, in_rest), (out_own, out_rest) = attn
+    (up_own, up_rest), (down_own, down_rest) = mlp
+    inputs_float = layer_in.astype(F32)
+    normed = rms_parts(inputs_float, gain_table[0])[0].astype(BF16)
+    qkv_own, mixed_own = attend_forward(normed, in_own, *tables, lanes)
+    qkv_rest, mixed_rest = attend_forward(normed, in_rest, *tables, lanes)
+    branch = both_cores(nt(mixed_own, out_own) + nt(mixed_rest, out_rest))
+    middle = inputs_float + rms_parts(branch, gain_table[1])[0]
+    normed_mid = rms_parts(middle, gain_table[2])[0].astype(BF16)
+    hid_own, slope_own = gelu_forward(
+        normed_mid, up_own, 0, up_own.shape[1] // hidden_block, hidden_block
+    )
+    hid_rest, slope_rest = gelu_forward(
+        normed_mid, up_rest, 0, up_rest.shape[1] // hidden_block, hidden_block
+    )
+    mixed = both_cores(nt(hid_own, down_own) + nt(hid_rest, down_rest))
+    result = (middle + rms_parts(mixed, gain_table[3])[0]).astype(BF16)
+    kept = (
+        branch,
+        mixed,
+        normed,
+        normed_mid,
+        (qkv_own, qkv_rest),
+        (mixed_own, mixed_rest),
+        (hid_own, hid_rest),
+        (slope_own, slope_rest),
+    )
+    return result, kept
+
+
+def packed_backward(layer_in, weights, gain_table, tables, lanes, kept, upstream, reduce):
+    attn, mlp = weights
+    in_parts, out_parts = attn
+    up_parts, down_parts = mlp
+    branch, mixed, normed, normed_mid, qkv, attended, hidden, slope = kept
+    inputs_float = layer_in.astype(F32)
+    _, in_inverse = rms_parts(inputs_float, gain_table[0])
+    branch_normed, branch_inverse = rms_parts(branch, gain_table[1])
+    middle = inputs_float + branch_normed
+    _, mid_inverse = rms_parts(middle, gain_table[2])
+    _, mixed_inverse = rms_parts(mixed, gain_table[3])
+    mixed_grad, gain_three = rms_back(mixed, mixed_inverse, gain_table[3], upstream)
+    mixed_grad = mixed_grad.astype(BF16)
+    down_grads = [transposed_times(mixed_grad, part).astype(BF16) for part in hidden]
+    preact_grads = [
+        (nn(mixed_grad, weight) * factor.astype(F32)).astype(BF16)
+        for weight, factor in zip(down_parts, slope)
+    ]
+    up_grads = [transposed_times(normed_mid, part).astype(BF16) for part in preact_grads]
+    mlp_sum = reduce((tuple(up_grads), tuple(down_grads)), 1)
+    mid_grad = both_cores(nt(preact_grads[0], up_parts[0]) + nt(preact_grads[1], up_parts[1]))
+    middle_back, gain_two = rms_back(middle, mid_inverse, gain_table[2], mid_grad)
+    middle_grad = upstream + middle_back
+    branch_grad, gain_one = rms_back(branch, branch_inverse, gain_table[1], middle_grad)
+    branch_grad = branch_grad.astype(BF16)
+    out_grads = [transposed_times(branch_grad, part).astype(BF16) for part in attended]
+    attended_grads = [nn(branch_grad, weight).astype(BF16) for weight in out_parts]
+    projected_grads = [
+        attend_backward(part, above, *tables, lanes) for part, above in zip(qkv, attended_grads)
+    ]
+    in_grads = [transposed_times(normed, part).astype(BF16) for part in projected_grads]
+    attn_sum = reduce((tuple(in_grads), tuple(out_grads)), 0)
+    normed_grad = both_cores(
+        nt(projected_grads[0], in_parts[0]) + nt(projected_grads[1], in_parts[1])
+    )
+    input_back, gain_zero = rms_back(inputs_float, in_inverse, gain_table[0], normed_grad)
+    gain_parts = jnp.stack([gain_zero, gain_one, gain_two, gain_three])
+    return middle_grad + input_back, (attn_sum, mlp_sum), gain_parts
+
+
+def per_chip(
+    inputs, segments, projection_in, projection_out, up_weight, down_weight, norm_gains, cotangent
+):
+    section = lax.axis_index("section")
+    column = lax.axis_index("dp")
+    tensor = lax.axis_index("tensor")
+    dp = lax.axis_size("dp")
+    count = lax.axis_size("tensor")
+    width = inputs.shape[3]
+    length = inputs.shape[2] * count
+    lanes = projection_out.shape[1] // 2
+    hidden = up_weight.shape[2] // 2
+    groups = ((3 * lanes, lanes), (hidden, hidden))
+    up_down = down_weight[0].T
+    out_turned = projection_out[0].T
+
+    def half(core):
+        cut = lambda table, size: lax.dynamic_slice(table, (0, core * size), (width, size))
+        attn = [cut(projection_in[0][:, part, :], lanes) for part in range(3)]
+        attn.append(cut(out_turned, lanes))
+        mlp = [cut(up_weight[0], hidden), cut(up_down, hidden)]
+        return [jnp.concatenate(attn, axis=1), jnp.concatenate(mlp, axis=1)]
+
+    keep = half(section)
+    swapped = [other_core(part) for part in half(1 - section)]
+    own = [
+        [jnp.where(section == layer, a, b) for a, b in zip(keep, swapped)] for layer in range(2)
+    ]
+    gains_other = other_core(norm_gains[0])
+    gains = [jnp.where(section == layer, norm_gains[0], gains_other) for layer in range(2)]
+    weights = []
+    for layer in range(2):
+        pair = []
+        for kind in range(2):
+            rest = gather_weights(own[layer][kind], column, groups[kind], count, dp)
+            pair.append(split_group(own[layer][kind], rest, groups[kind], count))
+        weights.append(pair)
+    segment = lax.dynamic_index_in_dim(segments[0], tensor, 0, keepdims=False)
+    cosine, sine = rope_lanes(length, lanes)
+    tables = (cosine, sine, segment[:, None], segment[None, :])
+    layer_in = pack_rows(inputs[0], section, tensor, count)
+    upstream = pack_rows(cotangent[0], section, tensor, count)
+    entering = []
+    saved = []
+    for layer in range(2):
+        entering.append(layer_in)
+        layer_in, kept = packed_forward(
+            layer_in, weights[layer], gains[layer], tables, lanes, min(512, hidden)
+        )
+        saved.append(kept)
+    outputs = jnp.where(section == 0, entering[1], layer_in)
+    layer_store = unpack_rows(outputs, tensor, count)
+
+    def reduce(parts, kind):
+        return reduce_weights(parts, groups[kind], count)
+
+    sums = [None, None]
+    gain_sums = [None, None]
+    input_grads = [None, None]
+    for layer in (1, 0):
+        grad, sums[layer], gain_sums[layer] = packed_backward(
+            entering[layer],
+            weights[layer],
+            gains[layer],
+            tables,
+            lanes,
+            saved[layer],
+            upstream.astype(F32),
+            reduce,
+        )
+        upstream = grad.astype(BF16)
+        input_grads[layer] = upstream
+    grad_store = unpack_rows(
+        jnp.where(section == 0, input_grads[0], input_grads[1]), tensor, count
+    )
+    gain_total = lax.psum(jnp.stack(gain_sums), ("dp", "tensor"))
+    gain_total = jnp.where(section == 0, gain_total[0], gain_total[1])
+    finished = []
+    for kind in range(2):
+        mine = jnp.where(section == 0, sums[0][kind], sums[1][kind])
+        sent = jnp.where(section == 0, sums[1][kind], sums[0][kind])
+        theirs = other_core(sent)
+        finished.append(
+            (jnp.where(section == 0, mine, theirs), jnp.where(section == 0, theirs, mine))
+        )
+    (attn_low, attn_high), (mlp_low, mlp_high) = finished
+    in_grad = jnp.stack(
+        [
+            jnp.concatenate(
+                [item[:, part * lanes : (part + 1) * lanes] for item in (attn_low, attn_high)],
+                axis=1,
+            )
+            for part in range(3)
+        ],
+        axis=1,
+    ).astype(F32)
+    out_grad = jnp.concatenate([attn_low[:, 3 * lanes :], attn_high[:, 3 * lanes :]], axis=1)
+    up_grad = jnp.concatenate([mlp_low[:, :hidden], mlp_high[:, :hidden]], axis=1).astype(F32)
+    down_grad = jnp.concatenate([mlp_low[:, hidden:], mlp_high[:, hidden:]], axis=1)
+    return (
+        layer_store[None, None],
+        grad_store[None, None],
+        in_grad[None],
+        out_grad.T.astype(F32)[None],
+        up_grad[None],
+        down_grad.T.astype(F32)[None],
+        gain_total[None],
+    )
+
+
+def one_pack_per_chip(mesh):
+    return mesh.shape["section"] == 2 and mesh.shape["tensor"] == 4 and mesh.shape["dp"] == 4
+
+
 def solution(mesh):
     placed = (
         P("dp", None, "tensor", None),
@@ -366,8 +876,9 @@
         P("section", None, None),
         P("dp", None, "tensor", None),
     )
+    body = per_chip if one_pack_per_chip(mesh) else per_device
     return jax.shard_map(
-        per_device,
+        body,
         mesh=mesh,
         in_specs=placed,
         out_specs=(

time: 2870 us -> 1010 us (0.35)
  waiting for transfers between devices: 1540 us -> 351 us
  matrix products: 551 us -> 110 us
  local copies, waits for them, and re-layouts: 329 us -> 120 us
  other arithmetic: 309 us -> 134 us
  Pallas kernels: 0 us -> 114 us
  blocking collectives: 76.5 us -> 107 us
    all_gather x20 -> x8, waiting for transfers between devices: 730 us -> 0.07 us  [the longest x4 0.04 us: reduce_weights(): return lax.all_gather(running, 'dp', axis=0, tiled=True)]
    reduce_scatter x20 -> x4, waiting for transfers between devices: 738 us -> 100 us  [reduce_weights(): summed = lax.psum_scatter(whole, 'dp', scatter_dimension=0, tiled=True)]
    dot_general x115 -> x24, matrix products: 449 us -> 73.1 us  [the longest x16 55.6 us: nt(): lax.dot_general(left, right, (((1,), (1,)), ((), ())), preferred_element_...]
    ppermute x8 -> x51, waiting for transfers between devices: 11.8 us -> 251 us  [the longest x12 108 us: gather_weights(): piece = lax.ppermute(piece, 'tensor', ring(count, 1))]
    pallas_call x0 -> x12, Pallas kernels: none -> 114 us  [the longest x4 49.6 us: attend_backward(): pl.pallas_call(attend_back_kernel, grid=(pieces,), in_specs=[pl.BlockSpec...]
    dynamic_update_slice x41 -> x22, local copies, waits for them, and re-layouts: 137 us -> 28 us  [the longest x8 15.2 us: unpack_rows(): out = lax.dynamic_update_slice(out, block[None], (source, 0, 0))]
    dynamic_update_slice x54 -> x0, other arithmetic: 68.9 us -> none  [the longest x44 65.2 us: put_slot(): return lax.dynamic_update_index_in_dim(buffer, merged, slot, 0)]
    dot_general x20 -> x16, matrix products: 102 us -> 37.1 us  [transposed_times(): lax.dot_general(left, right, (((0,), (0,)), ((), ())), preferred_element_...]
  transfers between devices with their start and end apart: 49 -> 63, of which waited for: 48 -> 31; matrix products, arithmetic and copies ran while one was open for 10% -> 28% of each run, Pallas kernels for 0% -> 9%
where the time goes in v1:
time: 1010 us; the launch traced here: 998 us
  waiting for transfers between devices  351 us (35%)
  other arithmetic  134 us (13%)
  local copies, waits for them, and re-layouts  120 us (12%)
  Pallas kernels  114 us (11%)
  matrix products  110 us (11%)
  blocking collectives  107 us (11%)
  starting transfers between devices  44.9 us (4%)
  between operations  17.2 us (2%)
    ppermute x12, waiting for transfers between devices, gather_weights(): piece = lax.ppermute(piece, 'tensor', ring(count, 1))  108 us
    psum x1, blocking collectives, per_chip(): gain_total = lax.psum(jnp.stack(gain_sums), ('dp', 'tensor'))  107 us
    ppermute x12, waiting for transfers between devices, reduce_weights(): arrived = lax.ppermute(running, 'tensor', ring(count, 1))  102 us
    reduce_scatter x4, waiting for transfers between devices, reduce_weights(): summed = lax.psum_scatter(whole, 'dp', scatter_dimension=0, tiled=True)  100 us
    dot_general x16, matrix products, nt(): lax.dot_general(left, right, (((1,), (1,)), ((), ())), preferred_element_...  55.6 us
    pallas_call x4, Pallas kernels, attend_backward(): pl.pallas_call(attend_back_kernel, grid=(pieces,), in_specs=[pl.BlockSpec...  49.6 us
    pallas_call x4, Pallas kernels, attend_forward(): pl.pallas_call(attend_kernel, grid=(pieces,), in_specs=[whole((length, wi...  42.9 us
    unnamed x282, local copies, waits for them, and re-layouts  40.8 us
  transfers between devices with their start and end apart: 63, of which 31 were waited for; matrix products, arithmetic and copies ran while one was open for 28% of the time, Pallas kernels for 9%

profile of v1, /device:TPU:0, one launch (start us, length us, event | category | flops | bytes accessed | tf_op | source)
XLA Modules:
  0.0 998.0 jit_solution(7746058815286882327)
XLA Ops:
  56.7 13.4 %collective-permute-done.11 = bf16[256,1024]{1,0:T(8,128)(2,1)S(1)} collective-permute-done((bf16[256,1024]{1,0:T(8,128)(2,1)S(1)}, bf16[256,1024]{1,0:T(8,128)(2,1)S(1)}, u32[]{:S(2)}, u32[]{:S(2)}) %collective-permute-start.11) | collective-permute-done | bytes 524320 | tf_op jit(solution)/shard_map/ppermute | solution.py:632
  70.1 12.5 %collective-permute-done.12 = bf16[256,1024]{1,0:T(8,128)(2,1)S(1)} collective-permute-done((bf16[256,1024]{1,0:T(8,128)(2,1)S(1)}, bf16[256,1024]{1,0:T(8,128)(2,1)S(1)}, u32[]{:S(2)}, u32[]{:S(2)}) %collective-permute-start.12) | collective-permute-done | bytes 524320 | tf_op jit(solution)/shard_map/ppermute | solution.py:632
  82.7 11.5 %collective-permute-done.13 = bf16[256,1024]{1,0:T(8,128)(2,1)S(1)} collective-permute-done((bf16[256,1024]{1,0:T(8,128)(2,1)S(1)}, bf16[256,1024]{1,0:T(8,128)(2,1)S(1)}, u32[]{:S(2)}, u32[]{:S(2)}) %collective-permute-start.13) | collective-permute-done | bytes 524320 | tf_op jit(solution)/shard_map/ppermute | solution.py:632
  172.3 16.7 %shard_map.136 = (bf16[1024,1152]{1,0:T(8,128)(2,1)}, bf16[1024,384]{1,0:T(8,128)(2,1)S(1)}) custom-call(bf16[1024,1024]{1,0:T(8,128)(2,1)S(1)} %fusion.28.normed, bf16[1024,1152]{1,0:T(8,128)(2,1)} %slice.433.weight, f32[1024,128]{1,0:T(8,128)S(1)} %copy-done.16, f32[1024,128]{1,0:T(8,128)S(1)} %copy-done.21, s32[1024,1]{1,0:T(8,128)S(1)} %copy.44.seg_col, ...), custom_call_target="tpu_custom_call" | custom-call | flops 4831838208 | bytes 7602176 | tf_op jit(solution)/shard_map/pallas_call | solution.py:448
  193.1 16.5 %collective-permute-done.20 = bf16[256,1024]{1,0:T(8,128)(2,1)S(1)} collective-permute-done((bf16[256,1024]{1,0:T(8,128)(2,1)}, bf16[256,1024]{1,0:T(8,128)(2,1)S(1)}, u32[]{:S(2)}, u32[]{:S(2)}) %collective-permute-start.20) | collective-permute-done | bytes 524320 | tf_op jit(solution)/shard_map/ppermute | solution.py:632
  212.2 12.9 %collective-permute-done.21 = bf16[256,1024]{1,0:T(8,128)(2,1)S(1)} collective-permute-done((bf16[256,1024]{1,0:T(8,128)(2,1)S(1)}, bf16[256,1024]{1,0:T(8,128)(2,1)S(1)}, u32[]{:S(2)}, u32[]{:S(2)}) %collective-permute-start.21) | collective-permute-done | bytes 524320 | tf_op jit(solution)/shard_map/ppermute | solution.py:632
  250.4 8.4 shard_map.138
  286.4 16.6 %shard_map.140 = (bf16[1024,1152]{1,0:T(8,128)(2,1)}, bf16[1024,384]{1,0:T(8,128)(2,1)S(1)}) custom-call(bf16[1024,1024]{1,0:T(8,128)(2,1)S(1)} %fusion.14.normed, bf16[1024,1152]{1,0:T(8,128)(2,1)} %slice.457.weight, f32[1024,128]{1,0:T(8,128)S(1)} %copy-done.17, f32[1024,128]{1,0:T(8,128)S(1)} %copy-done.22, s32[1024,1]{1,0:T(8,128)S(1)} %copy-done.14, ...), custom_call_target="tpu_custom_call" | custom-call | flops 4831838208 | bytes 7602176 | tf_op jit(solution)/shard_map/pallas_call | solution.py:448
  323.7 9.7 shard_map.142
  398.2 19.0 %shard_map.144 = bf16[1024,1152]{1,0:T(8,128)(2,1)S(1)} custom-call(bf16[1024,1152]{1,0:T(8,128)(2,1)} %get-tuple-element.34.qkv, bf16[1024,384]{1,0:T(8,128)(2,1)S(1)} %convolution_convert_fusion.15.upstream, f32[1024,128]{1,0:T(8,128)S(1)} %copy-done.18, f32[1024,128]{1,0:T(8,128)S(1)} %copy-done.23, s32[1024,1]{1,0:T(8,128)S(1)} %copy-done.14, ...), custom_call_target="tpu_custom_call" | custom-call | flops 4026531840 | bytes 5505024 | tf_op jit(solution)/shard_map/pallas_call | solution.py:525
  489.3 18.9 %shard_map.146 = bf16[1024,1152]{1,0:T(8,128)(2,1)S(1)} custom-call(bf16[1024,1152]{1,0:T(8,128)(2,1)} %get-tuple-element.38.qkv, bf16[1024,384]{1,0:T(8,128)(2,1)S(1)} %convolution_convert_fusion.14.upstream, f32[1024,128]{1,0:T(8,128)S(1)} %copy-done.19, f32[1024,128]{1,0:T(8,128)S(1)} %copy-done.24, s32[1024,1]{1,0:T(8,128)S(1)} %copy-done.14, ...), custom_call_target="tpu_custom_call" | custom-call | flops 4026531840 | bytes 5505024 | tf_op jit(solution)/shard_map/pallas_call | solution.py:525
  551.1 9.9 collective-permute-done.40
  561.2 9.7 collective-permute-done.41
  573.3 8.8 collective-permute-done.42
  586.2 67.7 %reduce-scatter.11.cloned.1.call-done = bf16[256,4096]{1,0:T(8,128)(2,1)} async-done(((bf16[1024,4096]{1,0:T(8,128)(2,1)}), bf16[256,4096]{1,0:T(8,128)(2,1)}) %reduce-scatter.11.cloned.1.call-update) | async-done | bytes 2097168 | tf_op jit(solution)/shard_map/reduce_scatter | solution.py:661
  659.4 18.2 %collective-permute-done.39 = bf16[256,512]{1,0:T(8,128)(2,1)S(1)} collective-permute-done((bf16[256,512]{1,0:T(8,128)(2,1)S(1)}, bf16[256,512]{1,0:T(8,128)(2,1)S(1)}, u32[]{:S(2)}, u32[]{:S(2)}) %collective-permute-start.39) | collective-permute-done | bytes 262176 | tf_op jit(solution)/shard_map/ppermute | solution.py:677
  680.9 14.6 %collective-permute-done.48 = bf16[256,1024]{1,0:T(8,128)(2,1)S(1)} collective-permute-done((bf16[256,1024]{1,0:T(8,128)(2,1)S(1)}, bf16[256,1024]{1,0:T(8,128)(2,1)S(1)}, u32[]{:S(2)}, u32[]{:S(2)}) %collective-permute-start.48) | collective-permute-done | bytes 524320 | tf_op jit(solution)/shard_map/ppermute | solution.py:677
  699.0 10.4 %collective-permute-done.49 = bf16[256,1024]{1,0:T(8,128)(2,1)S(1)} collective-permute-done((bf16[256,1024]{1,0:T(8,128)(2,1)S(1)}, bf16[256,1024]{1,0:T(8,128)(2,1)S(1)}, u32[]{:S(2)}, u32[]{:S(2)}) %collective-permute-start.49) | collective-permute-done | bytes 524320 | tf_op jit(solution)/shard_map/ppermute | solution.py:677
  711.5 32.3 %reduce-scatter.9.cloned.1.call-done = bf16[256,4096]{1,0:T(8,128)(2,1)} async-done(((bf16[1024,4096]{1,0:T(8,128)(2,1)}), bf16[256,4096]{1,0:T(8,128)(2,1)}) %reduce-scatter.9.cloned.1.call-update) | async-done | bytes 2097168 | tf_op jit(solution)/shard_map/reduce_scatter | solution.py:661
  765.9 12.0 %collective-permute-done.45 = bf16[256,1024]{1,0:T(8,128)(2,1)S(1)} collective-permute-done((bf16[256,1024]{1,0:T(8,128)(2,1)S(1)}, bf16[256,1024]{1,0:T(8,128)(2,1)S(1)}, u32[]{:S(2)}, u32[]{:S(2)}) %collective-permute-start.45) | collective-permute-done | bytes 524320 | tf_op jit(solution)/shard_map/ppermute | solution.py:677
  791.3 9.3 collective-permute-done.46
  802.9 18.1 %collective-permute-done.24 = bf16[256,1024]{1,0:T(8,128)(2,1)} collective-permute-done((bf16[256,1024]{1,0:T(8,128)(2,1)S(1)}, bf16[256,1024]{1,0:T(8,128)(2,1)}, u32[]{:S(2)}, u32[]{:S(2)}) %collective-permute-start.24) | collective-permute-done | bytes 524320 | tf_op jit(solution)/shard_map/ppermute | solution.py:621
  834.9 9.8 collective-permute-start.34
  847.1 107.1 %psum.7 = f32[2,4,1024]{2,1,0:T(4,128)S(1)} all-reduce(f32[2,4,1024]{2,1,0:T(4,128)S(1)} %pad_maximum_fusion.14), channel_id=1, replica_groups=mesh['section'=2,'dp'=4,'tensor'=4] {'dp','tensor'}, use_global_device_ids=true, to_apply=%region_28.29 | all-reduce | flops 8192 | bytes 65536 | tf_op jit(solution)/shard_map/psum | solution.py:829
  (613 shorter events, 496.8 us)
Async XLA Ops:
  7.2 161.8 %all-gather.9.cloned.1.call-start = ((), (), s32[]{:S(2)}) async-start(), calls=%async_computation.4 | async-start | bytes 3932160 | tf_op jit(solution)/shard_map/all_gather | solution.py:639
  50.9 195.7 %all-gather.11.cloned.1.call-start = ((), (), s32[]{:S(2)}) async-start(), calls=%async_computation.5 | async-start | bytes 7864320 | tf_op jit(solution)/shard_map/all_gather | solution.py:639
  95.5 171.2 %all-gather.13.cloned.1.call-start = ((), (), s32[]{:S(2)}) async-start(), calls=%async_computation.6 | async-start | bytes 3932160 | tf_op jit(solution)/shard_map/all_gather | solution.py:639
  152.1 161.8 %all-gather.15.cloned.1.call-start = ((), (), s32[]{:S(2)}) async-start(), calls=%async_computation.7 | async-start | bytes 7864320 | tf_op jit(solution)/shard_map/all_gather | solution.py:639
  193.1 36.5 %collective-permute-start.9 = (bf16[1024,1024]{1,0:T(8,128)(2,1)}, bf16[1024,1024]{1,0:T(8,128)(2,1)}, u32[]{:S(2)}, u32[]{:S(2)}) collective-permute-start(bf16[1024,1024]{1,0:T(8,128)(2,1)} %add_convert_fusion.9), channel_id=1, source_target_pairs={{0,16},{16,0},{1,17},{17,1},{2,18},{18,2},{3,19},{19,3},{4,20},{20... | collective-permute-start | bytes 6291464 | tf_op jit(solution)/shard_map/ppermute | solution.py:584
  229.1 318.9 %reduce-scatter.7.cloned.1.call-start = ((), (), s32[]{:S(2)}) async-start(), calls=%async_computation.10 | async-start | bytes 5242880 | tf_op jit(solution)/shard_map/reduce_scatter | solution.py:661
  309.0 34.1 %collective-permute-start.26 = (bf16[128,1024]{1,0:T(8,128)(2,1)}, bf16[128,1024]{1,0:T(8,128)(2,1)}, u32[]{:S(2)}, u32[]{:S(2)}) collective-permute-start(bf16[128,1024]{1,0:T(8,128)(2,1)} %get-tuple-element.104), channel_id=1, source_target_pairs={{0,1},{1,2},{2,3},{3,0},{4,5},{5,6},{6,7},{7,4},{8,9},{9,10},{10,1... | collective-permute-start | bytes 786440 | tf_op jit(solution)/shard_map/ppermute | solution.py:599
  309.0 34.1 %collective-permute-start.27 = (bf16[128,1024]{1,0:T(8,128)(2,1)}, bf16[128,1024]{1,0:T(8,128)(2,1)}, u32[]{:S(2)}, u32[]{:S(2)}) collective-permute-start(bf16[128,1024]{1,0:T(8,128)(2,1)} %get-tuple-element.107), channel_id=1, source_target_pairs={{0,2},{1,3},{2,0},{3,1},{4,6},{5,7},{6,4},{7,5},{8,10},{9,11},{10,... | collective-permute-start | bytes 786440 | tf_op jit(solution)/shard_map/ppermute | solution.py:599
  309.0 34.1 %collective-permute-start.28 = (bf16[128,1024]{1,0:T(8,128)(2,1)}, bf16[128,1024]{1,0:T(8,128)(2,1)}, u32[]{:S(2)}, u32[]{:S(2)}) collective-permute-start(bf16[128,1024]{1,0:T(8,128)(2,1)} %get-tuple-element.106), channel_id=1, source_target_pairs={{0,3},{1,0},{2,1},{3,2},{4,7},{5,4},{6,5},{7,6},{8,11},{9,8},{10,9... | collective-permute-start | bytes 786440 | tf_op jit(solution)/shard_map/ppermute | solution.py:599
  432.8 138.2 %reduce-scatter.5.cloned.1.call-start = ((), (), s32[]{:S(2)}) async-start(), calls=%async_computation.8 | async-start | bytes 5242880 | tf_op jit(solution)/shard_map/reduce_scatter | solution.py:661
  513.8 140.2 %reduce-scatter.11.cloned.1.call-start = ((), (), s32[]{:S(2)}) async-start(), calls=%async_computation.14 | async-start | bytes 10485760 | tf_op jit(solution)/shard_map/reduce_scatter | solution.py:661
  530.4 213.3 %reduce-scatter.9.cloned.1.call-start = ((), (), s32[]{:S(2)}) async-start(), calls=%async_computation.12 | async-start | bytes 10485760 | tf_op jit(solution)/shard_map/reduce_scatter | solution.py:661
  548.0 410.3 %all-gather.19.cloned.1.call-start = ((), (), s32[]{:S(2)}) async-start(), calls=%async_computation.11 | async-start | bytes 1310720 | tf_op jit(solution)/shard_map/all_gather | solution.py:679
  583.8 374.5 %all-gather.17.cloned.1.call-start = ((), (), s32[]{:S(2)}) async-start(), calls=%async_computation.9 | async-start | bytes 1310720 | tf_op jit(solution)/shard_map/all_gather | solution.py:679
  586.2 71.5 %collective-permute-start.38 = (bf16[256,512]{1,0:T(8,128)(2,1)}, bf16[256,512]{1,0:T(8,128)(2,1)S(1)}, u32[]{:S(2)}, u32[]{:S(2)}) collective-permute-start(bf16[256,512]{1,0:T(8,128)(2,1)} %add_convert_fusion.21), channel_id=1, source_target_pairs={{0,1},{1,2},{2,3},{3,0},{4,5},{5,6},{6,7},{7,4},{8,9},{9,10},{10,1... | collective-permute-start | bytes 786440 | tf_op jit(solution)/shard_map/ppermute | solution.py:677
  679.3 280.4 %all-gather.23.cloned.1.call-start = ((), (), s32[]{:S(2)}) async-start(), calls=%async_computation.15 | async-start | bytes 2621440 | tf_op jit(solution)/shard_map/all_gather | solution.py:679
  711.4 248.3 %all-gather.21.cloned.1.call-start = ((), (), s32[]{:S(2)}) async-start(), calls=%async_computation.13 | async-start | bytes 2621440 | tf_op jit(solution)/shard_map/all_gather | solution.py:679
  753.1 71.7 %collective-permute-start.33 = (bf16[1024,1024]{1,0:T(8,128)(2,1)}, bf16[1024,1024]{1,0:T(8,128)(2,1)}, u32[]{:S(2)}, u32[]{:S(2)}) collective-permute-start(bf16[1024,1024]{1,0:T(8,128)(2,1)} %add_convert_fusion), channel_id=1, source_target_pairs={{0,16},{16,0},{1,17},{17,1},{2,18},{18,2},{3,19},{19,3},{4,20},{20... | collective-permute-start | bytes 6291464 | tf_op jit(solution)/shard_map/ppermute | solution.py:584
  764.8 24.7 %collective-permute-start.23 = (bf16[256,1024]{1,0:T(8,128)(2,1)}, bf16[256,1024]{1,0:T(8,128)(2,1)}, u32[]{:S(2)}, u32[]{:S(2)}) collective-permute-start(bf16[256,1024]{1,0:T(8,128)(2,1)} %get-tuple-element.110), channel_id=1, source_target_pairs={{0,1},{1,2},{2,3},{3,0},{4,5},{5,6},{6,7},{7,4},{8,9},{9,10},{10,1... | collective-permute-start | bytes 1572872 | tf_op jit(solution)/shard_map/ppermute | solution.py:621
  778.9 42.1 %collective-permute-start.24 = (bf16[256,1024]{1,0:T(8,128)(2,1)S(1)}, bf16[256,1024]{1,0:T(8,128)(2,1)}, u32[]{:S(2)}, u32[]{:S(2)}) collective-permute-start(bf16[256,1024]{1,0:T(8,128)(2,1)S(1)} %get-tuple-element.109), channel_id=1, source_target_pairs={{0,2},{1,3},{2,0},{3,1},{4,6},{5,7},{6,4},{7,5},{8,10},{9,11},{10,... | collective-permute-start | bytes 1572872 | tf_op jit(solution)/shard_map/ppermute | solution.py:621
  779.2 43.7 %collective-permute-start.25 = (bf16[256,1024]{1,0:T(8,128)(2,1)S(1)}, bf16[256,1024]{1,0:T(8,128)(2,1)}, u32[]{:S(2)}, u32[]{:S(2)}) collective-permute-start(bf16[256,1024]{1,0:T(8,128)(2,1)S(1)} %get-tuple-element.108), channel_id=1, source_target_pairs={{0,3},{1,0},{2,1},{3,2},{4,7},{5,4},{6,5},{7,6},{8,11},{9,8},{10,9... | collective-permute-start | bytes 1572872 | tf_op jit(solution)/shard_map/ppermute | solution.py:621
  834.9 127.2 %collective-permute-start.34 = (bf16[256,1024]{1,0:T(8,128)(2,1)}, bf16[256,1024]{1,0:T(8,128)(2,1)}, u32[]{:S(2)}, u32[]{:S(2)}) collective-permute-start(bf16[256,1024]{1,0:T(8,128)(2,1)} %get-tuple-element.102), channel_id=1, source_target_pairs={{0,1},{1,2},{2,3},{3,0},{4,5},{5,6},{6,7},{7,4},{8,9},{9,10},{10,1... | collective-permute-start | bytes 1572872 | tf_op jit(solution)/shard_map/ppermute | solution.py:621
  844.7 119.4 %collective-permute-start.35 = (bf16[256,1024]{1,0:T(8,128)(2,1)}, bf16[256,1024]{1,0:T(8,128)(2,1)}, u32[]{:S(2)}, u32[]{:S(2)}) collective-permute-start(bf16[256,1024]{1,0:T(8,128)(2,1)} %get-tuple-element.101), channel_id=1, source_target_pairs={{0,2},{1,3},{2,0},{3,1},{4,6},{5,7},{6,4},{7,5},{8,10},{9,11},{10,... | collective-permute-start | bytes 1572872 | tf_op jit(solution)/shard_map/ppermute | solution.py:621
  846.3 119.6 %collective-permute-start.36 = (bf16[256,1024]{1,0:T(8,128)(2,1)}, bf16[256,1024]{1,0:T(8,128)(2,1)}, u32[]{:S(2)}, u32[]{:S(2)}) collective-permute-start(bf16[256,1024]{1,0:T(8,128)(2,1)} %get-tuple-element.100), channel_id=1, source_target_pairs={{0,3},{1,0},{2,1},{3,2},{4,7},{5,4},{6,5},{7,6},{8,11},{9,8},{10,9... | collective-permute-start | bytes 1572872 | tf_op jit(solution)/shard_map/ppermute | solution.py:621
  (169 other events, 2079.5 us)
Sparse Core Ops, SparseCore 0:
  51.0 41.6 all-gather.8
  95.6 69.0 all-gather.10
  166.6 43.9 all-gather.12
  229.3 66.6 all-gather.14
  433.0 50.5 reduce-scatter.6
  513.9 50.5 reduce-scatter.4
  567.5 86.3 reduce-scatter.10
  657.3 86.4 reduce-scatter.8
  745.6 26.6 all-gather.18
  773.9 26.6 all-gather.16
  802.4 35.2 all-gather.22
  839.5 35.2 all-gather.20

commit v2 on v0

--- a/solution.py
+++ b/solution.py
@@ -4,6 +4,8 @@
 import jax
 import jax.numpy as jnp
 from jax import lax
+from jax.experimental import pallas as pl
+from jax.experimental.pallas import tpu as pltpu
 from jax.sharding import PartitionSpec as P
 
 HEAD_DIM = 64
@@ -355,6 +357,1223 @@
     )
 
 
+BF16 = jnp.bfloat16
+F32 = jnp.float32
+QROWS = 256
+COLUMNS = 4
+ROOMY = pltpu.CompilerParams(vmem_limit_bytes=56 * 1024 * 1024)
+WINDOW = 512
+BYTES_PER_MICRO = 3400000
+COLUMN_DEPTH = 2
+TENSOR_DEPTH = 2
+
+
+def cost(micros):
+    return pl.CostEstimate(
+        flops=int(micros * 3e8), bytes_accessed=int(micros * BYTES_PER_MICRO), transcendentals=0
+    )
+
+
+def rope_lanes(length, lanes):
+    half = HEAD_DIM // 2
+    lane = jnp.arange(lanes, dtype=jnp.int32)
+    freqs = ROTARY_BASE ** (-2.0 * jnp.arange(half, dtype=F32) / HEAD_DIM)
+    angles = jnp.arange(length, dtype=F32)[:, None] * freqs[None, :]
+    repeat = lanes // half
+    cosine = jnp.tile(jnp.cos(angles), (1, repeat))
+    sine = jnp.tile(jnp.sin(angles), (1, repeat))
+    first = (lane % HEAD_DIM) < half
+    return (cosine, jnp.where(first[None, :], -sine, sine))
+
+
+def partner(values):
+    lanes = values.shape[-1]
+    half = HEAD_DIM // 2
+    lane = lax.broadcasted_iota(jnp.int32, values.shape, 1)
+    return jnp.where(
+        (lane % HEAD_DIM) < half,
+        pltpu.roll(values, lanes - half, 1),
+        pltpu.roll(values, half, 1),
+    )
+
+
+def head_lanes(shape, head):
+    lane = lax.broadcasted_iota(jnp.int32, shape, 1)
+    return (lane // HEAD_DIM) == head
+
+
+def nt(left, right):
+    return lax.dot_general(left, right, (((1,), (1,)), ((), ())), preferred_element_type=F32)
+
+
+def nn(left, right):
+    return lax.dot_general(left, right, (((1,), (0,)), ((), ())), preferred_element_type=F32)
+
+
+def allowed_keys(row0, rows, key0, keys, seg_col, seg_row):
+    query_at = row0 + lax.broadcasted_iota(jnp.int32, (rows, keys), 0)
+    key_at = key0 + lax.broadcasted_iota(jnp.int32, (rows, keys), 1)
+    same = seg_col[row0 : row0 + rows, :] == seg_row[:, key0 : key0 + keys]
+    return same & (query_at >= key_at)
+
+
+def windows(length):
+    rows = min(QROWS, length)
+    for row0 in range(0, length, rows):
+        key0 = max(0, row0 - WINDOW)
+        yield row0, rows, key0, row0 + rows - key0
+
+
+def attend_kernel(normed, weight, cosine, sine, seg_col, seg_row, qkv, mixed):
+    length = normed.shape[0]
+    lanes = mixed.shape[1]
+    projected = nn(normed[...], weight[...])
+    for part in range(2):
+        raw = projected[:, part * lanes : (part + 1) * lanes]
+        turned = raw * cosine[...] + partner(raw) * sine[...]
+        qkv[:, part * lanes : (part + 1) * lanes] = turned.astype(BF16)
+    qkv[:, 2 * lanes :] = projected[:, 2 * lanes :].astype(BF16)
+    scale = 1.0 / math.sqrt(HEAD_DIM)
+    for row0, rows, key0, keys in windows(length):
+        keep = allowed_keys(row0, rows, key0, keys, seg_col, seg_row)
+        query = qkv[row0 : row0 + rows, :lanes].astype(F32) * scale
+        key = qkv[key0 : key0 + keys, lanes : 2 * lanes]
+        value = qkv[key0 : key0 + keys, 2 * lanes :]
+        total = jnp.zeros((rows, lanes), F32)
+        for head in range(lanes // HEAD_DIM):
+            mine = head_lanes((rows, lanes), head)
+            scores = nt(jnp.where(mine, query, 0.0).astype(BF16), key)
+            scores = jnp.where(keep, scores, NEGATIVE)
+            largest = jnp.max(scores, axis=-1, keepdims=True)
+            exponent = jnp.exp(scores - largest)
+            inverse = 1.0 / jnp.sum(exponent, axis=-1, keepdims=True)
+            probs = (exponent * inverse).astype(BF16)
+            total = jnp.where(mine, nn(probs, value), total)
+        mixed[row0 : row0 + rows, :] = total.astype(BF16)
+
+
+def attend_forward(normed, weight, tables, lanes, first, count, kept=()):
+    length, width = normed.shape
+    pieces = weight.shape[1] // (3 * lanes)
+    whole = lambda shape: pl.BlockSpec(shape, lambda j: (0, 0))
+
+    def kernel(*refs):
+        attend_kernel(*refs[:6], *refs[6 + len(kept) :])
+
+    return pl.pallas_call(
+        kernel,
+        grid=(count,),
+        in_specs=[
+            whole((length, width)),
+            pl.BlockSpec((width, 3 * lanes), lambda j: (0, first + j)),
+            whole((length, lanes)),
+            whole((length, lanes)),
+            whole((length, 1)),
+            whole((1, length)),
+        ]
+        + [pl.BlockSpec(memory_space=pl.ANY)] * len(kept),
+        out_specs=[
+            pl.BlockSpec((length, 3 * lanes), lambda j: (0, first + j)),
+            pl.BlockSpec((length, lanes), lambda j: (0, first + j)),
+        ],
+        out_shape=[
+            jax.ShapeDtypeStruct((length, pieces * 3 * lanes), BF16),
+            jax.ShapeDtypeStruct((length, pieces * lanes), BF16),
+        ],
+        input_output_aliases={6 + at: at for at in range(len(kept))},
+        compiler_params=ROOMY,
+        cost_estimate=cost(13),
+    )(normed, weight, *tables, *kept)
+
+
+def tn(left, right):
+    return lax.dot_general(left, right, (((0,), (0,)), ((), ())), preferred_element_type=F32)
+
+
+def attend_back_kernel(
+    carried,
+    place,
+    branch_grad,
+    normed,
+    qkv,
+    attended,
+    w_in,
+    w_out,
+    cosine,
+    sine,
+    seg_col,
+    seg_row,
+    *refs,
+):
+    before, refs = refs[:carried], refs[carried:]
+    outs, (normed_grad, grads, key_acc, value_acc, total) = refs[:-5], refs[-5:]
+    step = pl.program_id(0)
+    length = qkv.shape[0]
+    lanes = attended.shape[1]
+    scale = 1.0 / math.sqrt(HEAD_DIM)
+
+    @pl.when(step == 0)
+    def _():
+        total[...] = before[-1][...] if carried else jnp.zeros_like(total)
+
+    key_acc[...] = jnp.zeros_like(key_acc)
+    value_acc[...] = jnp.zeros_like(value_acc)
+    for row0, rows, key0, keys in windows(length):
+        keep = allowed_keys(row0, rows, key0, keys, seg_col, seg_row)
+        query = qkv[row0 : row0 + rows, :lanes].astype(F32) * scale
+        above = nn(branch_grad[row0 : row0 + rows, :], w_out[...]).astype(BF16).astype(F32)
+        key = qkv[key0 : key0 + keys, lanes : 2 * lanes]
+        value = qkv[key0 : key0 + keys, 2 * lanes :]
+        query_grad = jnp.zeros((rows, lanes), F32)
+        key_sum = jnp.zeros((lanes, keys), F32)
+        value_sum = jnp.zeros((lanes, keys), F32)
+        for head in range(lanes // HEAD_DIM):
+            mine = head_lanes((rows, lanes), head)
+            query_mine = jnp.where(mine, query, 0.0)
+            above_mine = jnp.where(mine, above, 0.0)
+            scores = jnp.where(keep, nt(query_mine.astype(BF16), key), NEGATIVE)
+            largest = jnp.max(scores, axis=-1, keepdims=True)
+            exponent = jnp.exp(scores - largest)
+            probs = exponent * (1.0 / jnp.sum(exponent, axis=-1, keepdims=True))
+            prob_grad = nt(above_mine.astype(BF16), value)
+            centre = jnp.sum(probs * prob_grad, axis=-1, keepdims=True)
+            score_grad = (probs * (prob_grad - centre)).astype(BF16)
+            query_grad = jnp.where(mine, nn(score_grad, key), query_grad)
+            key_sum = key_sum + nn(query_mine.T.astype(BF16), score_grad)
+            value_sum = value_sum + nn(above_mine.T.astype(BF16), probs.astype(BF16))
+        key_acc[:, key0 : key0 + keys] += key_sum
+        value_acc[:, key0 : key0 + keys] += value_sum
+        query_grad = query_grad * scale
+        near, far = (cosine[row0 : row0 + rows, :], sine[row0 : row0 + rows, :])
+        grads[row0 : row0 + rows, :lanes] = (query_grad * near - partner(query_grad) * far).astype(
+            BF16
+        )
+    key_grad = key_acc[...].T
+    grads[:, lanes : 2 * lanes] = (key_grad * cosine[...] - partner(key_grad) * sine[...]).astype(
+        BF16
+    )
+    grads[:, 2 * lanes :] = value_acc[...].T.astype(BF16)
+    width = normed.shape[1]
+    block = width // COLUMNS
+    targets = [(out, slice(0, out.shape[0])) for out in outs]
+    if len(outs) == 1:
+        owners = [place[1] ^ block_mask(at, place[0]) for at in range(COLUMNS)]
+        targets = [(outs[0], spot(owner, block)) for owner in owners]
+    low = 0
+    for out, rows in targets:
+        high = low + (block if len(outs) == 1 else out.shape[0])
+        out[rows, : 3 * lanes] = tn(normed[:, low:high], grads[...]).astype(BF16)
+        out[rows, 3 * lanes :] = tn(branch_grad[:, low:high], attended[...]).astype(BF16)
+        low = high
+    for row0 in range(0, length, QROWS):
+        total[row0 : row0 + QROWS, :] += nt(grads[row0 : row0 + QROWS, :], w_in[...])
+
+    @pl.when(step == pl.num_programs(0) - 1)
+    def _():
+        normed_grad[...] = total[...].astype(normed_grad.dtype)
+
+
+def attend_backward(
+    place,
+    branch_grad,
+    normed,
+    qkv,
+    attended,
+    w_in,
+    w_out,
+    tables,
+    lanes,
+    heights,
+    first,
+    count,
+    kept=(),
+):
+    length, width = normed.shape
+    pieces = attended.shape[1] // lanes
+    last = first + count == pieces
+    whole = lambda shape: pl.BlockSpec(shape, lambda j, place: (0, 0))
+    by_piece = lambda rows, size: pl.BlockSpec((rows, size), lambda j, place: (0, first + j))
+    aliases = {11 + at: at for at in range(len(heights))} if kept else {}
+    specs = [pl.BlockSpec(memory_space=pl.ANY)] * len(heights) + [whole((length, width))]
+    return placed_call(
+        partial(attend_back_kernel, len(kept)),
+        place,
+        (branch_grad, normed, qkv, attended, w_in, w_out, *tables, *kept),
+        [
+            whole((length, width)),
+            whole((length, width)),
+            by_piece(length, 3 * lanes),
+            by_piece(length, lanes),
+            by_piece(width, 3 * lanes),
+            by_piece(width, lanes),
+            whole((length, lanes)),
+            whole((length, lanes)),
+            whole((length, 1)),
+            whole((1, length)),
+        ]
+        + (specs if kept else []),
+        [by_piece(rows, 4 * lanes) for rows in heights] + [whole((length, width))],
+        [((rows, 4 * lanes * pieces), BF16) for rows in heights]
+        + [((length, width), BF16 if last else F32)],
+        (count,),
+        [
+            pltpu.VMEM((length, 3 * lanes), BF16),
+            pltpu.VMEM((lanes, length), F32),
+            pltpu.VMEM((lanes, length), F32),
+            pltpu.VMEM((length, width), F32),
+        ],
+        aliases,
+    )
+
+
+def outward_kernel(values, weight, out):
+    out[...] = nt(values[...], weight[...]).astype(BF16)
+
+
+def outward(values, weight):
+    length, inner = values.shape
+    width = weight.shape[0]
+    return pl.pallas_call(
+        outward_kernel,
+        grid=(length // QROWS,),
+        in_specs=[
+            pl.BlockSpec((QROWS, inner), lambda j: (j, 0)),
+            pl.BlockSpec((width, inner), lambda j: (0, 0)),
+        ],
+        out_specs=pl.BlockSpec((QROWS, width), lambda j: (j, 0)),
+        out_shape=jax.ShapeDtypeStruct((length, width), BF16),
+        compiler_params=ROOMY,
+        cost_estimate=cost(5),
+    )(values, weight)
+
+
+def hidden_kernel(rows_ref, w_up, w_down, hidden, slope, mixed, total):
+    step = pl.program_id(0)
+
+    @pl.when(step == 0)
+    def _():
+        total[...] = jnp.zeros_like(total)
+
+    for row0 in range(0, rows_ref.shape[0], QROWS):
+        rows = slice(row0, row0 + QROWS)
+        preact = nn(rows_ref[rows, :], w_up[...])
+        cumulative = 0.5 + 0.5 * lax.erf(preact * (1.0 / math.sqrt(2.0)))
+        density = jnp.exp(preact * preact * -0.5) * (1.0 / math.sqrt(2.0 * math.pi))
+        hidden[rows, :] = (preact * cumulative).astype(BF16)
+        slope[rows, :] = (cumulative + preact * density).astype(BF16)
+        total[rows, :] += nt(hidden[rows, :], w_down[...])
+
+    @pl.when(step == pl.num_programs(0) - 1)
+    def _():
+        mixed[...] = total[...].astype(BF16)
+
+
+def hidden_forward(rows, w_up, w_down, block):
+    length, width = rows.shape
+    size = w_up.shape[1]
+    whole = pl.BlockSpec((length, width), lambda j: (0, 0))
+    return pl.pallas_call(
+        hidden_kernel,
+        grid=(size // block,),
+        in_specs=[whole] + [pl.BlockSpec((width, block), lambda j: (0, j))] * 2,
+        out_specs=[pl.BlockSpec((length, block), lambda j: (0, j))] * 2 + [whole],
+        out_shape=[jax.ShapeDtypeStruct((length, size), BF16)] * 2
+        + [jax.ShapeDtypeStruct((length, width), BF16)],
+        scratch_shapes=[pltpu.VMEM((length, width), F32)],
+        compiler_params=ROOMY,
+        cost_estimate=cost(19),
+    )(rows, w_up, w_down)
+
+
+def hidden_back_kernel(
+    place,
+    mixed_grad,
+    normed_mid,
+    w_up,
+    w_down,
+    hidden,
+    slope,
+    *refs,
+):
+    outs, (mid_grad, preact_grad, total) = refs[:-3], refs[-3:]
+    step = pl.program_id(0)
+
+    @pl.when(step == 0)
+    def _():
+        total[...] = jnp.zeros_like(total)
+
+    for row0 in range(0, mixed_grad.shape[0], QROWS):
+        rows = slice(row0, row0 + QROWS)
+        back = nn(mixed_grad[rows, :], w_down[...]) * slope[rows, :].astype(F32)
+        preact_grad[rows, :] = back.astype(BF16)
+        total[rows, :] += nt(preact_grad[rows, :], w_up[...])
+    block = mixed_grad.shape[1] // COLUMNS
+    for at in range(COLUMNS):
+        features = slice(block * at, block * (at + 1))
+        if len(outs) == 1:
+            owner = place[1] ^ block_mask(at, place[0])
+            up, down = outs[0].at[spot(2 * owner, block)], outs[0].at[spot(2 * owner + 1, block)]
+        elif at < 3:
+            up, down = outs[at].at[:block], outs[at].at[block:]
+        else:
+            up, down = outs[3:]
+        up[...] = tn(normed_mid[:, features], preact_grad[...]).astype(BF16)
+        down[...] = tn(mixed_grad[:, features], hidden[...]).astype(BF16)
+
+    @pl.when(step == pl.num_programs(0) - 1)
+    def _():
+        mid_grad[...] = total[...].astype(BF16)
+
+
+def hidden_backward(place, mixed_grad, normed_mid, w_up, w_down, hidden, slope, size, heights):
+    length, width = mixed_grad.shape
+    total = hidden.shape[1]
+    whole = pl.BlockSpec((length, width), lambda j, place: (0, 0))
+    column = lambda rows: pl.BlockSpec((rows, size), lambda j, place: (0, j))
+    return placed_call(
+        hidden_back_kernel,
+        place,
+        (mixed_grad, normed_mid, w_up, w_down, hidden, slope),
+        [whole, whole, column(width), column(width), column(length), column(length)],
+        [column(rows) for rows in heights] + [whole],
+        [((rows, total), BF16) for rows in heights] + [((length, width), BF16)],
+        (total // size,),
+        [pltpu.VMEM((length, size), BF16), pltpu.VMEM((length, width), F32)],
+    )
+
+
+def rms_row(values):
+    return lax.rsqrt(jnp.mean(values * values, axis=-1, keepdims=True) + EPSILON)
+
+
+def both(left, right):
+    block = left.shape[1] // COLUMNS
+    turned = [right[:, block * at : block * (at + 1)].astype(F32) for at in (0, 2, 1, 3)]
+    return left[...].astype(F32) + jnp.concatenate(turned, axis=1)
+
+
+def back_row(values, gain, upstream):
+    inverse = rms_row(values)
+    normed = values * inverse
+    scaled = upstream * gain
+    back = inverse * (scaled - normed * jnp.mean(scaled * normed, axis=-1, keepdims=True))
+    product = upstream * normed
+    return back, jnp.sum(product.reshape(-1, 8, product.shape[1]), axis=0)
+
+
+def gather_gain(out, parts):
+    @pl.when(pl.program_id(0) == 0)
+    def _():
+        out[...] = jnp.zeros_like(out)
+
+    for at, part in enumerate(parts):
+        out[at] += part
+
+
+def row_call(kernel, arrays, tables, outs, gains=0):
+    length, width = arrays[0].shape
+    by_row = pl.BlockSpec((QROWS, width), lambda i: (i, 0))
+    out_specs = [by_row] * len(outs)
+    out_shape = [jax.ShapeDtypeStruct((length, width), kind) for kind in outs]
+    if gains:
+        out_specs.append(pl.BlockSpec((gains, 8, width), lambda i: (0, 0, 0)))
+        out_shape.append(jax.ShapeDtypeStruct((gains, 8, width), F32))
+    return pl.pallas_call(
+        kernel,
+        grid=(length // QROWS,),
+        in_specs=[by_row] * len(arrays)
+        + [pl.BlockSpec(table.shape, lambda i: (0, 0)) for table in tables],
+        out_specs=out_specs,
+        out_shape=out_shape,
+        compiler_params=ROOMY,
+        cost_estimate=cost(6),
+    )(*arrays, *tables)
+
+
+def norm_kernel(values, gain, normed):
+    rows = values[...].astype(F32)
+    normed[...] = (rows * rms_row(rows) * gain[0:1, :]).astype(BF16)
+
+
+def middle_row(layer_in, low, other, gain):
+    branch = both(low, other)
+    return layer_in[...].astype(F32) + branch * rms_row(branch) * gain[1:2, :], branch
+
+
+def middle_kernel(layer_in, low, other, gain, normed_mid):
+    middle, _ = middle_row(layer_in, low, other, gain)
+    normed_mid[...] = (middle * rms_row(middle) * gain[2:3, :]).astype(BF16)
+
+
+def result_kernel(layer_in, low, other, mixed_low, mixed_other, gain, follow, result, normed):
+    middle, _ = middle_row(layer_in, low, other, gain)
+    mixed = both(mixed_low, mixed_other)
+    result[...] = (middle + mixed * rms_row(mixed) * gain[3:4, :]).astype(BF16)
+    rows = result[...].astype(F32)
+    normed[...] = (rows * rms_row(rows) * follow[0:1, :]).astype(BF16)
+
+
+def mixed_back_kernel(mixed_low, mixed_other, upstream, gain, mixed_grad, gains):
+    back, part = back_row(
+        both(mixed_low, mixed_other), gain[3:4, :], upstream[...].astype(F32)
+    )
+    mixed_grad[...] = back.astype(BF16)
+    gather_gain(gains, [part])
+
+
+def middle_back_kernel(
+    layer_in, low, other, upstream, mid_low, mid_other, gain, branch_grad, middle_grad, gains
+):
+    middle, branch = middle_row(layer_in, low, other, gain)
+    back, part_two = back_row(middle, gain[2:3, :], both(mid_low, mid_other))
+    total = upstream[...].astype(F32) + back
+    middle_grad[...] = total
+    back, part_one = back_row(branch, gain[1:2, :], total)
+    branch_grad[...] = back.astype(BF16)
+    gather_gain(gains, [part_one, part_two])
+
+
+def input_back_kernel(layer_in, middle_grad, low, other, gain, grad, gains):
+    back, part = back_row(layer_in[...].astype(F32), gain[0:1, :], both(low, other))
+    grad[...] = (middle_grad[...] + back).astype(BF16)
+    gather_gain(gains, [part])
+
+
+def join_kernel(near, arrived, out):
+    out[...] = (near[...].astype(F32) + arrived[...].astype(F32)).astype(BF16)
+
+
+def join_half(near, arrived, half):
+    rows, size = arrived.shape
+    return pl.pallas_call(
+        join_kernel,
+        grid=(4,),
+        in_specs=[
+            pl.BlockSpec((rows, size // 4), lambda j: (half, j)),
+            pl.BlockSpec((rows, size // 4), lambda j: (0, j)),
+        ],
+        out_specs=pl.BlockSpec((rows, size // 4), lambda j: (half, j)),
+        out_shape=jax.ShapeDtypeStruct(near.shape, BF16),
+        input_output_aliases={0: 0},
+        compiler_params=ROOMY,
+        cost_estimate=cost(3.7),
+    )(near, arrived)
+
+
+def total_kernel(count, *refs):
+    sources, slots = refs[:-count], refs[-count:]
+    low = 0
+    for own, from_x, from_y in zip(sources[0::3], sources[1::3], sources[2::3]):
+        high = low + own.shape[0]
+        size = own.shape[1] // count
+        for at, slot in enumerate(slots):
+            part = slice(size * at, size * (at + 1))
+            slot[low:high, :] = (
+                own[:, part].astype(F32) + from_x[:, part].astype(F32) + from_y[:, part].astype(F32)
+            ).astype(BF16)
+        low = high
+
+
+def total_slots(triples, count):
+    sources = [item for triple in triples for item in triple]
+    rows = sum(triple[0].shape[0] for triple in triples)
+    shape = (rows, sources[0].shape[1] // count)
+    return pl.pallas_call(
+        partial(total_kernel, count),
+        out_shape=[jax.ShapeDtypeStruct(shape, BF16)] * count,
+        compiler_params=ROOMY,
+        cost_estimate=cost(5),
+    )(*sources)
+
+
+def ring(length, by):
+    return [(i, (i + by) % length) for i in range(length)]
+
+
+def other_core(values):
+    return lax.ppermute(values, "section", [(0, 1), (1, 0)])
+
+
+def block_mask(at, section):
+    return at ^ (3 * section * ((at ^ (at >> 1)) & 1))
+
+
+def turn_blocks(values, section, column, axis):
+    size = values.shape[axis] // COLUMNS
+    blocks = [
+        lax.dynamic_slice_in_dim(
+            values, (column ^ block_mask(block, section)) * size, size, axis
+        )
+        for block in range(COLUMNS)
+    ]
+    return jnp.concatenate(blocks, axis=axis)
+
+
+def unturn(values, section, column):
+    size = values.shape[1] // COLUMNS
+    blocks = []
+    for block in range(COLUMNS):
+        at = block_mask(column ^ block, section)
+        blocks.append(lax.dynamic_slice_in_dim(values, at * size, size, 1))
+    return jnp.concatenate(blocks, axis=1)
+
+
+class Channel:
+    def __init__(self, depth):
+        self.depth = depth
+        self.sent = []
+
+    def send(self, values, axes, pairs):
+        if len(self.sent) >= self.depth:
+            (values,) = hold([values], self.sent[-self.depth])
+        got = lax.ppermute(values, axes, pairs)
+        self.sent.append(got)
+        return got
+
+
+class Links:
+    def __init__(self, count):
+        self.count = count
+        self.columns = Channel(COLUMN_DEPTH)
+        self.tensor = Channel(TENSOR_DEPTH)
+
+    def across(self, values, masks):
+        pairs = [
+            (core * COLUMNS + at, core * COLUMNS + (at ^ masks[core]))
+            for core in range(2)
+            for at in range(COLUMNS)
+        ]
+        return self.columns.send(values, ("section", "dp"), pairs)
+
+    def near(self, values):
+        return self.across(values, (1, 2))
+
+    def other(self, values):
+        return self.across(values, (2, 1))
+
+    def along(self, values, by):
+        return self.tensor.send(values, "tensor", ring(self.count, by % self.count))
+
+    def relay(self, first, second):
+        half = first.shape[0] // 2
+        return self.other(first[:half]), self.near(second[half:])
+
+
+def spot(index, size):
+    return pl.ds(pl.multiple_of(index * size, size), size)
+
+
+def placed_call(
+    kernel, place, operands, in_specs, out_specs, shapes, grid, scratch=(), aliases=None
+):
+    return pl.pallas_call(
+        kernel,
+        grid_spec=pltpu.PrefetchScalarGridSpec(
+            num_scalar_prefetch=1,
+            grid=grid,
+            in_specs=in_specs,
+            out_specs=out_specs,
+            scratch_shapes=scratch,
+        ),
+        out_shape=[jax.ShapeDtypeStruct(shape, kind) for shape, kind in shapes],
+        input_output_aliases=aliases or {},
+        compiler_params=ROOMY,
+        cost_estimate=cost(6),
+    )(place, *operands)
+
+
+def whole_spec(shape):
+    return pl.BlockSpec(shape, lambda *_: (0,) * len(shape))
+
+
+def slab_kernel(place, *refs):
+    (keep_attn, keep_mlp, send_attn, send_mlp) = refs[8:]
+    lanes = refs[1].shape[0] // 2
+    hidden = refs[3].shape[0] // 2
+    for sources, attn, mlp, core in (
+        (refs[:4], keep_attn, keep_mlp, place[0]),
+        (refs[4:8], send_attn, send_mlp, 1 - place[0]),
+    ):
+        w_in, w_out, w_up, w_down = sources
+        for part in range(3):
+            attn[:, lanes * part : lanes * (part + 1)] = w_in[:, spot(2 * part + core, lanes)]
+        attn[:, 3 * lanes :] = w_out[spot(core, lanes), :].T
+        mlp[:, :hidden] = w_up[:, spot(core, hidden)]
+        mlp[:, hidden:] = w_down[spot(core, hidden), :].T
+
+
+def make_slabs(place, w_in, w_out, w_up, w_down):
+    width = w_in.shape[0]
+    rows = width // COLUMNS
+    lanes, hidden = (w_out.shape[0] // 2, w_down.shape[0] // 2)
+    at = lambda r, place: place[1] ^ block_mask(r, place[0])
+    other = lambda r, place: place[1] ^ block_mask(r, 1 - place[0])
+    by_row = lambda size, which: pl.BlockSpec((rows, size), lambda r, p: (which(r, p), 0))
+    by_column = lambda size, which: pl.BlockSpec((size, rows), lambda r, p: (0, which(r, p)))
+    result = lambda size: pl.BlockSpec((rows, size), lambda r, place: (r, 0))
+    sizes = (4 * lanes, 2 * hidden, 4 * lanes, 2 * hidden)
+    return placed_call(
+        slab_kernel,
+        place,
+        (w_in, w_out, w_up, w_down) * 2,
+        [
+            make(size, which)
+            for which in (at, other)
+            for make, size in (
+                (by_row, 6 * lanes),
+                (by_column, 2 * lanes),
+                (by_row, 2 * hidden),
+                (by_column, 2 * hidden),
+            )
+        ],
+        [result(size) for size in sizes],
+        [((width, size), BF16) for size in sizes],
+        (COLUMNS,),
+    )
+
+
+def enter_kernel(place, owned, theirs, out):
+    count = 4
+    half = owned.shape[0] // count
+    block = out.shape[1] // COLUMNS
+    for by in range(count):
+        source = (place[2] + count - by) % count
+        for held, core in ((owned, place[0]), (theirs, 1 - place[0])):
+            for at in range(COLUMNS):
+                out[spot(2 * source + core, half), block * at : block * (at + 1)] = held[
+                    half * by : half * (by + 1), spot(place[1] ^ block_mask(at, place[0]), block)
+                ]
+
+
+def hold(values, *others):
+    return lax.optimization_barrier((*values, *others))[: len(values)]
+
+
+def send_rows(links, blocks, section, tensor, count, *others):
+    _, rows, width = blocks.shape
+    half = rows // 2
+    mine = lambda pack: lax.dynamic_slice(blocks, (pack, section * half, 0), (1, half, width))[0]
+    sent = hold([mine((tensor + by) % count) for by in range(count)], *others)
+    return [sent[0]] + [links.along(sent[by], by) for by in range(1, count)]
+
+
+def enter_rows(place, got):
+    owned = jnp.concatenate(got)
+    theirs = other_core(owned)
+    shape = (2 * owned.shape[0], owned.shape[1])
+    return placed_call(
+        enter_kernel,
+        place,
+        (owned, theirs),
+        [whole_spec(owned.shape)] * 2,
+        [whole_spec(shape)],
+        [(shape, BF16)],
+        (1,),
+    )[0]
+
+
+def leave_kernel(place, *refs):
+    out = refs[-1]
+    rows = refs[0].shape[0]
+    count = out.shape[0] // rows
+    block = out.shape[1] // COLUMNS
+    for layer in range(2):
+
+        @pl.when(place[0] == layer)
+        def _():
+            start = count * layer if len(refs) > count + 1 else 0
+            for by, held in enumerate(refs[start : start + count]):
+                source = (place[2] + count - by) % count
+                for at in range(COLUMNS):
+                    target = spot(place[1] ^ block_mask(at, layer), block)
+                    out[spot(source, rows), target] = held[:, block * at : block * (at + 1)]
+
+
+def rows_out(values, core, tensor, count, *others):
+    length, width = values.shape
+    rows = length // count
+    blocks = hold(
+        [
+            lax.dynamic_slice(values, (((tensor + by) % count) * rows, 0), (rows, width))
+            for by in range(count)
+        ],
+        *others,
+    )
+    pairs = lambda by: [(core * count + i, core * count + (i + by) % count) for i in range(count)]
+    return [blocks[0]] + [
+        lax.ppermute(blocks[by], ("section", "tensor"), pairs(by)) for by in range(1, count)
+    ]
+
+
+def leave_rows(place, first, second=()):
+    rows, width = first[0].shape
+    count = len(first)
+    shape = (rows * count, width)
+    out = placed_call(
+        leave_kernel,
+        place,
+        (*first, *second),
+        [whole_spec((rows, width))] * (count + len(second)),
+        [whole_spec(shape)],
+        [(shape, BF16)],
+        (1,),
+    )[0]
+    return out.reshape(count, rows, width)
+
+
+def assemble_kernel(layer, pieces, place, keep, theirs, *refs):
+    blocks, outs = refs[:pieces], refs[pieces:]
+    rows = keep.shape[0] // COLUMNS
+
+    def put(target, size, read):
+        start = 0
+        for out in outs:
+            part = out.shape[1] // 4
+            out[target : target + size, read[0] * part : (read[0] + 1) * part] = read[1](
+                start, start + part
+            )
+            start += part
+
+    for mine, held in ((True, keep), (False, theirs)):
+
+        @pl.when((place[0] == layer) == mine)
+        def _():
+            put(0, keep.shape[0], (0, lambda low, high: held[:, low:high]))
+
+    if pieces == 1:
+        for at in range(COLUMNS):
+            owner = place[1] ^ block_mask(at, place[0])
+            for slot in range(3):
+                source = spot(3 * owner + slot, rows)
+                put(rows * at, rows, (slot + 1, lambda low, high: blocks[0][source, low:high]))
+        return
+    own, from_x, from_y, far_low, far_high = blocks
+    half = far_low.shape[0]
+    for at, held in enumerate((own, from_x, from_y)):
+        for slot in range(3):
+            put(
+                rows * at,
+                rows,
+                (slot + 1, lambda low, high: held[rows * slot : rows * (slot + 1), low:high]),
+            )
+    step = rows // 2
+    for chunk in range(6):
+        held, start = (far_low, chunk * step) if chunk < 3 else (far_high, chunk * step - half)
+        put(
+            3 * rows + (chunk % 2) * step,
+            step,
+            (chunk // 2 + 1, lambda low, high: held[start : start + step, low:high]),
+        )
+
+
+def assemble(layer, place, keep, theirs, blocks, parts):
+    operands = (keep, theirs, *blocks)
+    return placed_call(
+        partial(assemble_kernel, layer, len(blocks)),
+        place,
+        operands,
+        [whole_spec(item.shape) for item in operands],
+        [whole_spec((keep.shape[0], 4 * part)) for part in parts],
+        [((keep.shape[0], 4 * part), BF16) for part in parts],
+        (1,),
+    )
+
+
+def add_low(*terms):
+    total = terms[0].astype(F32)
+    for term in terms[1:]:
+        total = total + term.astype(F32)
+    return total.astype(BF16)
+
+
+def finish_kernel(place, *refs):
+    sources, (g_in, g_out, g_up, g_down, attn, mlp, sems) = refs[:8], refs[8:]
+    step = pl.program_id(0)
+    rows = g_in.shape[0]
+    lanes = g_out.shape[0] // 2
+    hidden = g_down.shape[0] // 2
+    core = place[0]
+
+    @pl.when(step == 0)
+    def _():
+        for layer in range(2):
+
+            @pl.when(core == layer)
+            def _():
+                own_attn, own_mlp, got_attn, got_mlp = sources[4 * layer : 4 * layer + 4]
+                copies = [
+                    pltpu.make_async_copy(own_attn, attn.at[layer], sems.at[0]),
+                    pltpu.make_async_copy(got_attn, attn.at[1 - layer], sems.at[1]),
+                    pltpu.make_async_copy(own_mlp, mlp.at[layer], sems.at[2]),
+                    pltpu.make_async_copy(got_mlp, mlp.at[1 - layer], sems.at[3]),
+                ]
+                for copy in copies:
+                    copy.start()
+                for copy in copies:
+                    copy.wait()
+
+    for half in range(2):
+        at = block_mask(place[1] ^ step, half)
+        attn_rows = spot(at, rows)
+        up_rows = spot(2 * at, rows)
+        down_rows = spot(2 * at + 1, rows)
+        for part in range(3):
+            start = (2 * part + half) * lanes
+            g_in[:, start : start + lanes] = attn[
+                half, attn_rows, lanes * part : lanes * (part + 1)
+            ].astype(F32)
+        g_out[lanes * half : lanes * (half + 1), :] = (
+            attn[half, attn_rows, 3 * lanes :].astype(F32).T
+        )
+        g_up[:, hidden * half : hidden * (half + 1)] = mlp[half, up_rows, :].astype(F32)
+        g_down[hidden * half : hidden * (half + 1), :] = mlp[half, down_rows, :].astype(F32).T
+
+
+def finish(place, sources, lanes, hidden):
+    width = sources[0].shape[0]
+    rows = width // COLUMNS
+    return placed_call(
+        finish_kernel,
+        place,
+        sources,
+        [pl.BlockSpec(memory_space=pl.ANY)] * 8,
+        [
+            pl.BlockSpec((rows, 6 * lanes), lambda b, place: (b, 0)),
+            pl.BlockSpec((2 * lanes, rows), lambda b, place: (0, b)),
+            pl.BlockSpec((rows, 2 * hidden), lambda b, place: (b, 0)),
+            pl.BlockSpec((2 * hidden, rows), lambda b, place: (0, b)),
+        ],
+        [
+            ((width, 6 * lanes), F32),
+            ((2 * lanes, width), F32),
+            ((width, 2 * hidden), F32),
+            ((2 * hidden, width), F32),
+        ],
+        (COLUMNS,),
+        [
+            pltpu.VMEM((2, *sources[0].shape), BF16),
+            pltpu.VMEM((2, *sources[1].shape), BF16),
+            pltpu.SemaphoreType.DMA((4,)),
+        ],
+    )
+
+
+class Flow:
+    def __init__(self):
+        self.table = {}
+        self.at = 0
+
+    def plan(self, at, action):
+        self.table.setdefault(max(at, self.at), []).append(action)
+
+    def point(self, token, *inputs):
+        launched = []
+        while self.table.get(self.at):
+            launched += self.table[self.at].pop(0)(token)
+        self.at += 1
+        return hold(inputs, *launched) if launched else inputs
+
+    def drain(self):
+        while any(self.table.values()):
+            at = min(key for key, actions in self.table.items() if actions)
+            self.table[at].pop(0)(None)
+
+
+def held(values, token):
+    return values if token is None else hold(values, token)
+
+
+def column_stage(links, state, token):
+    far_low, far_high = held(state["far"], token)
+    to_x = join_half(state["at_x"], far_low, 0)
+    to_y = join_half(state["at_y"], far_high, 1)
+    state["near"] = (links.near(to_x), links.other(to_y))
+    return [to_x, to_y]
+
+
+def slot_stage(links, states, total, token):
+    count = links.count
+    if "sum" in states[0]:
+        sums = held(tuple(state["sum"] for state in states), token)
+        size = sums[0].shape[1] // count
+        slots = [
+            jnp.concatenate([item[:, size * at : size * (at + 1)] for item in sums])
+            for at in range(count)
+        ]
+    else:
+        slots = total_slots([(state["own"], *held(state["near"], token)) for state in states], count)
+    total["slots"] = slots
+    total["near"] = links.along(slots[2], -1)
+    total["last"] = links.along(slots[3], 1)
+    return slots[2:]
+
+
+def arrive(state, token):
+    (state["sum"],) = held((state["sum"],), token)
+    return [state["sum"]]
+
+
+def relay_stage(links, total, token):
+    (near,) = held((total["near"],), token)
+    relayed = add_low(total["slots"][1], near)
+    total["near"] = links.along(relayed, -1)
+    return [relayed]
+
+
+def spread_stage(links, total, token):
+    came = held((total["near"], total["last"]), token)
+    own = add_low(total["slots"][0], *came)
+    total["blocks"] = (own, links.near(own), links.other(own))
+    return [own]
+
+
+def far_stage(links, total, token):
+    own, from_x, from_y = total["blocks"]
+    from_x, from_y = held((from_x, from_y), token)
+    total["blocks"] = (own, from_x, from_y, *links.relay(from_x, from_y))
+    return []
+
+
+def sum_everywhere(values):
+    swap = lambda axis, by: lax.ppermute(
+        values, axis, [(i, i ^ by) for i in range(lax.axis_size(axis))]
+    )
+    for axis, by in (("dp", 1), ("dp", 2), ("tensor", 1), ("tensor", 2)):
+        values = values + swap(axis, by)
+    return values
+
+
+def per_chip(
+    inputs, segments, projection_in, projection_out, up_weight, down_weight, norm_gains, cotangent
+):
+    section = lax.axis_index("section")
+    column = lax.axis_index("dp")
+    tensor = lax.axis_index("tensor")
+    count = lax.axis_size("tensor")
+    width = inputs.shape[3]
+    length = inputs.shape[2] * count
+    lanes = projection_out.shape[1] // 2
+    hidden = up_weight.shape[2] // 2
+
+    place = jnp.stack([section, column, tensor]).astype(jnp.int32)
+    keep_attn, keep_mlp, send_attn, send_mlp = make_slabs(
+        place,
+        projection_in[0].reshape(width, 6 * lanes),
+        projection_out[0],
+        up_weight[0],
+        down_weight[0],
+    )
+    attn_slabs = (keep_attn, other_core(send_attn))
+    mlp_slabs = (keep_mlp, other_core(send_mlp))
+    gains_other = other_core(norm_gains[0])
+    gains = [
+        turn_blocks(
+            jnp.where(section == layer, norm_gains[0], gains_other), section, column, 1
+        )
+        for layer in range(2)
+    ]
+    rows = width // COLUMNS
+    piece = lambda slabs, layer: jnp.where(section == layer, slabs[0][:rows], slabs[1][:rows])
+    attn_parts, mlp_parts = ((3 * lanes, lanes), (hidden, hidden))
+    links = Links(count)
+    everywhere = lambda values: lax.all_gather(values, "dp", axis=0, tiled=True)
+    hop = lambda values: (links.along(values, 1), links.along(values, -1))
+    segment = lax.dynamic_index_in_dim(segments[0], tensor, 0, keepdims=False)
+    cosine, sine = rope_lanes(length, lanes)
+    tables = (cosine, sine, segment[:, None], segment[None, :])
+
+    block = min(512, hidden)
+    a_first, a_last = hop(piece(attn_slabs, 0))
+    (m_own,) = hold([piece(mlp_slabs, 0)], a_first, a_last, cosine, sine, *gains)
+    a_second = links.along(a_first, 1)
+    m_first, m_last = hop(m_own)
+    a_z = jnp.concatenate([a_first, a_second, a_last])
+    a_x, a_y = links.near(a_z), links.other(a_z)
+    m_second = links.along(m_first, 1)
+    got = send_rows(links, inputs[0], section, tensor, count, m_first, m_last)
+    a_far = links.relay(a_x, a_y)
+    (m_z,) = hold([jnp.concatenate([m_first, m_second, m_last])], *a_far)
+    m_all = everywhere(m_z)
+    w_in, w_out = assemble(0, place, *attn_slabs, (a_z, a_x, a_y, *a_far), attn_parts)
+    got = hold(got, w_out)
+    layer_in = enter_rows(place, got)
+    (b_own,) = hold([piece(attn_slabs, 1)], *got)
+    b_first, b_last = hop(b_own)
+    (normed,) = row_call(norm_kernel, [layer_in], [gains[0]], [BF16])
+    b_second = links.along(b_first, 1)
+    (n_own,) = hold([piece(mlp_slabs, 1)], b_first, b_last)
+    qkv, attended = attend_forward(normed, w_in, tables, lanes, 0, 2)
+    b_second, b_last = hold((b_second, b_last), attended)
+    n_first, n_last = hop(n_own)
+    b_z = jnp.concatenate([b_first, b_second, b_last])
+    b_all = everywhere(b_z)
+    (normed_b,) = hold([normed], b_z, n_own)
+    qkv, attended = attend_forward(normed_b, w_in, tables, lanes, 2, 2, (qkv, attended))
+    n_first, n_last = hold((n_first, n_last), attended)
+    n_second = links.along(n_first, 1)
+    (attended_b,) = hold([attended], n_first)
+    branch = outward(attended_b, w_out)
+    branch = (branch, other_core(branch))
+    (normed_mid,) = row_call(middle_kernel, [layer_in, *branch], [gains[0]], [BF16])
+    m_all, n_second, n_last = hold((m_all, n_second, n_last), normed_mid)
+    w_up, w_down = assemble(0, place, *mlp_slabs, (m_all,), mlp_parts)
+    n_z = jnp.concatenate([n_first, n_second, n_last])
+    n_all = everywhere(n_z)
+    got = send_rows(links, cotangent[0], section, tensor, count, n_z)
+    (normed_b,) = hold([normed_mid], n_z)
+    hid, slope, mixed = hidden_forward(normed_b, w_up, w_down, block)
+    mixed_b, *got = hold([mixed, *got])
+    upstream = enter_rows(place, got)
+    mixed = (mixed_b, other_core(mixed_b))
+    result, normed_next = row_call(
+        result_kernel, [layer_in, *branch, *mixed], [gains[0], gains[1]], [BF16, BF16]
+    )
+    entering = [layer_in, result]
+    weights = [(w_in, w_out, w_up, w_down)]
+    saved = [(branch, mixed, normed, normed_mid, qkv, attended, hid, slope)]
+    b_all, upstream = hold((b_all, upstream), result)
+    w_in, w_out = assemble(1, place, *attn_slabs, (b_all,), attn_parts)
+    layer_in = result
+    normed = normed_next
+    left = [rows_out(entering[1], 0, tensor, count, w_in)]
+    (normed_b,) = hold([normed], left[0][0])
+    qkv, attended = attend_forward(normed_b, w_in, tables, lanes, 0, 4)
+    attended_b, *left[0] = hold([attended, *left[0]])
+    branch = outward(attended_b, w_out)
+    branch = (branch, other_core(branch))
+    (normed_mid,) = row_call(middle_kernel, [layer_in, *branch], [gains[1]], [BF16])
+    (n_all,) = hold([n_all], normed_mid)
+    w_up, w_down = assemble(1, place, *mlp_slabs, (n_all,), mlp_parts)
+    hid, slope, mixed = hidden_forward(normed_mid, w_up, w_down, block)
+    mixed = (mixed, other_core(mixed))
+    result, _ = row_call(
+        result_kernel, [layer_in, *branch, *mixed], [gains[1], gains[1]], [BF16, BF16]
+    )
+    weights.append((w_in, w_out, w_up, w_down))
+    saved.append((branch, mixed, normed, normed_mid, qkv, attended, hid, slope))
+    flow = Flow()
+
+    def plan_totals(layer, states, steps):
+        total = {}
+        totals[layer].append(total)
+        for at, stage in zip(steps, (slot_stage, relay_stage, spread_stage, far_stage)):
+            item = (states, total) if stage is slot_stage else (total,)
+            flow.plan(at, partial(stage, links, *item))
+
+    totals = [[], []]
+    gain_sums = [None, None]
+    input_grads = [None, None]
+
+    def send_grads(token):
+        grads = jnp.where(section == 0, *input_grads)
+        size = grads.shape[0] // count
+        blocks = [
+            lax.dynamic_slice_in_dim(grads, ((tensor + by) % count) * size, size, 0)
+            for by in range(count)
+        ]
+        left.append([blocks[0]] + [links.along(blocks[by], by) for by in range(1, count)])
+        return []
+
+    def reduction(parts):
+        if len(parts) == 1:
+            return {"sum": lax.psum_scatter(parts[0], "dp", scatter_dimension=0, tiled=True)}
+        own, at_x, at_y, far_low, far_high = parts
+        far = (links.other(far_low), links.near(far_high))
+        return {"own": own, "at_x": at_x, "at_y": at_y, "far": far}
+
+    for layer in (1, 0):
+        layer_in = entering[layer]
+        gain = gains[layer]
+        w_in, w_out, w_up, w_down = weights[layer]
+        branch, mixed, normed, normed_mid, qkv, attended, hid, slope = saved[layer]
+        mixed_grad, part_three = row_call(
+            mixed_back_kernel, [*mixed, upstream], [gain], [BF16], 1
+        )
+        (mixed_grad,) = flow.point(mixed_grad, mixed_grad)
+        heights = (2 * rows, 2 * rows, 2 * rows, rows, rows) if layer == 0 else (2 * width,)
+        *parts, mid_low = hidden_backward(
+            place, mixed_grad, normed_mid, w_up, w_down, hid, slope, block, heights
+        )
+        mlp = reduction(parts)
+        (mid_low,) = flow.point(mid_low, mid_low)
+        mid_other = other_core(mid_low)
+        branch_grad, middle_grad, part_two = row_call(
+            middle_back_kernel,
+            [layer_in, *branch, upstream, mid_low, mid_other],
+            [gain],
+            [BF16, F32],
+            2,
+        )
+        if layer == 0:
+            flow.plan(7, partial(column_stage, links, mlp))
+        (branch_grad,) = flow.point(branch_grad, branch_grad)
+        heights = (rows, rows, rows, rows // 2, rows // 2) if layer == 0 else (width,)
+        shared = (normed, qkv, attended, w_in, w_out, tables, lanes, heights)
+        if layer:
+            leaving = rows_out(result, 1, tensor, count, branch_grad)
+            (branch_grad,) = hold([branch_grad], leaving[0])
+            parts = attend_backward(place, branch_grad, *shared, 0, 2)
+            branch_grad, *leaving = hold([branch_grad, *leaving], parts[-1])
+            left.append(leaving)
+            *parts, normed_low = attend_backward(place, branch_grad, *shared, 2, 2, parts)
+        else:
+            *parts, normed_low = attend_backward(place, branch_grad, *shared, 0, 4)
+        attn = reduction(parts)
+        if layer:
+            flow.plan(6, partial(arrive, mlp))
+            plan_totals(1, [mlp, attn], (7, 8, 10, 13))
+        else:
+            flow.plan(9, partial(column_stage, links, attn))
+            plan_totals(0, [mlp], (8, 11, 14, 16))
+            plan_totals(0, [attn], (12, 15, 17, 18))
+            flow.plan(13, send_grads)
+        (normed_low,) = flow.point(normed_low, normed_low)
+        normed_other = other_core(normed_low)
+        grad, part_zero = row_call(
+            input_back_kernel, [layer_in, middle_grad, normed_low, normed_other], [gain], [BF16], 1
+        )
+        (grad,) = flow.point(grad, grad)
+        gain_sums[layer] = jnp.sum(
+            jnp.concatenate([part_zero, part_two, part_three]), axis=1
+        )
+        input_grads[layer] = grad
+        upstream = grad
+    flow.drain()
+    layer_store = leave_rows(place, left[0], left[1])
+    grad_store = leave_rows(place, left[2])
+    gain_total = sum_everywhere(unturn(jnp.concatenate(gain_sums), section, column))
+    gain_total = jnp.where(section == 0, gain_total[:4], gain_total[4:])
+    (both_parts,) = totals[1]
+    own, from_x, from_y, far_low, far_high = both_parts["blocks"]
+    far_rows = jnp.concatenate([far_low, far_high])
+    upper = (own, from_x, from_y, far_rows)
+    sums = [
+        tuple(jnp.concatenate(total["blocks"]) for total in reversed(totals[0])),
+        (
+            jnp.concatenate([item[2 * rows :] for item in upper]),
+            jnp.concatenate([item[: 2 * rows] for item in upper]),
+        ),
+    ]
+    sources = []
+    for layer in range(2):
+        got = [lax.ppermute(item, "section", [(1 - layer, layer)]) for item in sums[layer]]
+        sources += [*sums[layer], *got]
+    in_grad, out_grad, up_grad, down_grad = finish(place, sources, lanes, hidden)
+    return (
+        layer_store[None, None],
+        grad_store[None, None],
+        in_grad.reshape(1, width, 3, 2 * lanes),
+        out_grad[None],
+        up_grad[None],
+        down_grad[None],
+        gain_total[None],
+    )
+
+
+def one_pack_per_chip(mesh):
+    return mesh.shape["section"] == 2 and mesh.shape["tensor"] == 4 and mesh.shape["dp"] == 4
+
+
 def solution(mesh):
     placed = (
         P("dp", None, "tensor", None),
@@ -366,8 +1585,9 @@
         P("section", None, None),
         P("dp", None, "tensor", None),
     )
+    body = per_chip if one_pack_per_chip(mesh) else per_device
     return jax.shard_map(
-        per_device,
+        body,
         mesh=mesh,
         in_specs=placed,
         out_specs=(

time: 2870 us -> 816 us (0.28)
  waiting for transfers between devices: 1540 us -> 213 us
  matrix products: 551 us -> 0 us
  Pallas kernels: 0 us -> 408 us
  other arithmetic: 309 us -> 17.9 us
  local copies, waits for them, and re-layouts: 329 us -> 48.9 us
  starting transfers between devices: 17 us -> 104 us
  blocking collectives: 76.5 us -> 0 us
    reduce_scatter x20 -> x2, waiting for transfers between devices: 738 us -> 0.02 us  [reduction(): lax.psum_scatter(parts[0], 'dp', scatter_dimension=0, tiled=True)]
    all_gather x20 -> x3, waiting for transfers between devices: 730 us -> 0.01 us  [per_chip(): everywhere = lambda values: lax.all_gather(values, 'dp', axis=0, tiled=True)]
    dot_general x135 -> x0, matrix products: 551 us -> none  [the longest x20 102 us: transposed_times(): lax.dot_general(left, right, (((0,), (0,)), ((), ())), preferred_element_...]
    pallas_call x0 -> x39, Pallas kernels: none -> 408 us  [the longest x15 213 us: placed_call(): pl.pallas_call(kernel, grid_spec=pltpu.PrefetchScalarGridSpec(num_scalar_...]
    ppermute x8 -> x81, waiting for transfers between devices: 11.8 us -> 213 us  [the longest x54 181 us: send(): got = lax.ppermute(values, axes, pairs)]
    dynamic_update_slice x41 -> x0, local copies, waits for them, and re-layouts: 137 us -> none  [the longest x20 118 us: attend_back(): lax.scan(one_block, (zeros, zeros), (queries.reshape(blocks, QBLOCK, head...]
    reduce_sum x52 -> x2, other arithmetic: 105 us -> 1.74 us  [per_chip(): jnp.sum(jnp.concatenate([part_zero, part_two, part_three]), axis=1)]
    ppermute x8 -> x81, starting transfers between devices: 11.6 us -> 104 us  [the longest x54 69.8 us: send(): got = lax.ppermute(values, axes, pairs)]
  transfers between devices with their start and end apart: 49 -> 86, of which waited for: 48 -> 37; matrix products, arithmetic and copies ran while one was open for 10% -> 5% of each run, Pallas kernels for 0% -> 40%
where the time goes in v2:
time: 816 us; the launch traced here: 807 us
  Pallas kernels  408 us (50%)
  waiting for transfers between devices  213 us (26%)
  starting transfers between devices  104 us (13%)
  local copies, waits for them, and re-layouts  48.9 us (6%)
  other arithmetic  17.9 us (2%)
  between operations  15.2 us (2%)
    pallas_call x15, Pallas kernels, placed_call(): pl.pallas_call(kernel, grid_spec=pltpu.PrefetchScalarGridSpec(num_scalar_...  213 us
    ppermute x54, waiting for transfers between devices, send(): got = lax.ppermute(values, axes, pairs)  181 us
    pallas_call x11, Pallas kernels, row_call(): pl.pallas_call(kernel, grid=(length // QROWS,), in_specs=[by_row] * len(a...  77.7 us
    ppermute x54, starting transfers between devices, send(): got = lax.ppermute(values, axes, pairs)  69.8 us
    pallas_call x3, Pallas kernels, attend_forward(): pl.pallas_call(kernel, grid=(count,), in_specs=[whole((length, width)), p...  47.9 us
    pallas_call x2, Pallas kernels, hidden_forward(): pl.pallas_call(hidden_kernel, grid=(size // block,), in_specs=[whole] + [...  38.1 us
    unnamed x136, local copies, waits for them, and re-layouts  28.3 us
    ppermute x13, waiting for transfers between devices, other_core(): return lax.ppermute(values, 'section', [(0, 1), (1, 0)])  21.8 us
  transfers between devices with their start and end apart: 86, of which 37 were waited for; matrix products, arithmetic and copies ran while one was open for 5% of the time, Pallas kernels for 40%

profile of v2, /device:TPU:0, one launch (start us, length us, event | category | flops | bytes accessed | tf_op | source)
XLA Modules:
  0.0 806.6 jit_solution(10906902181262763828)
XLA Ops:
  11.1 9.1 %shard_map.135 = (bf16[1024,512]{1,0:T(8,128)(2,1)}, bf16[1024,1024]{1,0:T(8,128)(2,1)}, bf16[1024,512]{1,0:T(8,128)(2,1)}, bf16[1024,1024]{1,0:T(8,128)(2,1)}) custom-call(s32[3]{0:T(128)} %pad_add_fusion.place, bf16[1024,768]{1,0:T(8,128)(2,1)} %copy.25.refs_0_.refs_4_, bf16[256,1024]{1,0:T(8,128)(2,1)} %bitcast.46, bf16[1024,1024]{1,0:T(8,128)(2,1)} %bitcast.41, ...), custom_call_target="tpu_custom_call" | custom-call | flops 1800000000 | bytes 20400000 | tf_op jit(solution)/shard_map/pallas_call | solution.py:969
  28.8 8.6 %collective-permute-done.2 = bf16[256,512]{1,0:T(8,128)(2,1)S(1)} collective-permute-done((bf16[256,512]{1,0:T(8,128)(2,1)S(1)}, bf16[256,512]{1,0:T(8,128)(2,1)S(1)}, u32[]{:S(2)}, u32[]{:S(2)}) %collective-permute-start.2) | collective-permute-done | bytes 262176 | tf_op jit(solution)/shard_map/ppermute | solution.py:929
  58.6 10.3 %collective-permute-done.5 = bf16[256,1024]{1,0:T(8,128)(2,1)S(1)} collective-permute-done((bf16[256,1024]{1,0:T(8,128)(2,1)S(1)}, bf16[256,1024]{1,0:T(8,128)(2,1)S(1)}, u32[]{:S(2)}, u32[]{:S(2)}) %collective-permute-start.5) | collective-permute-done | bytes 524320 | tf_op jit(solution)/shard_map/ppermute | solution.py:929
  80.1 9.6 %collective-permute-done.9 = bf16[256,1024]{1,0:T(8,128)(2,1)S(1)} collective-permute-done((bf16[256,1024]{1,0:T(8,128)(2,1)S(1)}, bf16[256,1024]{1,0:T(8,128)(2,1)S(1)}, u32[]{:S(2)}, u32[]{:S(2)}) %collective-permute-start.9) | collective-permute-done | bytes 524320 | tf_op jit(solution)/shard_map/ppermute | solution.py:929
  91.2 10.0 %collective-permute-done.8 = bf16[128,1024]{1,0:T(8,128)(2,1)S(1)} collective-permute-done((bf16[128,1024]{1,0:T(8,128)(2,1)S(1)}, bf16[128,1024]{1,0:T(8,128)(2,1)S(1)}, u32[]{:S(2)}, u32[]{:S(2)}) %collective-permute-start.8) | collective-permute-done | bytes 262176 | tf_op jit(solution)/shard_map/ppermute | solution.py:929
  138.3 12.7 %shard_map.139 = (bf16[1024,1536]{1,0:T(8,128)(2,1)}, bf16[1024,512]{1,0:T(8,128)(2,1)}) custom-call(bf16[1024,1024]{1,0:T(8,128)(2,1)} %shard_map.138.refs_0_.normed, bf16[1024,1536]{1,0:T(8,128)(2,1)} %get-tuple-element.223.refs_1_.w_in, f32[1024,128]{1,0:T(8,128)} %copy.29.refs_2_.cosine, f32[1024,128]{1,0:T(8,128)} %negate_select_fusion.refs_3_.sine, ...), custom_call_target="tpu_custom_call" | custom-call | flops 3900000000 | bytes 44200000 | tf_op jit(solution)/shard_map/pallas_call | solution.py:463
  156.5 12.8 %shard_map.140 = (bf16[1024,1536]{1,0:T(8,128)(2,1)}, bf16[1024,512]{1,0:T(8,128)(2,1)}) custom-call(bf16[1024,1024]{1,0:T(8,128)(2,1)} %shard_map.138.refs_0_.normed, bf16[1024,1536]{1,0:T(8,128)(2,1)} %get-tuple-element.223.refs_1_.w_in, f32[1024,128]{1,0:T(8,128)} %copy.29.refs_2_.cosine, ...), custom_call_target="tpu_custom_call", output_to_operand_aliasing={{0}: (6, {}), {1}: (7, {})} | custom-call | flops 3900000000 | bytes 44200000 | tf_op jit(solution)/shard_map/pallas_call | solution.py:463
  202.4 8.8 %shard_map.143 = (bf16[1024,2048]{1,0:T(8,128)(2,1)}, bf16[1024,2048]{1,0:T(8,128)(2,1)}) custom-call(s32[3]{0:T(128)} %pad_add_fusion.place, bf16[1024,1024]{1,0:T(8,128)(2,1)} %get-tuple-element.196.keep, bf16[1024,1024]{1,0:T(8,128)(2,1)} %copy-done.2, bf16[3072,1024]{1,0:T(8,128)(2,1)} %all-gather.4.cloned.1.call-done.refs_0_), custom_call_target="tpu_custom_call" | custom-call | flops 1800000000 | bytes 20400000 | tf_op jit(solution)/shard_map/pallas_call | solution.py:969
  213.3 19.4 %shard_map.144 = (bf16[1024,2048]{1,0:T(8,128)(2,1)}, bf16[1024,2048]{1,0:T(8,128)(2,1)}, bf16[1024,1024]{1,0:T(8,128)(2,1)}) custom-call(bf16[1024,1024]{1,0:T(8,128)(2,1)} %shard_map.142.rows_ref.normed_mid, bf16[1024,2048]{1,0:T(8,128)(2,1)} %get-tuple-element.242.w_up, bf16[1024,2048]{1,0:T(8,128)(2,1)} %get-tuple-element.243.w_down), custom_call_target="tpu_custom_call" | custom-call | flops 5699999744 | bytes 64600000 | tf_op jit(solution)/shard_map/pallas_call | solution.py:675
  270.7 22.4 %shard_map.148 = (bf16[1024,1536]{1,0:T(8,128)(2,1)}, bf16[1024,512]{1,0:T(8,128)(2,1)}) custom-call(bf16[1024,1024]{1,0:T(8,128)(2,1)} %get-tuple-element.262.refs_0_.normed, bf16[1024,1536]{1,0:T(8,128)(2,1)} %get-tuple-element.260.refs_1_.w_in, f32[1024,128]{1,0:T(8,128)} %copy.29.refs_2_.cosine, f32[1024,128]{1,0:T(8,128)} %negate_select_fusion.refs_3_.sine, ...), custom_call_target="tpu_custom_call" | custom-call | flops 3900000000 | bytes 44200000 | tf_op jit(solution)/shard_map/pallas_call | solution.py:463
  310.0 8.8 %shard_map.151 = (bf16[1024,2048]{1,0:T(8,128)(2,1)}, bf16[1024,2048]{1,0:T(8,128)(2,1)}) custom-call(s32[3]{0:T(128)} %pad_add_fusion.place, bf16[1024,1024]{1,0:T(8,128)(2,1)} %get-tuple-element.196.keep, bf16[1024,1024]{1,0:T(8,128)(2,1)} %copy-done.2, bf16[3072,1024]{1,0:T(8,128)(2,1)} %all-gather.8.cloned.1.call-done.refs_0_), custom_call_target="tpu_custom_call" | custom-call | flops 1800000000 | bytes 20400000 | tf_op jit(solution)/shard_map/pallas_call | solution.py:969
  318.8 18.7 %shard_map.152 = (bf16[1024,2048]{1,0:T(8,128)(2,1)}, bf16[1024,2048]{1,0:T(8,128)(2,1)}, bf16[1024,1024]{1,0:T(8,128)(2,1)}) custom-call(bf16[1024,1024]{1,0:T(8,128)(2,1)} %shard_map.150.rows_ref.normed_mid, bf16[1024,2048]{1,0:T(8,128)(2,1)} %get-tuple-element.275.w_up, bf16[1024,2048]{1,0:T(8,128)(2,1)} %get-tuple-element.276.w_down), custom_call_target="tpu_custom_call" | custom-call | flops 5699999744 | bytes 64600000 | tf_op jit(solution)/shard_map/pallas_call | solution.py:675
  349.0 26.6 %shard_map.154 = (bf16[2048,2048]{1,0:T(8,128)(2,1)}, bf16[1024,1024]{1,0:T(8,128)(2,1)}) custom-call(s32[3]{0:T(128)} %pad_add_fusion.place, bf16[1024,1024]{1,0:T(8,128)(2,1)} %get-tuple-element.278.mixed_grad, bf16[1024,1024]{1,0:T(8,128)(2,1)} %shard_map.150.rows_ref.normed_mid, bf16[1024,2048]{1,0:T(8,128)(2,1)} %get-tuple-element.275.w_up, ...), custom_call_target="tpu_custom_call" | custom-call | flops 1800000000 | bytes 20400000 | tf_op jit(solution)/shard_map/pallas_call | solution.py:969
  389.2 10.5 %shard_map.155 = (bf16[1024,1024]{1,0:T(8,128)(2,1)}, f32[1024,1024]{1,0:T(8,128)}, f32[2,8,1024]{2,1,0:T(8,128)}) custom-call(bf16[1024,1024]{1,0:T(8,128)(2,1)} %get-tuple-element.254.layer_in, bf16[1024,1024]{1,0:T(8,128)(2,1)} %shard_map.149.low, bf16[1024,1024]{1,0:T(8,128)(2,1)} %copy-done.1, bf16[1024,1024]{1,0:T(8,128)(2,1)} %shard_map.146.upstream, ...), custom_call_target="tpu_custom_call" | custom-call | flops 1800000000 | bytes 20400000 | tf_op jit(solution)/shard_map/pallas_call | solution.py:781
  402.2 26.1 %shard_map.157 = (bf16[1024,2048]{1,0:T(8,128)(2,1)}, f32[1024,1024]{1,0:T(8,128)}) custom-call(s32[3]{0:T(128)} %pad_add_fusion.place, bf16[1024,1024]{1,0:T(8,128)(2,1)} %get-tuple-element.296.branch_grad, bf16[1024,1024]{1,0:T(8,128)(2,1)} %get-tuple-element.262.refs_0_.normed, bf16[1024,1536]{1,0:T(8,128)(2,1)} %get-tuple-element.289.qkv, ...), custom_call_target="tpu_custom_call" | custom-call | flops 1800000000 | bytes 20400000 | tf_op jit(solution)/shard_map/pallas_call | solution.py:969
  428.4 26.6 %shard_map.159 = (bf16[1024,2048]{1,0:T(8,128)(2,1)}, bf16[1024,1024]{1,0:T(8,128)(2,1)}) custom-call(s32[3]{0:T(128)} %pad_add_fusion.place, bf16[1024,1024]{1,0:T(8,128)(2,1)} %get-tuple-element.296.branch_grad, bf16[1024,1024]{1,0:T(8,128)(2,1)} %get-tuple-element.262.refs_0_.normed, ...), custom_call_target="tpu_custom_call", output_to_operand_aliasing={{0}: (11, {})} | custom-call | flops 1800000000 | bytes 20400000 | tf_op jit(solution)/shard_map/pallas_call | solution.py:969
  482.8 27.1 %shard_map.162 = (bf16[512,2048]{1,0:T(8,128)(2,1)}, bf16[512,2048]{1,0:T(8,128)(2,1)}, bf16[512,2048]{1,0:T(8,128)(2,1)}, bf16[256,2048]{1,0:T(8,128)(2,1)}, bf...) custom-call(s32[3]{0:T(128)} %pad_add_fusion.place, bf16[1024,1024]{1,0:T(8,128)(2,1)} %get-tuple-element.300.mixed_grad, ...), custom_call_target="tpu_custom_call" | custom-call | flops 1800000000 | bytes 20400000 | tf_op jit(solution)/shard_map/pallas_call | solution.py:969
  515.6 10.2 %shard_map.163 = (bf16[1024,1024]{1,0:T(8,128)(2,1)}, f32[1024,1024]{1,0:T(8,128)}, f32[2,8,1024]{2,1,0:T(8,128)}) custom-call(bf16[1024,1024]{1,0:T(8,128)(2,1)} %shard_map.137.values.layer_in, bf16[1024,1024]{1,0:T(8,128)(2,1)} %shard_map.141.low, bf16[1024,1024]{1,0:T(8,128)(2,1)} %copy-done, bf16[1024,1024]{1,0:T(8,128)(2,1)} %get-tuple-element.299.upstream, ...), custom_call_target="tpu_custom_call" | custom-call | flops 1800000000 | bytes 20400000 | tf_op jit(solution)/shard_map/pallas_call | solution.py:781
  525.8 11.2 %collective-permute-done.41.arrived = bf16[256,2048]{1,0:T(8,128)(2,1)S(1)} collective-permute-done((bf16[256,2048]{1,0:T(8,128)(2,1)}, bf16[256,2048]{1,0:T(8,128)(2,1)S(1)}, u32[]{:S(2)}, u32[]{:S(2)}) %collective-permute-start.41) | collective-permute-done | bytes 1048608 | tf_op jit(solution)/shard_map/ppermute | solution.py:929
  554.1 44.5 %shard_map.166 = (bf16[256,2048]{1,0:T(8,128)(2,1)}, bf16[256,2048]{1,0:T(8,128)(2,1)}, bf16[256,2048]{1,0:T(8,128)(2,1)}, bf16[128,2048]{1,0:T(8,128)(2,1)}, bf...) custom-call(s32[3]{0:T(128)} %pad_add_fusion.place, bf16[1024,1024]{1,0:T(8,128)(2,1)} %get-tuple-element.320.branch_grad, ...), custom_call_target="tpu_custom_call" | custom-call | flops 1800000000 | bytes 20400000 | tf_op jit(solution)/shard_map/pallas_call | solution.py:969
  611.4 16.5 %collective-permute-done.54 = bf16[768,512]{1,0:T(8,128)(2,1)S(1)} collective-permute-done((bf16[768,512]{1,0:T(8,128)(2,1)S(1)}, bf16[768,512]{1,0:T(8,128)(2,1)S(1)}, u32[]{:S(2)}, u32[]{:S(2)}) %collective-permute-start.54) | collective-permute-done | bytes 786464 | tf_op jit(solution)/shard_map/ppermute | solution.py:929
  645.6 9.6 %collective-permute-done.55 = bf16[512,512]{1,0:T(8,128)(2,1)S(1)} collective-permute-done((bf16[512,512]{1,0:T(8,128)(2,1)}, bf16[512,512]{1,0:T(8,128)(2,1)S(1)}, u32[]{:S(2)}, u32[]{:S(2)}) %collective-permute-start.55) | collective-permute-done | bytes 524320 | tf_op jit(solution)/shard_map/ppermute | solution.py:929
  700.7 12.5 %collective-permute-done.52 = bf16[256,512]{1,0:T(8,128)(2,1)} collective-permute-done((bf16[256,512]{1,0:T(8,128)(2,1)}, bf16[256,512]{1,0:T(8,128)(2,1)}, u32[]{:S(2)}, u32[]{:S(2)}) %collective-permute-start.52) | collective-permute-done | bytes 262176 | tf_op jit(solution)/shard_map/ppermute | solution.py:929
  754.7 10.7 %collective-permute-done.53.refs_1_ = bf16[256,1024]{1,0:T(8,128)(2,1)S(1)} collective-permute-done((bf16[256,1024]{1,0:T(8,128)(2,1)S(1)}, bf16[256,1024]{1,0:T(8,128)(2,1)S(1)}, u32[]{:S(2)}, u32[]{:S(2)}) %collective-permute-start.53) | collective-permute-done | bytes 524320 | tf_op jit(solution)/shard_map/ppermute | solution.py:929
  (401 shorter events, 408.2 us)
Async XLA Ops:
  7.2 190.8 %all-gather.4.cloned.1.call-start = ((), (), s32[]{:S(2)}) async-start(), calls=%async_computation.2 | async-start | bytes 7864320 | tf_op jit(solution)/shard_map/all_gather | solution.py:1379
  20.7 27.7 %collective-permute-start = (bf16[1024,1024]{1,0:T(8,128)(2,1)}, bf16[1024,1024]{1,0:T(8,128)(2,1)S(1)}, u32[]{:S(2)}, u32[]{:S(2)}) collective-permute-start(bf16[1024,1024]{1,0:T(8,128)(2,1)} %get-tuple-element.197), channel_id=1, source_target_pairs={{0,16},{16,0},{1,17},{17,1},{2,18},{18,2},{3,19},{19,3},{4,20},{20... | collective-permute-start | bytes 6291464 | tf_op jit(solution)/shard_map/ppermute | solution.py:894
  90.9 160.4 %all-gather.6.cloned.1.call-start = ((), (), s32[]{:S(2)}) async-start(), calls=%async_computation.3 | async-start | bytes 3932160 | tf_op jit(solution)/shard_map/all_gather | solution.py:1379
  122.7 28.3 %collective-permute-start.19 = (bf16[256,512]{1,0:T(8,128)(2,1)S(1)}, bf16[256,512]{1,0:T(8,128)(2,1)S(1)}, u32[]{:S(2)}, u32[]{:S(2)}) collective-permute-start(bf16[256,512]{1,0:T(8,128)(2,1)S(1)} %copy-done.37), channel_id=1, source_target_pairs={{0,3},{1,0},{2,1},{3,2},{4,7},{5,4},{6,5},{7,6},{8,11},{9,8},{10,9... | collective-permute-start | bytes 786440 | tf_op jit(solution)/shard_map/ppermute | solution.py:929
  152.0 158.0 %all-gather.8.cloned.1.call-start = ((), (), s32[]{:S(2)}) async-start(), calls=%async_computation.4 | async-start | bytes 7864320 | tf_op jit(solution)/shard_map/all_gather | solution.py:1379
  199.3 310.6 %reduce-scatter.3.cloned.1.call-start = ((), (), s32[]{:S(2)}) async-start(), calls=%async_computation.5 | async-start | bytes 10485760 | tf_op jit(solution)/shard_map/reduce_scatter | solution.py:1479
  200.7 32.0 %collective-permute-start.25 = (bf16[128,1024]{1,0:T(8,128)(2,1)S(1)}, bf16[128,1024]{1,0:T(8,128)(2,1)S(1)}, u32[]{:S(2)}, u32[]{:S(2)}) collective-permute-start(bf16[128,1024]{1,0:T(8,128)(2,1)S(1)} %get-tuple-element.249), channel_id=1, source_target_pairs={{0,2},{1,3},{2,0},{3,1},{4,6},{5,7},{6,4},{7,5},{8,10},{9,11},{10,... | collective-permute-start | bytes 786440 | tf_op jit(solution)/shard_map/ppermute | solution.py:929
  259.5 33.7 %collective-permute-start.29 = (bf16[256,1024]{1,0:T(8,128)(2,1)S(1)}, bf16[256,1024]{1,0:T(8,128)(2,1)S(1)}, u32[]{:S(2)}, u32[]{:S(2)}) collective-permute-start(bf16[256,1024]{1,0:T(8,128)(2,1)S(1)} %get-tuple-element.264), channel_id=1, source_target_pairs={{0,1},{1,2},{2,3},{3,0},{4,5},{5,6},{6,7},{7,4},{8,9},{9,10},{10,1... | collective-permute-start | bytes 1572872 | tf_op jit(solution)/shard_map/ppermute | solution.py:1104
  262.0 31.1 %collective-permute-start.30 = (bf16[256,1024]{1,0:T(8,128)(2,1)S(1)}, bf16[256,1024]{1,0:T(8,128)(2,1)S(1)}, u32[]{:S(2)}, u32[]{:S(2)}) collective-permute-start(bf16[256,1024]{1,0:T(8,128)(2,1)S(1)} %get-tuple-element.265), channel_id=1, source_target_pairs={{0,2},{1,3},{2,0},{3,1},{4,6},{5,7},{6,4},{7,5},{8,10},{9,11},{10,... | collective-permute-start | bytes 1572872 | tf_op jit(solution)/shard_map/ppermute | solution.py:1104
  375.6 172.0 %reduce-scatter.5.cloned.1.call-start = ((), (), s32[]{:S(2)}) async-start(), calls=%async_computation.6 | async-start | bytes 5242880 | tf_op jit(solution)/shard_map/reduce_scatter | solution.py:1479
  399.7 28.7 %collective-permute-start.35 = (bf16[256,1024]{1,0:T(8,128)(2,1)S(1)}, bf16[256,1024]{1,0:T(8,128)(2,1)S(1)}, u32[]{:S(2)}, u32[]{:S(2)}) collective-permute-start(bf16[256,1024]{1,0:T(8,128)(2,1)S(1)} %get-tuple-element.286), channel_id=1, source_target_pairs={{16,17},{17,18},{18,19},{19,16},{20,21},{21,22},{22,23},{23,20},{2... | collective-permute-start | bytes 1572872 | tf_op jit(solution)/shard_map/ppermute | solution.py:1104
  400.4 28.0 %collective-permute-start.36 = (bf16[256,1024]{1,0:T(8,128)(2,1)S(1)}, bf16[256,1024]{1,0:T(8,128)(2,1)S(1)}, u32[]{:S(2)}, u32[]{:S(2)}) collective-permute-start(bf16[256,1024]{1,0:T(8,128)(2,1)S(1)} %get-tuple-element.287), channel_id=1, source_target_pairs={{16,18},{17,19},{18,16},{19,17},{20,22},{21,23},{22,20},{23,21},{2... | collective-permute-start | bytes 1572872 | tf_op jit(solution)/shard_map/ppermute | solution.py:1104
  541.8 58.0 %collective-permute-start.44 = (bf16[512,2048]{1,0:T(8,128)(2,1)}, bf16[512,2048]{1,0:T(8,128)(2,1)S(1)}, u32[]{:S(2)}, u32[]{:S(2)}) collective-permute-start(bf16[512,2048]{1,0:T(8,128)(2,1)} %shard_map.165), channel_id=1, source_target_pairs={{0,8},{4,12},{8,0},{12,4},{16,20},{20,16},{24,28},{28,24},{1,9},{5... | collective-permute-start | bytes 6291464 | tf_op jit(solution)/shard_map/ppermute | solution.py:929
  547.1 52.7 %collective-permute-start.43 = (bf16[512,2048]{1,0:T(8,128)(2,1)}, bf16[512,2048]{1,0:T(8,128)(2,1)}, u32[]{:S(2)}, u32[]{:S(2)}) collective-permute-start(bf16[512,2048]{1,0:T(8,128)(2,1)} %shard_map.164), channel_id=1, source_target_pairs={{0,4},{4,0},{8,12},{12,8},{16,24},{20,28},{24,16},{28,20},{1,5},{5... | collective-permute-start | bytes 6291464 | tf_op jit(solution)/shard_map/ppermute | solution.py:929
  549.8 48.9 %collective-permute-start.42 = (bf16[768,512]{1,0:T(8,128)(2,1)S(1)}, bf16[768,512]{1,0:T(8,128)(2,1)S(1)}, u32[]{:S(2)}, u32[]{:S(2)}) collective-permute-start(bf16[768,512]{1,0:T(8,128)(2,1)S(1)} %pad_maximum_fusion.3), channel_id=1, source_target_pairs={{0,3},{1,0},{2,1},{3,2},{4,7},{5,4},{6,5},{7,6},{8,11},{9,8},{10,9... | collective-permute-start | bytes 2359304 | tf_op jit(solution)/shard_map/ppermute | solution.py:929
  605.7 30.4 %collective-permute-start.47 = (bf16[128,2048]{1,0:T(8,128)(2,1)}, bf16[128,2048]{1,0:T(8,128)(2,1)S(1)}, u32[]{:S(2)}, u32[]{:S(2)}) collective-permute-start(bf16[128,2048]{1,0:T(8,128)(2,1)} %get-tuple-element.338), channel_id=1, source_target_pairs={{0,4},{4,0},{8,12},{12,8},{16,24},{20,28},{24,16},{28,20},{1,5},{5... | collective-permute-start | bytes 1572872 | tf_op jit(solution)/shard_map/ppermute | solution.py:929
  607.3 28.9 %collective-permute-start.46 = (bf16[128,2048]{1,0:T(8,128)(2,1)}, bf16[128,2048]{1,0:T(8,128)(2,1)}, u32[]{:S(2)}, u32[]{:S(2)}) collective-permute-start(bf16[128,2048]{1,0:T(8,128)(2,1)} %get-tuple-element.336), channel_id=1, source_target_pairs={{0,8},{4,12},{8,0},{12,4},{16,20},{20,16},{24,28},{28,24},{1,9},{5... | collective-permute-start | bytes 1572872 | tf_op jit(solution)/shard_map/ppermute | solution.py:929
  607.7 49.2 %collective-permute-start.50 = (bf16[768,512]{1,0:T(8,128)(2,1)}, bf16[768,512]{1,0:T(8,128)(2,1)S(1)}, u32[]{:S(2)}, u32[]{:S(2)}) collective-permute-start(bf16[768,512]{1,0:T(8,128)(2,1)} %add_convert_fusion.1), channel_id=1, source_target_pairs={{0,3},{1,0},{2,1},{3,2},{4,7},{5,4},{6,5},{7,6},{8,11},{9,8},{10,9... | collective-permute-start | bytes 2359304 | tf_op jit(solution)/shard_map/ppermute | solution.py:929
  692.7 27.8 %collective-permute-start.63 = (bf16[512,512]{1,0:T(8,128)(2,1)}, bf16[512,512]{1,0:T(8,128)(2,1)S(1)}, u32[]{:S(2)}, u32[]{:S(2)}) collective-permute-start(bf16[512,512]{1,0:T(8,128)(2,1)} %get-tuple-element.370), channel_id=1, source_target_pairs={{0,4},{4,0},{8,12},{12,8},{16,24},{20,28},{24,16},{28,20},{1,5},{5... | collective-permute-start | bytes 1572872 | tf_op jit(solution)/shard_map/ppermute | solution.py:929
  699.0 36.9 %collective-permute-start.77 = (f32[8,1024]{1,0:T(8,128)S(1)}, f32[8,1024]{1,0:T(8,128)S(1)}, u32[]{:S(2)}, u32[]{:S(2)}) collective-permute-start(f32[8,1024]{1,0:T(8,128)S(1)} %pad_maximum_fusion.5), channel_id=1, source_target_pairs={{0,4},{4,0},{8,12},{12,8},{1,5},{5,1},{9,13},{13,9},{2,6},{6,2},{1... | collective-permute-start | bytes 98312 | tf_op jit(solution)/shard_map/ppermute | solution.py:1338
  722.7 63.2 %collective-permute-start.76 = (bf16[2048,512]{1,0:T(8,128)(2,1)S(1)}, bf16[2048,512]{1,0:T(8,128)(2,1)}, u32[]{:S(2)}, u32[]{:S(2)}) collective-permute-start(bf16[2048,512]{1,0:T(8,128)(2,1)S(1)} %fusion.refs_5_), channel_id=1, source_target_pairs={{0,16},{1,17},{2,18},{3,19},{4,20},{5,21},{6,22},{7,23},{8,24},{9,... | collective-permute-start | bytes 6291464 | tf_op jit(solution)/shard_map/ppermute | solution.py:1559
  732.4 53.4 %collective-permute-start.74 = (bf16[2048,512]{1,0:T(8,128)(2,1)S(1)}, bf16[2048,512]{1,0:T(8,128)(2,1)}, u32[]{:S(2)}, u32[]{:S(2)}) collective-permute-start(bf16[2048,512]{1,0:T(8,128)(2,1)S(1)} %constant_dynamic-update-slice_fusion.22.refs_1_), channel_id=1, source_target_pairs={{16,0},{17,1},{18,2},{19,3},{20,4},{21,5},{22,6},{23,7},{24,8},{25... | collective-permute-start | bytes 6291464 | tf_op jit(solution)/shard_map/ppermute | solution.py:1559
  751.5 34.3 %collective-permute-start.75 = (bf16[1024,512]{1,0:T(8,128)(2,1)S(1)}, bf16[1024,512]{1,0:T(8,128)(2,1)S(1)}, u32[]{:S(2)}, u32[]{:S(2)}) collective-permute-start(bf16[1024,512]{1,0:T(8,128)(2,1)S(1)} %pad_maximum_fusion.2.refs_4_), channel_id=1, source_target_pairs={{0,16},{1,17},{2,18},{3,19},{4,20},{5,21},{6,22},{7,23},{8,24},{9,... | collective-permute-start | bytes 3145736 | tf_op jit(solution)/shard_map/ppermute | solution.py:1559
  753.4 32.5 %collective-permute-start.73 = (bf16[1024,512]{1,0:T(8,128)(2,1)S(1)}, bf16[1024,512]{1,0:T(8,128)(2,1)}, u32[]{:S(2)}, u32[]{:S(2)}) collective-permute-start(bf16[1024,512]{1,0:T(8,128)(2,1)S(1)} %constant_dynamic-update-slice_fusion.17.refs_0_), channel_id=1, source_target_pairs={{16,0},{17,1},{18,2},{19,3},{20,4},{21,5},{22,6},{23,7},{24,8},{25... | collective-permute-start | bytes 3145736 | tf_op jit(solution)/shard_map/ppermute | solution.py:1559
  (124 other events, 1463.9 us)
Sparse Core Ops, SparseCore 0:
  91.1 67.8 all-gather.3
  160.7 43.9 all-gather.5
  206.6 70.2 all-gather.7
  375.7 84.6 reduce-scatter.2
  463.5 53.5 reduce-scatter.4

commit v3 on v2

--- a/solution.py
+++ b/solution.py
@@ -360,17 +360,18 @@
 BF16 = jnp.bfloat16
 F32 = jnp.float32
 QROWS = 256
+ROW_BLOCK = 256
 COLUMNS = 4
-ROOMY = pltpu.CompilerParams(vmem_limit_bytes=56 * 1024 * 1024)
+ROOMY = pltpu.CompilerParams(vmem_limit_bytes=40 * 1024 * 1024)
 WINDOW = 512
 BYTES_PER_MICRO = 3400000
 COLUMN_DEPTH = 2
-TENSOR_DEPTH = 2
+TENSOR_DEPTH = 3
 
 
 def cost(micros):
     return pl.CostEstimate(
-        flops=int(micros * 3e8), bytes_accessed=int(micros * BYTES_PER_MICRO), transcendentals=0
+        flops=int(micros * 1e9), bytes_accessed=int(micros * BYTES_PER_MICRO), transcendentals=0
     )
 
 
@@ -772,7 +773,7 @@
 
 def row_call(kernel, arrays, tables, outs, gains=0):
     length, width = arrays[0].shape
-    by_row = pl.BlockSpec((QROWS, width), lambda i: (i, 0))
+    by_row = pl.BlockSpec((ROW_BLOCK, width), lambda i: (i, 0))
     out_specs = [by_row] * len(outs)
     out_shape = [jax.ShapeDtypeStruct((length, width), kind) for kind in outs]
     if gains:
@@ -780,7 +781,7 @@
         out_shape.append(jax.ShapeDtypeStruct((gains, 8, width), F32))
     return pl.pallas_call(
         kernel,
-        grid=(length // QROWS,),
+        grid=(length // ROW_BLOCK,),
         in_specs=[by_row] * len(arrays)
         + [pl.BlockSpec(table.shape, lambda i: (0, 0)) for table in tables],
         out_specs=out_specs,
@@ -860,30 +861,28 @@
     )(near, arrived)
 
 
-def total_kernel(count, *refs):
-    sources, slots = refs[:-count], refs[-count:]
-    low = 0
-    for own, from_x, from_y in zip(sources[0::3], sources[1::3], sources[2::3]):
-        high = low + own.shape[0]
-        size = own.shape[1] // count
-        for at, slot in enumerate(slots):
-            part = slice(size * at, size * (at + 1))
-            slot[low:high, :] = (
-                own[:, part].astype(F32) + from_x[:, part].astype(F32) + from_y[:, part].astype(F32)
-            ).astype(BF16)
-        low = high
-
-
-def total_slots(triples, count):
-    sources = [item for triple in triples for item in triple]
-    rows = sum(triple[0].shape[0] for triple in triples)
-    shape = (rows, sources[0].shape[1] // count)
+def total_kernel(own, from_x, from_y, *slots):
+    size = own.shape[1] // len(slots)
+    for at, slot in enumerate(slots):
+        part = slice(size * at, size * (at + 1))
+        slot[...] = (
+            own[:, part].astype(F32) + from_x[:, part].astype(F32) + from_y[:, part].astype(F32)
+        ).astype(BF16)
+
+
+def total_slots(own, from_x, from_y, count):
+    rows, size = own.shape
+    step = rows // 4
+    by_row = lambda size: pl.BlockSpec((step, size), lambda i: (i, 0))
     return pl.pallas_call(
-        partial(total_kernel, count),
-        out_shape=[jax.ShapeDtypeStruct(shape, BF16)] * count,
+        total_kernel,
+        grid=(4,),
+        in_specs=[by_row(size)] * 3,
+        out_specs=[by_row(size // count)] * count,
+        out_shape=[jax.ShapeDtypeStruct((rows, size // count), BF16)] * count,
         compiler_params=ROOMY,
-        cost_estimate=cost(5),
-    )(*sources)
+        cost_estimate=cost(3),
+    )(own, from_x, from_y)
 
 
 def ring(length, by):
@@ -1140,13 +1139,6 @@
         def _():
             put(0, keep.shape[0], (0, lambda low, high: held[:, low:high]))
 
-    if pieces == 1:
-        for at in range(COLUMNS):
-            owner = place[1] ^ block_mask(at, place[0])
-            for slot in range(3):
-                source = spot(3 * owner + slot, rows)
-                put(rows * at, rows, (slot + 1, lambda low, high: blocks[0][source, low:high]))
-        return
     own, from_x, from_y, far_low, far_high = blocks
     half = far_low.shape[0]
     for at, held in enumerate((own, from_x, from_y)):
@@ -1166,16 +1158,49 @@
         )
 
 
+def gathered_kernel(layer, place, keep, theirs, block, *outs):
+    rows = keep.shape[0]
+    start = 0
+    for out in outs:
+        part = out.shape[1] // 4
+        for mine, held in ((True, keep), (False, theirs)):
+
+            @pl.when((place[0] == layer) == mine)
+            def _():
+                out[:, :part] = held[:, start : start + part]
+
+        for slot in range(3):
+            out[:, part * (slot + 1) : part * (slot + 2)] = block[
+                rows * slot : rows * (slot + 1), start : start + part
+            ]
+        start += part
+
+
 def assemble(layer, place, keep, theirs, blocks, parts):
     operands = (keep, theirs, *blocks)
+    width, size = keep.shape
+    shapes = [((width, 4 * part), BF16) for part in parts]
+    if len(blocks) > 1:
+        return placed_call(
+            partial(assemble_kernel, layer, len(blocks)),
+            place,
+            operands,
+            [whole_spec(item.shape) for item in operands],
+            [whole_spec(shape) for shape, _ in shapes],
+            shapes,
+            (1,),
+        )
+    rows = width // COLUMNS
+    by_row = lambda size: pl.BlockSpec((rows, size), lambda r, place: (r, 0))
+    owner = lambda r, place: (place[1] ^ block_mask(r, place[0]), 0)
     return placed_call(
-        partial(assemble_kernel, layer, len(blocks)),
+        partial(gathered_kernel, layer),
         place,
         operands,
-        [whole_spec(item.shape) for item in operands],
-        [whole_spec((keep.shape[0], 4 * part)) for part in parts],
-        [((keep.shape[0], 4 * part), BF16) for part in parts],
-        (1,),
+        [by_row(size), by_row(size), pl.BlockSpec((3 * rows, size), owner)],
+        [by_row(4 * part) for part in parts],
+        shapes,
+        (COLUMNS,),
     )
 
 
@@ -1189,7 +1214,7 @@
 def finish_kernel(place, *refs):
     sources, (g_in, g_out, g_up, g_down, attn, mlp, sems) = refs[:8], refs[8:]
     step = pl.program_id(0)
-    rows = g_in.shape[0]
+    rows = g_in.shape[1]
     lanes = g_out.shape[0] // 2
     hidden = g_down.shape[0] // 2
     core = place[0]
@@ -1218,8 +1243,7 @@
         up_rows = spot(2 * at, rows)
         down_rows = spot(2 * at + 1, rows)
         for part in range(3):
-            start = (2 * part + half) * lanes
-            g_in[:, start : start + lanes] = attn[
+            g_in[part, :, lanes * half : lanes * (half + 1)] = attn[
                 half, attn_rows, lanes * part : lanes * (part + 1)
             ].astype(F32)
         g_out[lanes * half : lanes * (half + 1), :] = (
@@ -1238,13 +1262,13 @@
         sources,
         [pl.BlockSpec(memory_space=pl.ANY)] * 8,
         [
-            pl.BlockSpec((rows, 6 * lanes), lambda b, place: (b, 0)),
+            pl.BlockSpec((3, rows, 2 * lanes), lambda b, place: (0, b, 0)),
             pl.BlockSpec((2 * lanes, rows), lambda b, place: (0, b)),
             pl.BlockSpec((rows, 2 * hidden), lambda b, place: (b, 0)),
             pl.BlockSpec((2 * hidden, rows), lambda b, place: (0, b)),
         ],
         [
-            ((width, 6 * lanes), F32),
+            ((3, width, 2 * lanes), F32),
             ((2 * lanes, width), F32),
             ((width, 2 * hidden), F32),
             ((2 * hidden, width), F32),
@@ -1301,7 +1325,8 @@
             for at in range(count)
         ]
     else:
-        slots = total_slots([(state["own"], *held(state["near"], token)) for state in states], count)
+        (state,) = states
+        slots = total_slots(state["own"], *held(state["near"], token), count)
     total["slots"] = slots
     total["near"] = links.along(slots[2], -1)
     total["last"] = links.along(slots[3], 1)
@@ -1314,7 +1339,7 @@
 
 
 def relay_stage(links, total, token):
-    (near,) = held((total["near"],), token)
+    near, total["last"] = held((total["near"], total["last"]), token)
     relayed = add_low(total["slots"][1], near)
     total["near"] = links.along(relayed, -1)
     return [relayed]
@@ -1332,15 +1357,6 @@
     from_x, from_y = held((from_x, from_y), token)
     total["blocks"] = (own, from_x, from_y, *links.relay(from_x, from_y))
     return []
-
-
-def sum_everywhere(values):
-    swap = lambda axis, by: lax.ppermute(
-        values, axis, [(i, i ^ by) for i in range(lax.axis_size(axis))]
-    )
-    for axis, by in (("dp", 1), ("dp", 2), ("tensor", 1), ("tensor", 2)):
-        values = values + swap(axis, by)
-    return values
 
 
 def per_chip(
@@ -1474,6 +1490,24 @@
         left.append([blocks[0]] + [links.along(blocks[by], by) for by in range(1, count)])
         return []
 
+    running = {"hops": [("tensor", 1), ("tensor", 2), ("dp", 1), ("dp", 2)]}
+
+    def gain_start(token):
+        running["sum"] = unturn(jnp.concatenate(gain_sums), section, column)
+        running["sent"] = swap_gains()
+        return []
+
+    def swap_gains():
+        axis, by = running["hops"].pop(0)
+        pairs = [(i, i ^ by) for i in range(lax.axis_size(axis))]
+        return lax.ppermute(running["sum"], axis, pairs)
+
+    def gain_hop(token):
+        running["sum"] = running["sum"] + running["sent"]
+        if running["hops"]:
+            running["sent"] = swap_gains()
+        return []
+
     def reduction(parts):
         if len(parts) == 1:
             return {"sum": lax.psum_scatter(parts[0], "dp", scatter_dimension=0, tiled=True)}
@@ -1521,17 +1555,23 @@
         attn = reduction(parts)
         if layer:
             flow.plan(6, partial(arrive, mlp))
-            plan_totals(1, [mlp, attn], (7, 8, 10, 13))
+            plan_totals(1, [mlp, attn], (7, 8, 12, 15))
         else:
             flow.plan(9, partial(column_stage, links, attn))
-            plan_totals(0, [mlp], (8, 11, 14, 16))
-            plan_totals(0, [attn], (12, 15, 17, 18))
-            flow.plan(13, send_grads)
+            plan_totals(0, [mlp], (10, 13, 18, 22))
+            plan_totals(0, [attn], (15, 17, 21, 24))
+            flow.plan(11, gain_start)
+            for at in (14, 16, 19, 23):
+                flow.plan(at, gain_hop)
+            flow.plan(20, send_grads)
         (normed_low,) = flow.point(normed_low, normed_low)
         normed_other = other_core(normed_low)
         grad, part_zero = row_call(
             input_back_kernel, [layer_in, middle_grad, normed_low, normed_other], [gain], [BF16], 1
         )
+        if layer == 0:
+            layer_store = leave_rows(place, left[0], left[1])
+            grad = hold([grad], layer_store)[0]
         (grad,) = flow.point(grad, grad)
         gain_sums[layer] = jnp.sum(
             jnp.concatenate([part_zero, part_two, part_three]), axis=1
@@ -1539,9 +1579,8 @@
         input_grads[layer] = grad
         upstream = grad
     flow.drain()
-    layer_store = leave_rows(place, left[0], left[1])
     grad_store = leave_rows(place, left[2])
-    gain_total = sum_everywhere(unturn(jnp.concatenate(gain_sums), section, column))
+    gain_total = running["sum"]
     gain_total = jnp.where(section == 0, gain_total[:4], gain_total[4:])
     (both_parts,) = totals[1]
     own, from_x, from_y, far_low, far_high = both_parts["blocks"]
@@ -1562,7 +1601,7 @@
     return (
         layer_store[None, None],
         grad_store[None, None],
-        in_grad.reshape(1, width, 3, 2 * lanes),
+        in_grad.transpose(1, 0, 2)[None],
         out_grad[None],
         up_grad[None],
         down_grad[None],

time: 816 us -> 763 us (0.935)
  Pallas kernels: 408 us -> 299 us
  local copies, waits for them, and re-layouts: 48.9 us -> 144 us
  waiting for transfers between devices: 213 us -> 164 us
    unnamed x136 -> x317, local copies, waits for them, and re-layouts: 28.3 us -> 121 us
    pallas_call x15, Pallas kernels: 213 us -> 170 us  [placed_call(): pl.pallas_call(kernel, grid_spec=pltpu.PrefetchScalarGridSpec(num_scalar_...]
    pallas_call x13, Pallas kernels: 85.3 us -> 44.4 us  [the longest x11 42.3 us: row_call(): pl.pallas_call(kernel, grid=(length // ROW_BLOCK,), in_specs=[by_row] * l...]
    ppermute x54, waiting for transfers between devices: 181 us -> 141 us  [send(): got = lax.ppermute(values, axes, pairs)]
  transfers between devices with their start and end apart: 86 -> 86, of which waited for: 37 -> 31; matrix products, arithmetic and copies ran while one was open for 5% -> 6% of each run, Pallas kernels for 40% -> 32%
where the time goes in v3:
time: 763 us; the launch traced here: 750 us
  Pallas kernels  299 us (39%)
  waiting for transfers between devices  164 us (21%)
  local copies, waits for them, and re-layouts  144 us (19%)
  starting transfers between devices  110 us (14%)
  other arithmetic  17.8 us (2%)
  between operations  15.8 us (2%)
    pallas_call x15, Pallas kernels, placed_call(): pl.pallas_call(kernel, grid_spec=pltpu.PrefetchScalarGridSpec(num_scalar_...  170 us
    ppermute x54, waiting for transfers between devices, send(): got = lax.ppermute(values, axes, pairs)  141 us
    unnamed x317, local copies, waits for them, and re-layouts  121 us
    ppermute x54, starting transfers between devices, send(): got = lax.ppermute(values, axes, pairs)  76.3 us
    pallas_call x11, Pallas kernels, row_call(): pl.pallas_call(kernel, grid=(length // ROW_BLOCK,), in_specs=[by_row] * l...  42.3 us
    pallas_call x3, Pallas kernels, attend_forward(): pl.pallas_call(kernel, grid=(count,), in_specs=[whole((length, width)), p...  40.5 us
    pallas_call x2, Pallas kernels, hidden_forward(): pl.pallas_call(hidden_kernel, grid=(size // block,), in_specs=[whole] + [...  32.5 us
    ppermute x13, waiting for transfers between devices, other_core(): return lax.ppermute(values, 'section', [(0, 1), (1, 0)])  19.3 us
  transfers between devices with their start and end apart: 86, of which 31 were waited for; matrix products, arithmetic and copies ran while one was open for 6% of the time, Pallas kernels for 32%

profile of v3, /device:TPU:0, one launch (start us, length us, event | category | flops | bytes accessed | tf_op | source)
XLA Modules:
  0.0 750.3 jit_solution(7965373572413435809)
XLA Ops:
  30.4 8.6 %collective-permute-done.2 = bf16[256,512]{1,0:T(8,128)(2,1)S(1)} collective-permute-done((bf16[256,512]{1,0:T(8,128)(2,1)S(1)}, bf16[256,512]{1,0:T(8,128)(2,1)S(1)}, u32[]{:S(2)}, u32[]{:S(2)}) %collective-permute-start.2) | collective-permute-done | bytes 262176 | tf_op jit(solution)/shard_map/ppermute | solution.py:928
  42.9 7.1 collective-permute-done.9
  60.1 9.9 %collective-permute-done.5 = bf16[256,1024]{1,0:T(8,128)(2,1)S(1)} collective-permute-done((bf16[256,1024]{1,0:T(8,128)(2,1)S(1)}, bf16[256,1024]{1,0:T(8,128)(2,1)S(1)}, u32[]{:S(2)}, u32[]{:S(2)}) %collective-permute-start.5) | collective-permute-done | bytes 524320 | tf_op jit(solution)/shard_map/ppermute | solution.py:928
  70.1 7.5 collective-permute-start.10
  81.3 8.9 %collective-permute-done.10 = bf16[256,1024]{1,0:T(8,128)(2,1)S(1)} collective-permute-done((bf16[256,1024]{1,0:T(8,128)(2,1)S(1)}, bf16[256,1024]{1,0:T(8,128)(2,1)S(1)}, u32[]{:S(2)}, u32[]{:S(2)}) %collective-permute-start.10) | collective-permute-done | bytes 524320 | tf_op jit(solution)/shard_map/ppermute | solution.py:928
  101.5 8.1 %collective-permute-done.8 = bf16[128,1024]{1,0:T(8,128)(2,1)S(1)} collective-permute-done((bf16[128,1024]{1,0:T(8,128)(2,1)S(1)}, bf16[128,1024]{1,0:T(8,128)(2,1)S(1)}, u32[]{:S(2)}, u32[]{:S(2)}) %collective-permute-start.8) | collective-permute-done | bytes 262176 | tf_op jit(solution)/shard_map/ppermute | solution.py:928
  130.2 10.1 %shard_map.139 = (bf16[1024,1536]{1,0:T(8,128)(2,1)S(1)}, bf16[1024,512]{1,0:T(8,128)(2,1)S(1)}) custom-call(bf16[1024,1024]{1,0:T(8,128)(2,1)S(1)} %shard_map.138.refs_0_.normed, bf16[1024,1536]{1,0:T(8,128)(2,1)S(1)} %copy-done.110, f32[1024,128]{1,0:T(8,128)S(1)} %copy.28.refs_2_.cosine, f32[1024,128]{1,0:T(8,128)S(1)} %negate_select_fusion.refs_3_.sine, ...), custom_call_target="tpu_custom_call" | custom-call | flops 12999999488 | bytes 44200000 | tf_op jit(solution)/shard_map/pallas_call | solution.py:464
  153.0 10.1 %shard_map.140 = (bf16[1024,1536]{1,0:T(8,128)(2,1)S(1)}, bf16[1024,512]{1,0:T(8,128)(2,1)S(1)}) custom-call(bf16[1024,1024]{1,0:T(8,128)(2,1)S(1)} %copy-done.118, bf16[1024,1536]{1,0:T(8,128)(2,1)S(1)} %copy-done.111, f32[1024,128]{1,0:T(8,128)S(1)} %copy.28.refs_2_.cosine, ...), custom_call_target="tpu_custom_call", output_to_operand_aliasing={{0}: (6, {}), {1}: (7, {})} | custom-call | flops 12999999488 | bytes 44200000 | tf_op jit(solution)/shard_map/pallas_call | solution.py:464
  179.7 9.7 %collective-permute-done.23 = bf16[256,1024]{1,0:T(8,128)(2,1)S(1)} collective-permute-done((bf16[256,1024]{1,0:T(8,128)(2,1)S(1)}, bf16[256,1024]{1,0:T(8,128)(2,1)S(1)}, u32[]{:S(2)}, u32[]{:S(2)}) %collective-permute-start.23) | collective-permute-done | bytes 524320 | tf_op jit(solution)/shard_map/ppermute | solution.py:928
  203.4 16.2 %shard_map.144 = (bf16[1024,2048]{1,0:T(8,128)(2,1)S(1)}, bf16[1024,2048]{1,0:T(8,128)(2,1)S(1)}, bf16[1024,1024]{1,0:T(8,128)(2,1)S(1)}) custom-call(bf16[1024,1024]{1,0:T(8,128)(2,1)S(1)} %copy-done.104, bf16[1024,2048]{1,0:T(8,128)(2,1)} %copy-done.94, bf16[1024,2048]{1,0:T(8,128)(2,1)} %copy-done.95), custom_call_target="tpu_custom_call" | custom-call | flops 19000000512 | bytes 64600000 | tf_op jit(solution)/shard_map/pallas_call | solution.py:676
  258.9 20.2 %shard_map.148 = (bf16[1024,1536]{1,0:T(8,128)(2,1)S(1)}, bf16[1024,512]{1,0:T(8,128)(2,1)S(1)}) custom-call(bf16[1024,1024]{1,0:T(8,128)(2,1)S(1)} %copy-done.22, bf16[1024,1536]{1,0:T(8,128)(2,1)S(1)} %get-tuple-element.257.refs_1_.w_in, f32[1024,128]{1,0:T(8,128)S(1)} %copy-done.6, f32[1024,128]{1,0:T(8,128)S(1)} %copy-done.14, s32[1024,1]{1,0:T(8,128)S(1)} %copy-done.10, ...), custom_call_target="tpu_custom_call" | custom-call | flops 12999999488 | bytes 44200000 | tf_op jit(solution)/shard_map/pallas_call | solution.py:464
  306.2 16.3 %shard_map.152 = (bf16[1024,2048]{1,0:T(8,128)(2,1)S(1)}, bf16[1024,2048]{1,0:T(8,128)(2,1)S(1)}, bf16[1024,1024]{1,0:T(8,128)(2,1)S(1)}) custom-call(bf16[1024,1024]{1,0:T(8,128)(2,1)S(1)} %copy-done.108, bf16[1024,2048]{1,0:T(8,128)(2,1)} %copy-done.98, bf16[1024,2048]{1,0:T(8,128)(2,1)} %copy-done.100), custom_call_target="tpu_custom_call" | custom-call | flops 19000000512 | bytes 64600000 | tf_op jit(solution)/shard_map/pallas_call | solution.py:676
  333.0 24.3 %shard_map.154 = (bf16[2048,2048]{1,0:T(8,128)(2,1)}, bf16[1024,1024]{1,0:T(8,128)(2,1)S(1)}) custom-call(s32[3]{0:T(128)S(1)} %pad_add_fusion.place, bf16[1024,1024]{1,0:T(8,128)(2,1)S(1)} %get-tuple-element.275.mixed_grad, bf16[1024,1024]{1,0:T(8,128)(2,1)S(1)} %copy-done.108, bf16[1024,2048]{1,0:T(8,128)(2,1)S(1)} %copy-done.99, ...), custom_call_target="tpu_custom_call" | custom-call | flops 6000000000 | bytes 20400000 | tf_op jit(solution)/shard_map/pallas_call | solution.py:968
  374.2 8.4 %shard_map.155 = (bf16[1024,1024]{1,0:T(8,128)(2,1)S(1)}, f32[1024,1024]{1,0:T(8,128)}, f32[2,8,1024]{2,1,0:T(8,128)S(1)}) custom-call(bf16[1024,1024]{1,0:T(8,128)(2,1)S(1)} %copy-done.19, bf16[1024,1024]{1,0:T(8,128)(2,1)S(1)} %copy-done.56, bf16[1024,1024]{1,0:T(8,128)(2,1)S(1)} %copy-done.61, bf16[1024,1024]{1,0:T(8,128)(2,1)S(1)} %copy-done.129, ...), custom_call_target="tpu_custom_call" | custom-call | flops 6000000000 | bytes 20400000 | tf_op jit(solution)/shard_map/pallas_call | solution.py:782
  390.5 23.0 %shard_map.157 = (bf16[1024,2048]{1,0:T(8,128)(2,1)}, f32[1024,1024]{1,0:T(8,128)}) custom-call(s32[3]{0:T(128)S(1)} %pad_add_fusion.place, bf16[1024,1024]{1,0:T(8,128)(2,1)S(1)} %copy-done.25, bf16[1024,1024]{1,0:T(8,128)(2,1)S(1)} %copy-done.23, bf16[1024,1536]{1,0:T(8,128)(2,1)S(1)} %copy-done.2, bf16[1024,512]{1,0:T(8,128)(2,1)S(1)} %copy-done.30, ...), custom_call_target="tpu_custom_call" | custom-call | flops 6000000000 | bytes 20400000 | tf_op jit(solution)/shard_map/pallas_call | solution.py:968
  413.5 23.7 %shard_map.159 = (bf16[1024,2048]{1,0:T(8,128)(2,1)}, bf16[1024,1024]{1,0:T(8,128)(2,1)S(1)}) custom-call(s32[3]{0:T(128)S(1)} %pad_add_fusion.place, bf16[1024,1024]{1,0:T(8,128)(2,1)S(1)} %copy-done.26, bf16[1024,1024]{1,0:T(8,128)(2,1)S(1)} %copy-done.23, bf16[1024,1536]{1,0:T(8,128)(2,1)S(1)} %copy-done.2, ...), custom_call_target="tpu_custom_call", output_to_operand_aliasing={{0}: (11, {})} | custom-call | flops 6000000000 | bytes 20400000 | tf_op jit(solution)/shard_map/pallas_call | solution.py:968
  438.6 6.9 collective-permute-start.38
  461.5 25.7 %shard_map.162 = (bf16[512,2048]{1,0:T(8,128)(2,1)S(1)}, bf16[512,2048]{1,0:T(8,128)(2,1)S(1)}, bf16[512,2048]{1,0:T(8,128)(2,1)}, bf16[256,2048]{1,0:T(8,128)(2...) custom-call(s32[3]{0:T(128)S(1)} %pad_add_fusion.place, ...), custom_call_target="tpu_custom_call" | custom-call | flops 6000000000 | bytes 20400000 | tf_op jit(solution)/shard_map/pallas_call | solution.py:968
  505.3 7.4 shard_map.163
  533.8 40.8 %shard_map.166 = (bf16[256,2048]{1,0:T(8,128)(2,1)S(1)}, bf16[256,2048]{1,0:T(8,128)(2,1)S(1)}, bf16[256,2048]{1,0:T(8,128)(2,1)S(1)}, bf16[128,2048]{1,0:T(8,12...) custom-call(s32[3]{0:T(128)S(1)} %pad_add_fusion.place, bf16[1024,1024]{1,0:T(8,128)(2,1)S(1)} %copy-done.121, ...), custom_call_target="tpu_custom_call" | custom-call | flops 6000000000 | bytes 20400000 | tf_op jit(solution)/shard_map/pallas_call | solution.py:968
  603.4 17.2 %collective-permute-done.49.from_x = bf16[256,2048]{1,0:T(8,128)(2,1)S(1)} collective-permute-done((bf16[256,2048]{1,0:T(8,128)(2,1)S(1)}, bf16[256,2048]{1,0:T(8,128)(2,1)S(1)}, u32[]{:S(2)}, u32[]{:S(2)}) %collective-permute-start.49) | collective-permute-done | bytes 1048608 | tf_op jit(solution)/shard_map/ppermute | solution.py:928
  631.3 9.9 %collective-permute-done.61 = bf16[768,512]{1,0:T(8,128)(2,1)} collective-permute-done((bf16[768,512]{1,0:T(8,128)(2,1)}, bf16[768,512]{1,0:T(8,128)(2,1)}, u32[]{:S(2)}, u32[]{:S(2)}) %collective-permute-start.61) | collective-permute-done | bytes 786464 | tf_op jit(solution)/shard_map/ppermute | solution.py:928
  659.1 7.9 %collective-permute-done.63 = bf16[512,512]{1,0:T(8,128)(2,1)S(1)} collective-permute-done((bf16[512,512]{1,0:T(8,128)(2,1)S(1)}, bf16[512,512]{1,0:T(8,128)(2,1)S(1)}, u32[]{:S(2)}, u32[]{:S(2)}) %collective-permute-start.63) | collective-permute-done | bytes 524320 | tf_op jit(solution)/shard_map/ppermute | solution.py:928
  707.0 17.1 %collective-permute-done.56.refs_2_ = bf16[256,1024]{1,0:T(8,128)(2,1)S(1)} collective-permute-done((bf16[256,1024]{1,0:T(8,128)(2,1)S(1)}, bf16[256,1024]{1,0:T(8,128)(2,1)S(1)}, u32[]{:S(2)}, u32[]{:S(2)}) %collective-permute-start.56) | collective-permute-done | bytes 524320 | tf_op jit(solution)/shard_map/ppermute | solution.py:928
  (577 shorter events, 389.5 us)
Async XLA Ops:
  7.2 182.2 %all-gather.4.cloned.1.call-start = ((), (), s32[]{:S(2)}) async-start(), calls=%async_computation.2 | async-start | bytes 7864320 | tf_op jit(solution)/shard_map/all_gather | solution.py:1395
  21.5 28.5 %collective-permute-start = (bf16[1024,1024]{1,0:T(8,128)(2,1)}, bf16[1024,1024]{1,0:T(8,128)(2,1)S(1)}, u32[]{:S(2)}, u32[]{:S(2)}) collective-permute-start(bf16[1024,1024]{1,0:T(8,128)(2,1)} %get-tuple-element.195), channel_id=1, source_target_pairs={{0,16},{16,0},{1,17},{17,1},{2,18},{18,2},{3,19},{19,3},{4,20},{20... | collective-permute-start | bytes 6291464 | tf_op jit(solution)/shard_map/ppermute | solution.py:893
  91.5 149.0 %all-gather.6.cloned.1.call-start = ((), (), s32[]{:S(2)}) async-start(), calls=%async_computation.3 | async-start | bytes 3932160 | tf_op jit(solution)/shard_map/all_gather | solution.py:1395
  143.5 151.1 %all-gather.8.cloned.1.call-start = ((), (), s32[]{:S(2)}) async-start(), calls=%async_computation.4 | async-start | bytes 7864320 | tf_op jit(solution)/shard_map/all_gather | solution.py:1395
  191.0 32.4 %collective-permute-start.26 = (bf16[128,1024]{1,0:T(8,128)(2,1)}, bf16[128,1024]{1,0:T(8,128)(2,1)}, u32[]{:S(2)}, u32[]{:S(2)}) collective-permute-start(bf16[128,1024]{1,0:T(8,128)(2,1)} %get-tuple-element.248), channel_id=1, source_target_pairs={{0,3},{1,0},{2,1},{3,2},{4,7},{5,4},{6,5},{7,6},{8,11},{9,8},{10,9... | collective-permute-start | bytes 786440 | tf_op jit(solution)/shard_map/ppermute | solution.py:928
  191.1 32.4 %collective-permute-start.25 = (bf16[128,1024]{1,0:T(8,128)(2,1)}, bf16[128,1024]{1,0:T(8,128)(2,1)}, u32[]{:S(2)}, u32[]{:S(2)}) collective-permute-start(bf16[128,1024]{1,0:T(8,128)(2,1)} %get-tuple-element.246), channel_id=1, source_target_pairs={{0,2},{1,3},{2,0},{3,1},{4,6},{5,7},{6,4},{7,5},{8,10},{9,11},{10,... | collective-permute-start | bytes 786440 | tf_op jit(solution)/shard_map/ppermute | solution.py:928
  192.1 31.4 %collective-permute-start.24 = (bf16[128,1024]{1,0:T(8,128)(2,1)}, bf16[128,1024]{1,0:T(8,128)(2,1)}, u32[]{:S(2)}, u32[]{:S(2)}) collective-permute-start(bf16[128,1024]{1,0:T(8,128)(2,1)} %get-tuple-element.244), channel_id=1, source_target_pairs={{0,1},{1,2},{2,3},{3,0},{4,5},{5,6},{6,7},{7,4},{8,9},{9,10},{10,1... | collective-permute-start | bytes 786440 | tf_op jit(solution)/shard_map/ppermute | solution.py:928
  193.3 299.9 %reduce-scatter.3.cloned.1.call-start = ((), (), s32[]{:S(2)}) async-start(), calls=%async_computation.5 | async-start | bytes 10485760 | tf_op jit(solution)/shard_map/reduce_scatter | solution.py:1513
  247.3 33.5 %collective-permute-start.29 = (bf16[256,1024]{1,0:T(8,128)(2,1)S(1)}, bf16[256,1024]{1,0:T(8,128)(2,1)S(1)}, u32[]{:S(2)}, u32[]{:S(2)}) collective-permute-start(bf16[256,1024]{1,0:T(8,128)(2,1)S(1)} %get-tuple-element.261), channel_id=1, source_target_pairs={{0,1},{1,2},{2,3},{3,0},{4,5},{5,6},{6,7},{7,4},{8,9},{9,10},{10,1... | collective-permute-start | bytes 1572872 | tf_op jit(solution)/shard_map/ppermute | solution.py:1103
  250.7 30.2 %collective-permute-start.30 = (bf16[256,1024]{1,0:T(8,128)(2,1)S(1)}, bf16[256,1024]{1,0:T(8,128)(2,1)S(1)}, u32[]{:S(2)}, u32[]{:S(2)}) collective-permute-start(bf16[256,1024]{1,0:T(8,128)(2,1)S(1)} %get-tuple-element.262), channel_id=1, source_target_pairs={{0,2},{1,3},{2,0},{3,1},{4,6},{5,7},{6,4},{7,5},{8,10},{9,11},{10,... | collective-permute-start | bytes 1572872 | tf_op jit(solution)/shard_map/ppermute | solution.py:1103
  358.7 155.4 %reduce-scatter.5.cloned.1.call-start = ((), (), s32[]{:S(2)}) async-start(), calls=%async_computation.6 | async-start | bytes 5242880 | tf_op jit(solution)/shard_map/reduce_scatter | solution.py:1513
  383.9 29.6 %collective-permute-start.35 = (bf16[256,1024]{1,0:T(8,128)(2,1)S(1)}, bf16[256,1024]{1,0:T(8,128)(2,1)S(1)}, u32[]{:S(2)}, u32[]{:S(2)}) collective-permute-start(bf16[256,1024]{1,0:T(8,128)(2,1)S(1)} %get-tuple-element.283), channel_id=1, source_target_pairs={{16,17},{17,18},{18,19},{19,16},{20,21},{21,22},{22,23},{23,20},{2... | collective-permute-start | bytes 1572872 | tf_op jit(solution)/shard_map/ppermute | solution.py:1103
  384.6 28.9 %collective-permute-start.36 = (bf16[256,1024]{1,0:T(8,128)(2,1)S(1)}, bf16[256,1024]{1,0:T(8,128)(2,1)S(1)}, u32[]{:S(2)}, u32[]{:S(2)}) collective-permute-start(bf16[256,1024]{1,0:T(8,128)(2,1)S(1)} %get-tuple-element.284), channel_id=1, source_target_pairs={{16,18},{17,19},{18,16},{19,17},{20,22},{21,23},{22,20},{23,21},{2... | collective-permute-start | bytes 1572872 | tf_op jit(solution)/shard_map/ppermute | solution.py:1103
  493.6 28.5 %collective-permute-start.41 = (bf16[256,2048]{1,0:T(8,128)(2,1)}, bf16[256,2048]{1,0:T(8,128)(2,1)}, u32[]{:S(2)}, u32[]{:S(2)}) collective-permute-start(bf16[256,2048]{1,0:T(8,128)(2,1)} %copy-done.80), channel_id=1, source_target_pairs={{0,4},{4,0},{8,12},{12,8},{16,24},{20,28},{24,16},{28,20},{1,5},{5... | collective-permute-start | bytes 3145736 | tf_op jit(solution)/shard_map/ppermute | solution.py:928
  517.3 58.2 %collective-permute-start.43 = (bf16[768,512]{1,0:T(8,128)(2,1)}, bf16[768,512]{1,0:T(8,128)(2,1)}, u32[]{:S(2)}, u32[]{:S(2)}) collective-permute-start(bf16[768,512]{1,0:T(8,128)(2,1)} %pad_maximum_fusion.4), channel_id=1, source_target_pairs={{0,1},{1,2},{2,3},{3,0},{4,5},{5,6},{6,7},{7,4},{8,9},{9,10},{10,1... | collective-permute-start | bytes 2359304 | tf_op jit(solution)/shard_map/ppermute | solution.py:928
  519.0 56.5 %collective-permute-start.42 = (bf16[768,512]{1,0:T(8,128)(2,1)}, bf16[768,512]{1,0:T(8,128)(2,1)}, u32[]{:S(2)}, u32[]{:S(2)}) collective-permute-start(bf16[768,512]{1,0:T(8,128)(2,1)} %pad_maximum_fusion.3), channel_id=1, source_target_pairs={{0,3},{1,0},{2,1},{3,2},{4,7},{5,4},{6,5},{7,6},{8,11},{9,8},{10,9... | collective-permute-start | bytes 2359304 | tf_op jit(solution)/shard_map/ppermute | solution.py:928
  529.1 49.8 %collective-permute-start.47 = (bf16[512,2048]{1,0:T(8,128)(2,1)}, bf16[512,2048]{1,0:T(8,128)(2,1)S(1)}, u32[]{:S(2)}, u32[]{:S(2)}) collective-permute-start(bf16[512,2048]{1,0:T(8,128)(2,1)} %shard_map.165), channel_id=1, source_target_pairs={{0,8},{4,12},{8,0},{12,4},{16,20},{20,16},{24,28},{28,24},{1,9},{5... | collective-permute-start | bytes 6291464 | tf_op jit(solution)/shard_map/ppermute | solution.py:928
  530.7 49.7 %collective-permute-start.45 = (bf16[512,2048]{1,0:T(8,128)(2,1)S(1)}, bf16[512,2048]{1,0:T(8,128)(2,1)S(1)}, u32[]{:S(2)}, u32[]{:S(2)}) collective-permute-start(bf16[512,2048]{1,0:T(8,128)(2,1)S(1)} %shard_map.164), channel_id=1, source_target_pairs={{0,4},{4,0},{8,12},{12,8},{16,24},{20,28},{24,16},{28,20},{1,5},{5... | collective-permute-start | bytes 6291464 | tf_op jit(solution)/shard_map/ppermute | solution.py:928
  602.8 39.6 %collective-permute-start.54 = (bf16[512,512]{1,0:T(8,128)(2,1)}, bf16[512,512]{1,0:T(8,128)(2,1)}, u32[]{:S(2)}, u32[]{:S(2)}) collective-permute-start(bf16[512,512]{1,0:T(8,128)(2,1)} %get-tuple-element.347), channel_id=1, source_target_pairs={{0,1},{1,2},{2,3},{3,0},{4,5},{5,6},{6,7},{7,4},{8,9},{9,10},{10,1... | collective-permute-start | bytes 1572872 | tf_op jit(solution)/shard_map/ppermute | solution.py:928
  676.6 61.0 %collective-permute-start.76 = (bf16[2048,512]{1,0:T(8,128)(2,1)S(1)}, bf16[2048,512]{1,0:T(8,128)(2,1)S(1)}, u32[]{:S(2)}, u32[]{:S(2)}) collective-permute-start(bf16[2048,512]{1,0:T(8,128)(2,1)S(1)} %fusion.refs_5_), channel_id=1, source_target_pairs={{0,16},{1,17},{2,18},{3,19},{4,20},{5,21},{6,22},{7,23},{8,24},{9,... | collective-permute-start | bytes 6291464 | tf_op jit(solution)/shard_map/ppermute | solution.py:1598
  684.5 53.1 %collective-permute-start.74 = (bf16[2048,512]{1,0:T(8,128)(2,1)S(1)}, bf16[2048,512]{1,0:T(8,128)(2,1)S(1)}, u32[]{:S(2)}, u32[]{:S(2)}) collective-permute-start(bf16[2048,512]{1,0:T(8,128)(2,1)S(1)} %constant_dynamic-update-slice_fusion.22.refs_1_), channel_id=1, source_target_pairs={{16,0},{17,1},{18,2},{19,3},{20,4},{21,5},{22,6},{23,7},{24,8},{25... | collective-permute-start | bytes 6291464 | tf_op jit(solution)/shard_map/ppermute | solution.py:1598
  686.1 38.0 %collective-permute-start.56 = (bf16[256,1024]{1,0:T(8,128)(2,1)S(1)}, bf16[256,1024]{1,0:T(8,128)(2,1)S(1)}, u32[]{:S(2)}, u32[]{:S(2)}) collective-permute-start(bf16[256,1024]{1,0:T(8,128)(2,1)S(1)} %get-tuple-element.349), channel_id=1, source_target_pairs={{0,2},{1,3},{2,0},{3,1},{4,6},{5,7},{6,4},{7,5},{8,10},{9,11},{10,... | collective-permute-start | bytes 1572872 | tf_op jit(solution)/shard_map/ppermute | solution.py:928
  687.2 39.2 %collective-permute-start.53 = (bf16[256,1024]{1,0:T(8,128)(2,1)S(1)}, bf16[256,1024]{1,0:T(8,128)(2,1)S(1)}, u32[]{:S(2)}, u32[]{:S(2)}) collective-permute-start(bf16[256,1024]{1,0:T(8,128)(2,1)S(1)} %get-tuple-element.344), channel_id=1, source_target_pairs={{0,1},{1,2},{2,3},{3,0},{4,5},{5,6},{6,7},{7,4},{8,9},{9,10},{10,1... | collective-permute-start | bytes 1572872 | tf_op jit(solution)/shard_map/ppermute | solution.py:928
  706.2 29.3 %collective-permute-start.60 = (bf16[256,1024]{1,0:T(8,128)(2,1)S(1)}, bf16[256,1024]{1,0:T(8,128)(2,1)S(1)}, u32[]{:S(2)}, u32[]{:S(2)}) collective-permute-start(bf16[256,1024]{1,0:T(8,128)(2,1)S(1)} %get-tuple-element.355), channel_id=1, source_target_pairs={{0,3},{1,0},{2,1},{3,2},{4,7},{5,4},{6,5},{7,6},{8,11},{9,8},{10,9... | collective-permute-start | bytes 1572872 | tf_op jit(solution)/shard_map/ppermute | solution.py:928
  (211 other events, 2256.7 us)
Sparse Core Ops, SparseCore 0:
  91.7 67.8 all-gather.3
  161.4 43.9 all-gather.5
  207.2 70.1 all-gather.7
  358.8 84.4 reduce-scatter.2
  446.4 53.2 reduce-scatter.4

commit v4 on v3

--- a/solution.py
+++ b/solution.py
@@ -365,7 +365,7 @@
 ROOMY = pltpu.CompilerParams(vmem_limit_bytes=40 * 1024 * 1024)
 WINDOW = 512
 BYTES_PER_MICRO = 3400000
-COLUMN_DEPTH = 2
+COLUMN_DEPTH = 3
 TENSOR_DEPTH = 3
 
 

time: 763 us -> 757 us (level)
  local copies, waits for them, and re-layouts: 144 us -> 133 us
  Pallas kernels: 299 us -> 307 us
    unnamed x317 -> x311, local copies, waits for them, and re-layouts: 121 us -> 112 us
  transfers between devices with their start and end apart: 86 -> 86, of which waited for: 31 -> 31; matrix products, arithmetic and copies ran while one was open for 6% -> 5% of each run, Pallas kernels for 32% -> 34%
where the time goes in v4:
time: 757 us; the launch traced here: 744 us
  Pallas kernels  307 us (41%)
  waiting for transfers between devices  157 us (21%)
  local copies, waits for them, and re-layouts  133 us (18%)
  starting transfers between devices  114 us (15%)
  other arithmetic  16.4 us (2%)
  between operations  15.8 us (2%)
    pallas_call x15, Pallas kernels, placed_call(): pl.pallas_call(kernel, grid_spec=pltpu.PrefetchScalarGridSpec(num_scalar_...  170 us
    ppermute x54, waiting for transfers between devices, send(): got = lax.ppermute(values, axes, pairs)  134 us
    unnamed x311, local copies, waits for them, and re-layouts  112 us
    ppermute x54, starting transfers between devices, send(): got = lax.ppermute(values, axes, pairs)  81.3 us
    pallas_call x11, Pallas kernels, row_call(): pl.pallas_call(kernel, grid=(length // ROW_BLOCK,), in_specs=[by_row] * l...  42.5 us
    pallas_call x3, Pallas kernels, attend_forward(): pl.pallas_call(kernel, grid=(count,), in_specs=[whole((length, width)), p...  40.5 us
    pallas_call x2, Pallas kernels, hidden_forward(): pl.pallas_call(hidden_kernel, grid=(size // block,), in_specs=[whole] + [...  32.5 us
    ppermute x13, waiting for transfers between devices, other_core(): return lax.ppermute(values, 'section', [(0, 1), (1, 0)])  17.8 us
  transfers between devices with their start and end apart: 86, of which 31 were waited for; matrix products, arithmetic and copies ran while one was open for 5% of the time, Pallas kernels for 34%

profile of v4, /device:TPU:0, one launch (start us, length us, event | category | flops | bytes accessed | tf_op | source)
XLA Modules:
  0.0 743.8 jit_solution(14474780807865982647)
XLA Ops:
  30.4 8.6 %collective-permute-done.2 = bf16[256,512]{1,0:T(8,128)(2,1)S(1)} collective-permute-done((bf16[256,512]{1,0:T(8,128)(2,1)S(1)}, bf16[256,512]{1,0:T(8,128)(2,1)S(1)}, u32[]{:S(2)}, u32[]{:S(2)}) %collective-permute-start.2) | collective-permute-done | bytes 262176 | tf_op jit(solution)/shard_map/ppermute | solution.py:928
  42.9 7.1 collective-permute-done.9
  60.1 9.9 %collective-permute-done.5 = bf16[256,1024]{1,0:T(8,128)(2,1)S(1)} collective-permute-done((bf16[256,1024]{1,0:T(8,128)(2,1)S(1)}, bf16[256,1024]{1,0:T(8,128)(2,1)S(1)}, u32[]{:S(2)}, u32[]{:S(2)}) %collective-permute-start.5) | collective-permute-done | bytes 524320 | tf_op jit(solution)/shard_map/ppermute | solution.py:928
  70.1 7.5 %collective-permute-start.10 = (bf16[256,1024]{1,0:T(8,128)(2,1)S(1)}, bf16[256,1024]{1,0:T(8,128)(2,1)S(1)}, u32[]{:S(2)}, u32[]{:S(2)}) collective-permute-start(bf16[256,1024]{1,0:T(8,128)(2,1)S(1)} %collective-permute-done.5), channel_id=1, source_target_pairs={{0,1},{1,2},{2,3},{3,0},{4,5},{5,6},{6,7},{7,4},{8,9},{9,10},{10,1... | collective-permute-start | bytes 1572872 | tf_op jit(solution)/shard_map/ppermute | solution.py:928
  81.3 8.9 %collective-permute-done.10 = bf16[256,1024]{1,0:T(8,128)(2,1)S(1)} collective-permute-done((bf16[256,1024]{1,0:T(8,128)(2,1)S(1)}, bf16[256,1024]{1,0:T(8,128)(2,1)S(1)}, u32[]{:S(2)}, u32[]{:S(2)}) %collective-permute-start.10) | collective-permute-done | bytes 524320 | tf_op jit(solution)/shard_map/ppermute | solution.py:928
  101.5 8.1 %collective-permute-done.8 = bf16[128,1024]{1,0:T(8,128)(2,1)S(1)} collective-permute-done((bf16[128,1024]{1,0:T(8,128)(2,1)S(1)}, bf16[128,1024]{1,0:T(8,128)(2,1)S(1)}, u32[]{:S(2)}, u32[]{:S(2)}) %collective-permute-start.8) | collective-permute-done | bytes 262176 | tf_op jit(solution)/shard_map/ppermute | solution.py:928
  130.2 10.1 %shard_map.139 = (bf16[1024,1536]{1,0:T(8,128)(2,1)S(1)}, bf16[1024,512]{1,0:T(8,128)(2,1)S(1)}) custom-call(bf16[1024,1024]{1,0:T(8,128)(2,1)S(1)} %shard_map.138.refs_0_.normed, bf16[1024,1536]{1,0:T(8,128)(2,1)S(1)} %copy-done.106, f32[1024,128]{1,0:T(8,128)S(1)} %copy.28.refs_2_.cosine, f32[1024,128]{1,0:T(8,128)S(1)} %negate_select_fusion.refs_3_.sine, ...), custom_call_target="tpu_custom_call" | custom-call | flops 12999999488 | bytes 44200000 | tf_op jit(solution)/shard_map/pallas_call | solution.py:464
  153.0 10.1 %shard_map.140 = (bf16[1024,1536]{1,0:T(8,128)(2,1)S(1)}, bf16[1024,512]{1,0:T(8,128)(2,1)S(1)}) custom-call(bf16[1024,1024]{1,0:T(8,128)(2,1)S(1)} %copy-done.114, bf16[1024,1536]{1,0:T(8,128)(2,1)S(1)} %copy-done.107, f32[1024,128]{1,0:T(8,128)S(1)} %copy.28.refs_2_.cosine, ...), custom_call_target="tpu_custom_call", output_to_operand_aliasing={{0}: (6, {}), {1}: (7, {})} | custom-call | flops 12999999488 | bytes 44200000 | tf_op jit(solution)/shard_map/pallas_call | solution.py:464
  179.7 9.7 %collective-permute-done.23 = bf16[256,1024]{1,0:T(8,128)(2,1)S(1)} collective-permute-done((bf16[256,1024]{1,0:T(8,128)(2,1)S(1)}, bf16[256,1024]{1,0:T(8,128)(2,1)S(1)}, u32[]{:S(2)}, u32[]{:S(2)}) %collective-permute-start.23) | collective-permute-done | bytes 524320 | tf_op jit(solution)/shard_map/ppermute | solution.py:928
  203.4 16.2 %shard_map.144 = (bf16[1024,2048]{1,0:T(8,128)(2,1)S(1)}, bf16[1024,2048]{1,0:T(8,128)(2,1)S(1)}, bf16[1024,1024]{1,0:T(8,128)(2,1)S(1)}) custom-call(bf16[1024,1024]{1,0:T(8,128)(2,1)S(1)} %copy-done.100, bf16[1024,2048]{1,0:T(8,128)(2,1)} %copy-done.90, bf16[1024,2048]{1,0:T(8,128)(2,1)} %copy-done.91), custom_call_target="tpu_custom_call" | custom-call | flops 19000000512 | bytes 64600000 | tf_op jit(solution)/shard_map/pallas_call | solution.py:676
  259.1 20.2 %shard_map.148 = (bf16[1024,1536]{1,0:T(8,128)(2,1)S(1)}, bf16[1024,512]{1,0:T(8,128)(2,1)S(1)}) custom-call(bf16[1024,1024]{1,0:T(8,128)(2,1)S(1)} %copy-done.22, bf16[1024,1536]{1,0:T(8,128)(2,1)S(1)} %get-tuple-element.255.refs_1_.w_in, f32[1024,128]{1,0:T(8,128)S(1)} %copy-done.6, f32[1024,128]{1,0:T(8,128)S(1)} %copy-done.14, s32[1024,1]{1,0:T(8,128)S(1)} %copy-done.10, ...), custom_call_target="tpu_custom_call" | custom-call | flops 12999999488 | bytes 44200000 | tf_op jit(solution)/shard_map/pallas_call | solution.py:464
  306.4 16.3 %shard_map.152 = (bf16[1024,2048]{1,0:T(8,128)(2,1)S(1)}, bf16[1024,2048]{1,0:T(8,128)(2,1)S(1)}, bf16[1024,1024]{1,0:T(8,128)(2,1)S(1)}) custom-call(bf16[1024,1024]{1,0:T(8,128)(2,1)S(1)} %copy-done.104, bf16[1024,2048]{1,0:T(8,128)(2,1)} %copy-done.94, bf16[1024,2048]{1,0:T(8,128)(2,1)} %copy-done.96), custom_call_target="tpu_custom_call" | custom-call | flops 19000000512 | bytes 64600000 | tf_op jit(solution)/shard_map/pallas_call | solution.py:676
  333.2 24.3 %shard_map.154 = (bf16[2048,2048]{1,0:T(8,128)(2,1)}, bf16[1024,1024]{1,0:T(8,128)(2,1)S(1)}) custom-call(s32[3]{0:T(128)S(1)} %pad_add_fusion.place, bf16[1024,1024]{1,0:T(8,128)(2,1)S(1)} %get-tuple-element.273.mixed_grad, bf16[1024,1024]{1,0:T(8,128)(2,1)S(1)} %copy-done.104, bf16[1024,2048]{1,0:T(8,128)(2,1)S(1)} %copy-done.95, ...), custom_call_target="tpu_custom_call" | custom-call | flops 6000000000 | bytes 20400000 | tf_op jit(solution)/shard_map/pallas_call | solution.py:968
  374.3 8.4 %shard_map.155 = (bf16[1024,1024]{1,0:T(8,128)(2,1)S(1)}, f32[1024,1024]{1,0:T(8,128)}, f32[2,8,1024]{2,1,0:T(8,128)S(1)}) custom-call(bf16[1024,1024]{1,0:T(8,128)(2,1)S(1)} %copy-done.19, bf16[1024,1024]{1,0:T(8,128)(2,1)S(1)} %copy-done.56, bf16[1024,1024]{1,0:T(8,128)(2,1)S(1)} %copy-done.61, bf16[1024,1024]{1,0:T(8,128)(2,1)S(1)} %copy-done.125, ...), custom_call_target="tpu_custom_call" | custom-call | flops 6000000000 | bytes 20400000 | tf_op jit(solution)/shard_map/pallas_call | solution.py:782
  390.6 23.0 %shard_map.157 = (bf16[1024,2048]{1,0:T(8,128)(2,1)}, f32[1024,1024]{1,0:T(8,128)}) custom-call(s32[3]{0:T(128)S(1)} %pad_add_fusion.place, bf16[1024,1024]{1,0:T(8,128)(2,1)S(1)} %copy-done.25, bf16[1024,1024]{1,0:T(8,128)(2,1)S(1)} %copy-done.23, bf16[1024,1536]{1,0:T(8,128)(2,1)S(1)} %copy-done.2, bf16[1024,512]{1,0:T(8,128)(2,1)S(1)} %copy-done.30, ...), custom_call_target="tpu_custom_call" | custom-call | flops 6000000000 | bytes 20400000 | tf_op jit(solution)/shard_map/pallas_call | solution.py:968
  413.6 23.7 %shard_map.159 = (bf16[1024,2048]{1,0:T(8,128)(2,1)}, bf16[1024,1024]{1,0:T(8,128)(2,1)S(1)}) custom-call(s32[3]{0:T(128)S(1)} %pad_add_fusion.place, bf16[1024,1024]{1,0:T(8,128)(2,1)S(1)} %copy-done.26, bf16[1024,1024]{1,0:T(8,128)(2,1)S(1)} %copy-done.23, bf16[1024,1536]{1,0:T(8,128)(2,1)S(1)} %copy-done.2, ...), custom_call_target="tpu_custom_call", output_to_operand_aliasing={{0}: (11, {})} | custom-call | flops 6000000000 | bytes 20400000 | tf_op jit(solution)/shard_map/pallas_call | solution.py:968
  438.7 7.1 collective-permute-start.38
  461.7 25.0 %shard_map.162 = (bf16[512,2048]{1,0:T(8,128)(2,1)S(1)}, bf16[512,2048]{1,0:T(8,128)(2,1)S(1)}, bf16[512,2048]{1,0:T(8,128)(2,1)S(1)}, bf16[256,2048]{1,0:T(8,12...) custom-call(s32[3]{0:T(128)S(1)} %pad_add_fusion.place, ...), custom_call_target="tpu_custom_call" | custom-call | flops 6000000000 | bytes 20400000 | tf_op jit(solution)/shard_map/pallas_call | solution.py:968
  505.2 7.4 shard_map.163
  533.0 41.4 %shard_map.166 = (bf16[256,2048]{1,0:T(8,128)(2,1)S(1)}, bf16[256,2048]{1,0:T(8,128)(2,1)}, bf16[256,2048]{1,0:T(8,128)(2,1)}, bf16[128,2048]{1,0:T(8,128)(2,1)S...) custom-call(s32[3]{0:T(128)S(1)} %pad_add_fusion.place, bf16[1024,1024]{1,0:T(8,128)(2,1)S(1)} %copy-done.117, ...), custom_call_target="tpu_custom_call" | custom-call | flops 6000000000 | bytes 20400000 | tf_op jit(solution)/shard_map/pallas_call | solution.py:968
  606.5 14.5 %collective-permute-done.51 = bf16[512,512]{1,0:T(8,128)(2,1)} collective-permute-done((bf16[512,512]{1,0:T(8,128)(2,1)}, bf16[512,512]{1,0:T(8,128)(2,1)}, u32[]{:S(2)}, u32[]{:S(2)}) %collective-permute-start.51) | collective-permute-done | bytes 524320 | tf_op jit(solution)/shard_map/ppermute | solution.py:928
  638.6 7.0 collective-permute-done.52
  657.4 6.6 collective-permute-done.69
  699.8 18.1 %collective-permute-done.56.refs_2_ = bf16[256,1024]{1,0:T(8,128)(2,1)S(1)} collective-permute-done((bf16[256,1024]{1,0:T(8,128)(2,1)S(1)}, bf16[256,1024]{1,0:T(8,128)(2,1)S(1)}, u32[]{:S(2)}, u32[]{:S(2)}) %collective-permute-start.56) | collective-permute-done | bytes 524320 | tf_op jit(solution)/shard_map/ppermute | solution.py:928
  (571 shorter events, 388.7 us)
Async XLA Ops:
  7.2 182.2 %all-gather.4.cloned.1.call-start = ((), (), s32[]{:S(2)}) async-start(), calls=%async_computation.2 | async-start | bytes 7864320 | tf_op jit(solution)/shard_map/all_gather | solution.py:1395
  91.5 149.0 %all-gather.6.cloned.1.call-start = ((), (), s32[]{:S(2)}) async-start(), calls=%async_computation.3 | async-start | bytes 3932160 | tf_op jit(solution)/shard_map/all_gather | solution.py:1395
  143.5 151.3 %all-gather.8.cloned.1.call-start = ((), (), s32[]{:S(2)}) async-start(), calls=%async_computation.4 | async-start | bytes 7864320 | tf_op jit(solution)/shard_map/all_gather | solution.py:1395
  191.1 32.4 %collective-permute-start.26 = (bf16[128,1024]{1,0:T(8,128)(2,1)}, bf16[128,1024]{1,0:T(8,128)(2,1)}, u32[]{:S(2)}, u32[]{:S(2)}) collective-permute-start(bf16[128,1024]{1,0:T(8,128)(2,1)} %get-tuple-element.246), channel_id=1, source_target_pairs={{0,3},{1,0},{2,1},{3,2},{4,7},{5,4},{6,5},{7,6},{8,11},{9,8},{10,9... | collective-permute-start | bytes 786440 | tf_op jit(solution)/shard_map/ppermute | solution.py:928
  191.1 32.4 %collective-permute-start.25 = (bf16[128,1024]{1,0:T(8,128)(2,1)}, bf16[128,1024]{1,0:T(8,128)(2,1)}, u32[]{:S(2)}, u32[]{:S(2)}) collective-permute-start(bf16[128,1024]{1,0:T(8,128)(2,1)} %get-tuple-element.244), channel_id=1, source_target_pairs={{0,2},{1,3},{2,0},{3,1},{4,6},{5,7},{6,4},{7,5},{8,10},{9,11},{10,... | collective-permute-start | bytes 786440 | tf_op jit(solution)/shard_map/ppermute | solution.py:928
  192.1 31.4 %collective-permute-start.24 = (bf16[128,1024]{1,0:T(8,128)(2,1)}, bf16[128,1024]{1,0:T(8,128)(2,1)}, u32[]{:S(2)}, u32[]{:S(2)}) collective-permute-start(bf16[128,1024]{1,0:T(8,128)(2,1)} %get-tuple-element.242), channel_id=1, source_target_pairs={{0,1},{1,2},{2,3},{3,0},{4,5},{5,6},{6,7},{7,4},{8,9},{9,10},{10,1... | collective-permute-start | bytes 786440 | tf_op jit(solution)/shard_map/ppermute | solution.py:928
  193.4 299.7 %reduce-scatter.3.cloned.1.call-start = ((), (), s32[]{:S(2)}) async-start(), calls=%async_computation.5 | async-start | bytes 10485760 | tf_op jit(solution)/shard_map/reduce_scatter | solution.py:1513
  247.4 33.6 %collective-permute-start.29 = (bf16[256,1024]{1,0:T(8,128)(2,1)S(1)}, bf16[256,1024]{1,0:T(8,128)(2,1)S(1)}, u32[]{:S(2)}, u32[]{:S(2)}) collective-permute-start(bf16[256,1024]{1,0:T(8,128)(2,1)S(1)} %get-tuple-element.259), channel_id=1, source_target_pairs={{0,1},{1,2},{2,3},{3,0},{4,5},{5,6},{6,7},{7,4},{8,9},{9,10},{10,1... | collective-permute-start | bytes 1572872 | tf_op jit(solution)/shard_map/ppermute | solution.py:1103
  250.8 30.3 %collective-permute-start.30 = (bf16[256,1024]{1,0:T(8,128)(2,1)S(1)}, bf16[256,1024]{1,0:T(8,128)(2,1)S(1)}, u32[]{:S(2)}, u32[]{:S(2)}) collective-permute-start(bf16[256,1024]{1,0:T(8,128)(2,1)S(1)} %get-tuple-element.260), channel_id=1, source_target_pairs={{0,2},{1,3},{2,0},{3,1},{4,6},{5,7},{6,4},{7,5},{8,10},{9,11},{10,... | collective-permute-start | bytes 1572872 | tf_op jit(solution)/shard_map/ppermute | solution.py:1103
  358.9 155.0 %reduce-scatter.5.cloned.1.call-start = ((), (), s32[]{:S(2)}) async-start(), calls=%async_computation.6 | async-start | bytes 5242880 | tf_op jit(solution)/shard_map/reduce_scatter | solution.py:1513
  384.0 29.6 %collective-permute-start.35 = (bf16[256,1024]{1,0:T(8,128)(2,1)S(1)}, bf16[256,1024]{1,0:T(8,128)(2,1)S(1)}, u32[]{:S(2)}, u32[]{:S(2)}) collective-permute-start(bf16[256,1024]{1,0:T(8,128)(2,1)S(1)} %get-tuple-element.281), channel_id=1, source_target_pairs={{16,17},{17,18},{18,19},{19,16},{20,21},{21,22},{22,23},{23,20},{2... | collective-permute-start | bytes 1572872 | tf_op jit(solution)/shard_map/ppermute | solution.py:1103
  517.9 57.4 %collective-permute-start.43 = (bf16[768,512]{1,0:T(8,128)(2,1)}, bf16[768,512]{1,0:T(8,128)(2,1)}, u32[]{:S(2)}, u32[]{:S(2)}) collective-permute-start(bf16[768,512]{1,0:T(8,128)(2,1)} %pad_maximum_fusion.4), channel_id=1, source_target_pairs={{0,1},{1,2},{2,3},{3,0},{4,5},{5,6},{6,7},{7,4},{8,9},{9,10},{10,1... | collective-permute-start | bytes 2359304 | tf_op jit(solution)/shard_map/ppermute | solution.py:928
  519.9 55.5 %collective-permute-start.42 = (bf16[768,512]{1,0:T(8,128)(2,1)}, bf16[768,512]{1,0:T(8,128)(2,1)}, u32[]{:S(2)}, u32[]{:S(2)}) collective-permute-start(bf16[768,512]{1,0:T(8,128)(2,1)} %pad_maximum_fusion.3), channel_id=1, source_target_pairs={{0,3},{1,0},{2,1},{3,2},{4,7},{5,4},{6,5},{7,6},{8,11},{9,8},{10,9... | collective-permute-start | bytes 2359304 | tf_op jit(solution)/shard_map/ppermute | solution.py:928
  528.3 50.9 %collective-permute-start.46 = (bf16[512,2048]{1,0:T(8,128)(2,1)S(1)}, bf16[512,2048]{1,0:T(8,128)(2,1)S(1)}, u32[]{:S(2)}, u32[]{:S(2)}) collective-permute-start(bf16[512,2048]{1,0:T(8,128)(2,1)S(1)} %shard_map.164), channel_id=1, source_target_pairs={{0,4},{4,0},{8,12},{12,8},{16,24},{20,28},{24,16},{28,20},{1,5},{5... | collective-permute-start | bytes 6291464 | tf_op jit(solution)/shard_map/ppermute | solution.py:928
  529.9 51.2 %collective-permute-start.48 = (bf16[512,2048]{1,0:T(8,128)(2,1)S(1)}, bf16[512,2048]{1,0:T(8,128)(2,1)}, u32[]{:S(2)}, u32[]{:S(2)}) collective-permute-start(bf16[512,2048]{1,0:T(8,128)(2,1)S(1)} %shard_map.165), channel_id=1, source_target_pairs={{0,8},{4,12},{8,0},{12,4},{16,20},{20,16},{24,28},{28,24},{1,9},{5... | collective-permute-start | bytes 6291464 | tf_op jit(solution)/shard_map/ppermute | solution.py:928
  586.5 34.5 %collective-permute-start.51 = (bf16[512,512]{1,0:T(8,128)(2,1)}, bf16[512,512]{1,0:T(8,128)(2,1)}, u32[]{:S(2)}, u32[]{:S(2)}) collective-permute-start(bf16[512,512]{1,0:T(8,128)(2,1)} %get-tuple-element.340), channel_id=1, source_target_pairs={{0,3},{1,0},{2,1},{3,2},{4,7},{5,4},{6,5},{7,6},{8,11},{9,8},{10,9... | collective-permute-start | bytes 1572872 | tf_op jit(solution)/shard_map/ppermute | solution.py:928
  595.8 35.9 %collective-permute-start.50 = (bf16[256,2048]{1,0:T(8,128)(2,1)}, bf16[256,2048]{1,0:T(8,128)(2,1)}, u32[]{:S(2)}, u32[]{:S(2)}) collective-permute-start(bf16[256,2048]{1,0:T(8,128)(2,1)} %shard_map.169), channel_id=1, source_target_pairs={{0,8},{4,12},{8,0},{12,4},{16,20},{20,16},{24,28},{28,24},{1,9},{5... | collective-permute-start | bytes 3145736 | tf_op jit(solution)/shard_map/ppermute | solution.py:928
  600.2 33.0 %collective-permute-start.49 = (bf16[256,2048]{1,0:T(8,128)(2,1)}, bf16[256,2048]{1,0:T(8,128)(2,1)}, u32[]{:S(2)}, u32[]{:S(2)}) collective-permute-start(bf16[256,2048]{1,0:T(8,128)(2,1)} %shard_map.168), channel_id=1, source_target_pairs={{0,4},{4,0},{8,12},{12,8},{16,24},{20,28},{24,16},{28,20},{1,5},{5... | collective-permute-start | bytes 3145736 | tf_op jit(solution)/shard_map/ppermute | solution.py:928
  604.8 31.4 %collective-permute-start.54 = (bf16[512,512]{1,0:T(8,128)(2,1)}, bf16[512,512]{1,0:T(8,128)(2,1)S(1)}, u32[]{:S(2)}, u32[]{:S(2)}) collective-permute-start(bf16[512,512]{1,0:T(8,128)(2,1)} %copy-done.89), channel_id=1, source_target_pairs={{0,1},{1,2},{2,3},{3,0},{4,5},{5,6},{6,7},{7,4},{8,9},{9,10},{10,1... | collective-permute-start | bytes 1572872 | tf_op jit(solution)/shard_map/ppermute | solution.py:928
  668.8 62.3 %collective-permute-start.76 = (bf16[2048,512]{1,0:T(8,128)(2,1)S(1)}, bf16[2048,512]{1,0:T(8,128)(2,1)S(1)}, u32[]{:S(2)}, u32[]{:S(2)}) collective-permute-start(bf16[2048,512]{1,0:T(8,128)(2,1)S(1)} %fusion.refs_5_), channel_id=1, source_target_pairs={{0,16},{1,17},{2,18},{3,19},{4,20},{5,21},{6,22},{7,23},{8,24},{9,... | collective-permute-start | bytes 6291464 | tf_op jit(solution)/shard_map/ppermute | solution.py:1598
  679.3 51.9 %collective-permute-start.74 = (bf16[2048,512]{1,0:T(8,128)(2,1)S(1)}, bf16[2048,512]{1,0:T(8,128)(2,1)S(1)}, u32[]{:S(2)}, u32[]{:S(2)}) collective-permute-start(bf16[2048,512]{1,0:T(8,128)(2,1)S(1)} %constant_dynamic-update-slice_fusion.22.refs_1_), channel_id=1, source_target_pairs={{16,0},{17,1},{18,2},{19,3},{20,4},{21,5},{22,6},{23,7},{24,8},{25... | collective-permute-start | bytes 6291464 | tf_op jit(solution)/shard_map/ppermute | solution.py:1598
  681.8 36.1 %collective-permute-start.56 = (bf16[256,1024]{1,0:T(8,128)(2,1)S(1)}, bf16[256,1024]{1,0:T(8,128)(2,1)S(1)}, u32[]{:S(2)}, u32[]{:S(2)}) collective-permute-start(bf16[256,1024]{1,0:T(8,128)(2,1)S(1)} %get-tuple-element.347), channel_id=1, source_target_pairs={{0,2},{1,3},{2,0},{3,1},{4,6},{5,7},{6,4},{7,5},{8,10},{9,11},{10,... | collective-permute-start | bytes 1572872 | tf_op jit(solution)/shard_map/ppermute | solution.py:928
  681.8 38.0 %collective-permute-start.53 = (bf16[256,1024]{1,0:T(8,128)(2,1)S(1)}, bf16[256,1024]{1,0:T(8,128)(2,1)S(1)}, u32[]{:S(2)}, u32[]{:S(2)}) collective-permute-start(bf16[256,1024]{1,0:T(8,128)(2,1)S(1)} %get-tuple-element.342), channel_id=1, source_target_pairs={{0,1},{1,2},{2,3},{3,0},{4,5},{5,6},{6,7},{7,4},{8,9},{9,10},{10,1... | collective-permute-start | bytes 1572872 | tf_op jit(solution)/shard_map/ppermute | solution.py:928
  696.8 32.2 %collective-permute-start.60 = (bf16[256,1024]{1,0:T(8,128)(2,1)S(1)}, bf16[256,1024]{1,0:T(8,128)(2,1)S(1)}, u32[]{:S(2)}, u32[]{:S(2)}) collective-permute-start(bf16[256,1024]{1,0:T(8,128)(2,1)S(1)} %get-tuple-element.353), channel_id=1, source_target_pairs={{0,3},{1,0},{2,1},{3,2},{4,7},{5,4},{6,5},{7,6},{8,11},{9,8},{10,9... | collective-permute-start | bytes 1572872 | tf_op jit(solution)/shard_map/ppermute | solution.py:928
  (208 other events, 2314.1 us)
Sparse Core Ops, SparseCore 0:
  91.7 67.8 all-gather.3
  161.4 43.9 all-gather.5
  207.2 70.1 all-gather.7
  359.0 84.4 reduce-scatter.2
  446.6 53.4 reduce-scatter.4
